TPU v7x, 256 devices: a whole 4x4x8 slice. The times are simulated.
256 devices in a mesh: gx: 16 (over y_lo, z), gy: 8 (over x, core), gz: 2 (over y_hi).
Axes of the slice: x: 4, y: 4 (y_hi: 2, y_lo: 2; y = y_hi * 2 + y_lo), z: 8, core: 2. Of those that a mesh axis runs over, the one named last changes fastest.
Arguments:
- features: bfloat16 [32, 64, 256, 256], P(None, 'gx', 'gy', 'gz'), may hold values from -6 to 6
- conv_weight: bfloat16 [32, 32, 3, 3, 3], replicated, may hold values from -0.21875 to 0.21875
- conv_bias: float32 [32], replicated, may hold values from -3 to 3
- head_weight: bfloat16 [3, 32], replicated, may hold values from -1 to 1
- head_bias: float32 [3], replicated, may hold values from 1.5 to 3
- mask: int32 [64, 256, 256], P('gx', 'gy', 'gz'), may hold values 0 or 1
- seeds: int32 [64, 256, 256], P('gx', 'gy', 'gz'), may hold values from 0 to 15, as said below
Outputs:
- affinity: bfloat16 [3, 64, 256, 256], P(None, 'gx', 'gy', 'gz')
- propagated: float32 [64, 256, 256], P('gx', 'gy', 'gz')
Inputs may be any that keep to these rules, and one draw needn't show every extreme that they name: `seeds`: seed value of a voxel; 0 where the voxel holds no seed.
All inputs are finite; a program needn't handle non-finite values. No bound on the sum of `mask` on one device may be relied on, other than what follows from the above.
Results may differ from a plain program's by a relative error of at most 0.0026.
Values may be sent and summed in bfloat16 or wider, within the bound.
No kernel may reach another device: no remote copies, remote signals or barrier semaphores. Data moves between devices by JAX's collectives and lax.ppermute only.
A program may use at most 128 MiB of HBM per device.

v0:
```python
import jax
import jax.numpy as jnp
from jax import lax
from jax.sharding import PartitionSpec as P

ROUNDS = 4


def extended(block, sides, width):
    for axis, dim in sides:
        count = lax.axis_size(axis)
        forward = [(i, i + 1) for i in range(count - 1)]
        backward = [(target, source) for source, target in forward]
        low = lax.ppermute(
            lax.slice_in_dim(block, block.shape[dim] - width, None, axis=dim), axis, forward
        )
        high = lax.ppermute(lax.slice_in_dim(block, 0, width, axis=dim), axis, backward)
        block = jnp.concatenate([low, block, high], axis=dim)
    return block


def from_behind(x, axis, by):
    size = lax.axis_size(axis)
    pairs = [(i, i + by) for i in range(size) if 0 <= i + by < size]
    return lax.ppermute(x, axis, pairs)


def affinities(window, conv_weight, conv_bias, head_weight, head_bias):
    conv_out = lax.conv_general_dilated(
        window[None],
        conv_weight,
        (1, 1, 1),
        "VALID",
        dimension_numbers=("NCDHW", "OIDHW", "NCDHW"),
        preferred_element_type=jnp.float32,
    )[0]
    hidden = jnp.maximum(conv_out + conv_bias[:, None, None, None], 0.0).astype(jnp.bfloat16)
    hidden_shape = hidden.shape
    logits = (
        jnp.dot(
            head_weight, hidden.reshape(hidden_shape[0], -1), preferred_element_type=jnp.float32
        )
        + head_bias[:, None]
    )
    return jax.nn.sigmoid(logits).astype(jnp.bfloat16).reshape((3,) + hidden_shape[1:])


def one_round(strength, framed, foreground, own_edges, next_x, next_y, next_z):
    highest = strength
    highest = jnp.maximum(highest, jnp.minimum(framed[:-2, 1:-1, 1:-1], own_edges[0]))
    highest = jnp.maximum(highest, jnp.minimum(framed[2:, 1:-1, 1:-1], next_x))
    highest = jnp.maximum(highest, jnp.minimum(framed[1:-1, :-2, 1:-1], own_edges[1]))
    highest = jnp.maximum(highest, jnp.minimum(framed[1:-1, 2:, 1:-1], next_y))
    highest = jnp.maximum(highest, jnp.minimum(framed[1:-1, 1:-1, :-2], own_edges[2]))
    highest = jnp.maximum(highest, jnp.minimum(framed[1:-1, 1:-1, 2:], next_z))
    return foreground * highest


def body(features, conv_weight, conv_bias, head_weight, head_bias, mask, seeds):
    padded = extended(features, (("gx", 1), ("gy", 2), ("gz", 3)), 1)
    affinity = affinities(padded, conv_weight, conv_bias, head_weight, head_bias)
    from_x = from_behind(affinity[0, 0:1, :, :], "gx", -1)
    from_y = from_behind(affinity[1, :, 0:1, :], "gy", -1)
    from_z = from_behind(affinity[2, :, :, 0:1], "gz", -1)
    next_x = jnp.concatenate([affinity[0, 1:, :, :], from_x], axis=0).astype(jnp.float32)
    next_y = jnp.concatenate([affinity[1, :, 1:, :], from_y], axis=1).astype(jnp.float32)
    next_z = jnp.concatenate([affinity[2, :, :, 1:], from_z], axis=2).astype(jnp.float32)
    own_edges = affinity.astype(jnp.float32)
    foreground = mask.astype(jnp.float32)
    strength = foreground * (seeds.astype(jnp.float32) / 15.0)
    for round_index in range(ROUNDS):
        framed = extended(strength, (("gx", 0), ("gy", 1), ("gz", 2)), 1)
        strength = one_round(strength, framed, foreground, own_edges, next_x, next_y, next_z)
    return (affinity, strength)


def solution(mesh):
    in_specs = (
        P(None, "gx", "gy", "gz"),
        P(),
        P(),
        P(),
        P(),
        P("gx", "gy", "gz"),
        P("gx", "gy", "gz"),
    )
    out_specs = (P(None, "gx", "gy", "gz"), P("gx", "gy", "gz"))
    return jax.shard_map(body, mesh=mesh, in_specs=in_specs, out_specs=out_specs, check_vma=False)
```

profile of v0, /device:TPU:14, one launch (start us, length us, event | category | flops | bytes accessed | tf_op | source)
XLA Modules:
  0.0 228.6 jit_solution(11331214594648165144)
XLA Ops:
  1.8 3.8 %collective-permute-start = (bf16[32,1,32,128]{3,2,1,0:T(8,128)(2,1)S(1)}, bf16[32,1,32,128]{3,2,1,0:T(8,128)(2,1)S(1)}, u32[]{:S(2)}, u32[]{:S(2)}) collective-permute-start(bf16[32,1,32,128]{3,2,1,0:T(8,128)(2,1)S(1)} %get-tuple-element.9), channel_id=1, source_target_pairs={{0,16},{16,32},{32,48},{48,64},{64,80},{80,96},{96,112},{112,128},... | collective-permute-start | bytes 786440 | tf_op jit(solution)/shard_map/ppermute | solution.py:14
  6.5 3.8 %collective-permute-start.6 = (f32[1,32,128]{2,1,0:T(8,128)S(1)}, f32[1,32,128]{2,1,0:T(8,128)S(1)}, u32[]{:S(2)}, u32[]{:S(2)}) collective-permute-start(f32[1,32,128]{2,1,0:T(8,128)S(1)} %get-tuple-element.32), channel_id=1, source_target_pairs={{0,16},{16,32},{32,48},{48,64},{64,80},{80,96},{96,112},{112,128},... | collective-permute-start | bytes 49160 | tf_op jit(solution)/shard_map/ppermute | solution.py:14
  10.3 4.1 %collective-permute-start.7 = (f32[1,32,128]{2,1,0:T(8,128)S(1)}, f32[1,32,128]{2,1,0:T(8,128)S(1)}, u32[]{:S(2)}, u32[]{:S(2)}) collective-permute-start(f32[1,32,128]{2,1,0:T(8,128)S(1)} %get-tuple-element.33), channel_id=1, source_target_pairs={{16,0},{32,16},{48,32},{64,48},{80,64},{96,80},{112,96},{128,112},... | collective-permute-start | bytes 49160 | tf_op jit(solution)/shard_map/ppermute | solution.py:17
  26.1 3.6 %collective-permute-start.3 = (bf16[32,6,1,128]{3,0,2,1:T(8,128)(2,1)S(1)}, bf16[32,6,1,128]{3,0,2,1:T(8,128)(2,1)S(1)}, u32[]{:S(2)}, u32[]{:S(2)}) collective-permute-start(bf16[32,6,1,128]{3,0,2,1:T(8,128)(2,1)S(1)} %copy.53), channel_id=1, source_target_pairs={{2,0},{4,2},{6,4},{8,6},{10,8},{12,10},{14,12},{3,1},{5,3},{7,5},{... | collective-permute-start | bytes 147464 | tf_op jit(solution)/shard_map/ppermute | solution.py:17
  29.8 9.0 %copy.43 = bf16[32,6,32,128]{2,0,3,1:T(8,128)(2,1)} copy(bf16[32,6,32,128]{3,2,1,0:T(8,128)(2,1)S(1)} %constant_dynamic-update-slice_fusion) | data formatting | bytes 3145728 | tf_op jit(solution)/shard_map/concatenate | solution.py:18
  38.8 9.7 %copy.42 = bf16[32,6,1,128]{2,0,3,1:T(8,128)(2,1)} copy(bf16[32,6,1,128]{3,0,2,1:T(8,128)(2,1)S(1)} %collective-permute-done.2) | data formatting | bytes 98304 | tf_op jit(solution)/shard_map/ppermute | solution.py:14
  48.5 9.7 %copy.44 = bf16[32,6,1,128]{2,0,3,1:T(8,128)(2,1)} copy(bf16[32,6,1,128]{3,0,2,1:T(8,128)(2,1)S(1)} %collective-permute-done.3) | data formatting | bytes 98304 | tf_op jit(solution)/shard_map/ppermute | solution.py:17
  59.5 4.8 %collective-permute-start.4 = (bf16[32,6,34,1]{2,0,3,1:T(8,128)(2,1)S(1)}, bf16[32,6,34,1]{2,0,3,1:T(8,128)(2,1)S(1)}, u32[]{:S(2)}, u32[]{:S(2)}) collective-permute-start(bf16[32,6,34,1]{2,0,3,1:T(8,128)(2,1)S(1)} %get-tuple-element.4), channel_id=1, source_target_pairs={{0,1},{2,3},{4,5},{6,7},{8,9},{10,11},{12,13},{14,15},{16,17},{18,... | collective-permute-start | bytes 39176 | tf_op jit(solution)/shard_map/ppermute | solution.py:14
  65.7 6.1 %collective-permute-start.12 = (f32[6,34,1]{2,1,0:T(8,128)S(1)}, f32[6,34,1]{2,1,0:T(8,128)S(1)}, u32[]{:S(2)}, u32[]{:S(2)}) collective-permute-start(f32[6,34,1]{2,1,0:T(8,128)S(1)} %get-tuple-element.16), channel_id=1, source_target_pairs={{0,1},{2,3},{4,5},{6,7},{8,9},{10,11},{12,13},{14,15},{16,17},{18,... | collective-permute-start | bytes 2456 | tf_op jit(solution)/shard_map/ppermute | solution.py:14
  73.3 7.4 %maximum_bitcast_fusion = bf16[32,6,34,1,130]{2,0,4,1,3:T(8,128)(2,1)S(1)} fusion(bf16[32,6,34,1]{2,0,3,1:T(8,128)(2,1)S(1)} %collective-permute-done.5, bf16[32,6,1,128]{2,0,3,1:T(8,128)(2,1)S(1)} %copy-done.2, bf16[32,6,32,128]{2,0,3,1:T(8,128)(2,1)} %copy.43, bf16[32,6,1,128]{2,0,3,1:T(8,128)(2,1)S(1)} %bitcast.63, ...), kind=kLoop, calls=%fused_computation.15 | loop fusion | flops 8486400 | bytes 3394560 | tf_op jit(solution)/shard_map/broadcast_in_dim | solution.py:30
  80.7 4.1 %pad = bf16[32,6,34,1,136]{2,0,4,1,3:T(8,128)(2,1)} pad(bf16[32,6,34,1,130]{2,0,4,1,3:T(8,128)(2,1)S(1)} %maximum_bitcast_fusion, bf16[]{:T(256)} %constant.10), padding=0_0x0_0x0_0x0_0x0_6 | pad | bytes 3472898 | tf_op jit(solution)/shard_map/broadcast_in_dim | solution.py:30
  84.7 12.4 %copy.46 = bf16[32,6,34,1,8,17]{0,4,5,2,1,3:T(8,128)(2,1)} copy(bf16[32,6,34,1,8,17]{2,0,5,4,1,3:T(8,128)(2,1)} %bitcast.65) | data formatting | bytes 3551232 | tf_op jit(solution)/shard_map/conv_general_dilated | solution.py:29
  98.6 17.1 %broadcast_select_fusion = f32[4,32,8,17,32]{4,2,3,1,0:T(8,128)S(1)} fusion(pred[8,17]{0,1:T(8,128)(4,1)S(1)} %copy-done.8, bf16[32,32,3,3,3]{1,0,4,3,2:T(8,128)(2,1)S(1)} %copy-done, bf16[32,6,34,1,7,2]{0,4,5,2,1,3:T(8,128)(2,1)S(1)} %slice.289, bf16[32,6,34,1,8,17]{0,4,5,2,1,3:T(8,128)(2,1)} %copy.46), kind=kOutput, calls=%fused_computation.16 | convolution fusion | flops 969103360 | bytes 4242056 | tf_op jit(solution)/shard_map/conv_general_dilated | solution.py:29
  117.2 4.3 %slice_bitcast_fusion = f32[1,32,4,32,128]{1,3,4,2,0:T(8,128)} fusion(f32[4,32,1,136,32]{4,1,3,0,2:T(8,128)S(1)} %bitcast.64), kind=kLoop, calls=%fused_computation.8 | loop fusion | bytes 4194304 | tf_op jit(solution)/shard_map/conv_general_dilated | solution.py:29
  121.5 7.1 %copy.48 = f32[1,32,4,32,128]{4,3,2,1,0:T(8,128)S(1)} copy(f32[1,32,4,32,128]{1,3,4,2,0:T(8,128)} %slice_bitcast_fusion) | data formatting | bytes 4194304 | tf_op jit(solution)/shard_map/conv_general_dilated | solution.py:29
  132.4 6.2 %collective-permute-start.8 = (bf16[1,32,128]{2,1,0:T(8,128)(2,1)S(1)}, bf16[1,32,128]{2,1,0:T(8,128)(2,1)S(1)}, u32[]{:S(2)}, u32[]{:S(2)}) collective-permute-start(bf16[1,32,128]{2,1,0:T(8,128)(2,1)S(1)} %slice_bitcast_fusion.7), channel_id=1, source_target_pairs={{16,0},{32,16},{48,32},{64,48},{80,64},{96,80},{112,96},{128,112},... | collective-permute-start | bytes 24584 | tf_op jit(solution)/shard_map/ppermute | solution.py:25
  142.0 5.6 %collective-permute-done.14 = bf16[4,32,1]{1,0,2:T(4,128)(2,1)S(1)} collective-permute-done((bf16[4,32,1]{1,0,2:T(4,128)(2,1)S(1)}, bf16[4,32,1]{1,0,2:T(4,128)(2,1)S(1)}, u32[]{:S(2)}, u32[]{:S(2)}) %collective-permute-start.14) | collective-permute-done | bytes 288 | tf_op jit(solution)/shard_map/ppermute | solution.py:25
  149.9 6.0 %collective-permute-start.16 = (f32[1,32,128]{2,1,0:T(8,128)S(1)}, f32[1,32,128]{2,1,0:T(8,128)S(1)}, u32[]{:S(2)}, u32[]{:S(2)}) collective-permute-start(f32[1,32,128]{2,1,0:T(8,128)S(1)} %get-tuple-element.31), channel_id=1, source_target_pairs={{16,0},{32,16},{48,32},{64,48},{80,64},{96,80},{112,96},{128,112},... | collective-permute-start | bytes 49160 | tf_op jit(solution)/shard_map/ppermute | solution.py:17
  159.3 3.6 %collective-permute-start.18 = (f32[6,1,128]{2,1,0:T(1,128)S(1)}, f32[6,1,128]{2,1,0:T(1,128)S(1)}, u32[]{:S(2)}, u32[]{:S(2)}) collective-permute-start(f32[6,1,128]{2,1,0:T(1,128)S(1)} %get-tuple-element.23), channel_id=1, source_target_pairs={{2,0},{4,2},{6,4},{8,6},{10,8},{12,10},{14,12},{3,1},{5,3},{7,5},{... | collective-permute-start | bytes 9224 | tf_op jit(solution)/shard_map/ppermute | solution.py:17
  168.4 5.9 %collective-permute-done.20 = f32[6,34,1]{2,1,0:T(8,128)S(1)} collective-permute-done((f32[6,34,1]{2,1,0:T(8,128)S(1)}, f32[6,34,1]{2,1,0:T(8,128)S(1)}, u32[]{:S(2)}, u32[]{:S(2)}) %collective-permute-start.20) | collective-permute-done | bytes 848 | tf_op jit(solution)/shard_map/ppermute | solution.py:17
  176.3 6.9 %collective-permute-start.22 = (f32[1,32,128]{2,1,0:T(8,128)S(1)}, f32[1,32,128]{2,1,0:T(8,128)S(1)}, u32[]{:S(2)}, u32[]{:S(2)}) collective-permute-start(f32[1,32,128]{2,1,0:T(8,128)S(1)} %get-tuple-element.29), channel_id=1, source_target_pairs={{16,0},{32,16},{48,32},{64,48},{80,64},{96,80},{112,96},{128,112},... | collective-permute-start | bytes 49160 | tf_op jit(solution)/shard_map/ppermute | solution.py:17
  195.4 5.9 %collective-permute-done.26 = f32[6,34,1]{2,1,0:T(8,128)S(1)} collective-permute-done((f32[6,34,1]{2,1,0:T(8,128)S(1)}, f32[6,34,1]{2,1,0:T(8,128)S(1)}, u32[]{:S(2)}, u32[]{:S(2)}) %collective-permute-start.26) | collective-permute-done | bytes 848 | tf_op jit(solution)/shard_map/ppermute | solution.py:17
  203.3 6.5 %collective-permute-start.28 = (f32[1,32,128]{2,1,0:T(8,128)S(1)}, f32[1,32,128]{2,1,0:T(8,128)S(1)}, u32[]{:S(2)}, u32[]{:S(2)}) collective-permute-start(f32[1,32,128]{2,1,0:T(8,128)S(1)} %get-tuple-element.27), channel_id=1, source_target_pairs={{16,0},{32,16},{48,32},{64,48},{80,64},{96,80},{112,96},{128,112},... | collective-permute-start | bytes 49160 | tf_op jit(solution)/shard_map/ppermute | solution.py:17
  222.0 5.9 %collective-permute-done.32 = f32[6,34,1]{2,1,0:T(8,128)S(1)} collective-permute-done((f32[6,34,1]{2,1,0:T(8,128)S(1)}, f32[6,34,1]{2,1,0:T(8,128)S(1)}, u32[]{:S(2)}, u32[]{:S(2)}) %collective-permute-start.32) | collective-permute-done | bytes 848 | tf_op jit(solution)/shard_map/ppermute | solution.py:17
  (118 shorter events, 67.7 us)
Async XLA Ops:
  1.8 20.7 %collective-permute-start = (bf16[32,1,32,128]{3,2,1,0:T(8,128)(2,1)S(1)}, bf16[32,1,32,128]{3,2,1,0:T(8,128)(2,1)S(1)}, u32[]{:S(2)}, u32[]{:S(2)}) collective-permute-start(bf16[32,1,32,128]{3,2,1,0:T(8,128)(2,1)S(1)} %get-tuple-element.9), channel_id=1, source_target_pairs={{0,16},{16,32},{32,48},{48,64},{64,80},{80,96},{96,112},{112,128},... | collective-permute-start | bytes 786440 | tf_op jit(solution)/shard_map/ppermute | solution.py:14
  6.5 11.6 %collective-permute-start.6 = (f32[1,32,128]{2,1,0:T(8,128)S(1)}, f32[1,32,128]{2,1,0:T(8,128)S(1)}, u32[]{:S(2)}, u32[]{:S(2)}) collective-permute-start(f32[1,32,128]{2,1,0:T(8,128)S(1)} %get-tuple-element.32), channel_id=1, source_target_pairs={{0,16},{16,32},{32,48},{48,64},{64,80},{80,96},{96,112},{112,128},... | collective-permute-start | bytes 49160 | tf_op jit(solution)/shard_map/ppermute | solution.py:14
  10.3 7.8 %collective-permute-start.7 = (f32[1,32,128]{2,1,0:T(8,128)S(1)}, f32[1,32,128]{2,1,0:T(8,128)S(1)}, u32[]{:S(2)}, u32[]{:S(2)}) collective-permute-start(f32[1,32,128]{2,1,0:T(8,128)S(1)} %get-tuple-element.33), channel_id=1, source_target_pairs={{16,0},{32,16},{48,32},{64,48},{80,64},{96,80},{112,96},{128,112},... | collective-permute-start | bytes 49160 | tf_op jit(solution)/shard_map/ppermute | solution.py:17
  14.5 9.5 %collective-permute-start.1 = (bf16[32,1,32,128]{3,2,1,0:T(8,128)(2,1)S(1)}, bf16[32,1,32,128]{3,2,1,0:T(8,128)(2,1)S(1)}, u32[]{:S(2)}, u32[]{:S(2)}) collective-permute-start(bf16[32,1,32,128]{3,2,1,0:T(8,128)(2,1)S(1)} %get-tuple-element.8), channel_id=1, source_target_pairs={{16,0},{32,16},{48,32},{64,48},{80,64},{96,80},{112,96},{128,112},... | collective-permute-start | bytes 786440 | tf_op jit(solution)/shard_map/ppermute | solution.py:17
  18.1 11.6 %collective-permute-start.10 = (f32[6,1,128]{2,1,0:T(1,128)S(1)}, f32[6,1,128]{2,1,0:T(1,128)S(1)}, u32[]{:S(2)}, u32[]{:S(2)}) collective-permute-start(f32[6,1,128]{2,1,0:T(1,128)S(1)} %get-tuple-element.25), channel_id=1, source_target_pairs={{2,0},{4,2},{6,4},{8,6},{10,8},{12,10},{14,12},{3,1},{5,3},{7,5},{... | collective-permute-start | bytes 9224 | tf_op jit(solution)/shard_map/ppermute | solution.py:17
  20.1 9.7 %collective-permute-start.9 = (f32[6,1,128]{2,1,0:T(1,128)S(1)}, f32[6,1,128]{2,1,0:T(1,128)S(1)}, u32[]{:S(2)}, u32[]{:S(2)}) collective-permute-start(f32[6,1,128]{2,1,0:T(1,128)S(1)} %get-tuple-element.24), channel_id=1, source_target_pairs={{0,2},{2,4},{4,6},{6,8},{8,10},{10,12},{12,14},{1,3},{3,5},{5,7},{... | collective-permute-start | bytes 9224 | tf_op jit(solution)/shard_map/ppermute | solution.py:14
  24.2 14.7 %collective-permute-start.2 = (bf16[32,6,1,128]{3,0,2,1:T(8,128)(2,1)S(1)}, bf16[32,6,1,128]{3,0,2,1:T(8,128)(2,1)S(1)}, u32[]{:S(2)}, u32[]{:S(2)}) collective-permute-start(bf16[32,6,1,128]{3,0,2,1:T(8,128)(2,1)S(1)} %copy.52), channel_id=1, source_target_pairs={{0,2},{2,4},{4,6},{6,8},{8,10},{10,12},{12,14},{1,3},{3,5},{5,7},{... | collective-permute-start | bytes 147464 | tf_op jit(solution)/shard_map/ppermute | solution.py:14
  26.1 22.4 %collective-permute-start.3 = (bf16[32,6,1,128]{3,0,2,1:T(8,128)(2,1)S(1)}, bf16[32,6,1,128]{3,0,2,1:T(8,128)(2,1)S(1)}, u32[]{:S(2)}, u32[]{:S(2)}) collective-permute-start(bf16[32,6,1,128]{3,0,2,1:T(8,128)(2,1)S(1)} %copy.53), channel_id=1, source_target_pairs={{2,0},{4,2},{6,4},{8,6},{10,8},{12,10},{14,12},{3,1},{5,3},{7,5},{... | collective-permute-start | bytes 147464 | tf_op jit(solution)/shard_map/ppermute | solution.py:17
  59.5 13.7 %collective-permute-start.4 = (bf16[32,6,34,1]{2,0,3,1:T(8,128)(2,1)S(1)}, bf16[32,6,34,1]{2,0,3,1:T(8,128)(2,1)S(1)}, u32[]{:S(2)}, u32[]{:S(2)}) collective-permute-start(bf16[32,6,34,1]{2,0,3,1:T(8,128)(2,1)S(1)} %get-tuple-element.4), channel_id=1, source_target_pairs={{0,1},{2,3},{4,5},{6,7},{8,9},{10,11},{12,13},{14,15},{16,17},{18,... | collective-permute-start | bytes 39176 | tf_op jit(solution)/shard_map/ppermute | solution.py:14
  64.3 9.0 %collective-permute-start.5 = (bf16[32,6,34,1]{2,0,3,1:T(8,128)(2,1)S(1)}, bf16[32,6,34,1]{2,0,3,1:T(8,128)(2,1)S(1)}, u32[]{:S(2)}, u32[]{:S(2)}) collective-permute-start(bf16[32,6,34,1]{2,0,3,1:T(8,128)(2,1)S(1)} %get-tuple-element.5), channel_id=1, source_target_pairs={{1,0},{3,2},{5,4},{7,6},{9,8},{11,10},{13,12},{15,14},{17,16},{19,... | collective-permute-start | bytes 39176 | tf_op jit(solution)/shard_map/ppermute | solution.py:17
  65.7 82.1 %collective-permute-start.12 = (f32[6,34,1]{2,1,0:T(8,128)S(1)}, f32[6,34,1]{2,1,0:T(8,128)S(1)}, u32[]{:S(2)}, u32[]{:S(2)}) collective-permute-start(f32[6,34,1]{2,1,0:T(8,128)S(1)} %get-tuple-element.16), channel_id=1, source_target_pairs={{0,1},{2,3},{4,5},{6,7},{8,9},{10,11},{12,13},{14,15},{16,17},{18,... | collective-permute-start | bytes 2456 | tf_op jit(solution)/shard_map/ppermute | solution.py:14
  71.7 76.0 %collective-permute-start.13 = (f32[6,34,1]{2,1,0:T(8,128)S(1)}, f32[6,34,1]{2,1,0:T(8,128)S(1)}, u32[]{:S(2)}, u32[]{:S(2)}) collective-permute-start(f32[6,34,1]{2,1,0:T(8,128)S(1)} %get-tuple-element.17), channel_id=1, source_target_pairs={{1,0},{3,2},{5,4},{7,6},{9,8},{11,10},{13,12},{15,14},{17,16},{19,... | collective-permute-start | bytes 2456 | tf_op jit(solution)/shard_map/ppermute | solution.py:17
  132.4 15.3 %collective-permute-start.8 = (bf16[1,32,128]{2,1,0:T(8,128)(2,1)S(1)}, bf16[1,32,128]{2,1,0:T(8,128)(2,1)S(1)}, u32[]{:S(2)}, u32[]{:S(2)}) collective-permute-start(bf16[1,32,128]{2,1,0:T(8,128)(2,1)S(1)} %slice_bitcast_fusion.7), channel_id=1, source_target_pairs={{16,0},{32,16},{48,32},{64,48},{80,64},{96,80},{112,96},{128,112},... | collective-permute-start | bytes 24584 | tf_op jit(solution)/shard_map/ppermute | solution.py:25
  138.7 9.0 %collective-permute-start.11 = (bf16[4,1,128]{2,0,1:T(4,128)(2,1)S(1)}, bf16[4,1,128]{2,0,1:T(4,128)(2,1)S(1)}, u32[]{:S(2)}, u32[]{:S(2)}) collective-permute-start(bf16[4,1,128]{2,0,1:T(4,128)(2,1)S(1)} %bitcast.75), channel_id=1, source_target_pairs={{2,0},{4,2},{6,4},{8,6},{10,8},{12,10},{14,12},{3,1},{5,3},{7,5},{... | collective-permute-start | bytes 3080 | tf_op jit(solution)/shard_map/ppermute | solution.py:25
  140.6 7.0 %collective-permute-start.14 = (bf16[4,32,1]{1,0,2:T(4,128)(2,1)S(1)}, bf16[4,32,1]{1,0,2:T(4,128)(2,1)S(1)}, u32[]{:S(2)}, u32[]{:S(2)}) collective-permute-start(bf16[4,32,1]{1,0,2:T(4,128)(2,1)S(1)} %bitcast.74), channel_id=1, source_target_pairs={{1,0},{3,2},{5,4},{7,6},{9,8},{11,10},{13,12},{15,14},{17,16},{19,... | collective-permute-start | bytes 776 | tf_op jit(solution)/shard_map/ppermute | solution.py:25
  147.9 8.0 %collective-permute-start.15 = (f32[1,32,128]{2,1,0:T(8,128)S(1)}, f32[1,32,128]{2,1,0:T(8,128)S(1)}, u32[]{:S(2)}, u32[]{:S(2)}) collective-permute-start(f32[1,32,128]{2,1,0:T(8,128)S(1)} %get-tuple-element.30), channel_id=1, source_target_pairs={{0,16},{16,32},{32,48},{48,64},{64,80},{80,96},{96,112},{112,128},... | collective-permute-start | bytes 49160 | tf_op jit(solution)/shard_map/ppermute | solution.py:14
  149.9 7.5 %collective-permute-start.16 = (f32[1,32,128]{2,1,0:T(8,128)S(1)}, f32[1,32,128]{2,1,0:T(8,128)S(1)}, u32[]{:S(2)}, u32[]{:S(2)}) collective-permute-start(f32[1,32,128]{2,1,0:T(8,128)S(1)} %get-tuple-element.31), channel_id=1, source_target_pairs={{16,0},{32,16},{48,32},{64,48},{80,64},{96,80},{112,96},{128,112},... | collective-permute-start | bytes 49160 | tf_op jit(solution)/shard_map/ppermute | solution.py:17
  166.0 8.3 %collective-permute-start.20 = (f32[6,34,1]{2,1,0:T(8,128)S(1)}, f32[6,34,1]{2,1,0:T(8,128)S(1)}, u32[]{:S(2)}, u32[]{:S(2)}) collective-permute-start(f32[6,34,1]{2,1,0:T(8,128)S(1)} %get-tuple-element.15), channel_id=1, source_target_pairs={{1,0},{3,2},{5,4},{7,6},{9,8},{11,10},{13,12},{15,14},{17,16},{19,... | collective-permute-start | bytes 2456 | tf_op jit(solution)/shard_map/ppermute | solution.py:17
  174.4 8.9 %collective-permute-start.21 = (f32[1,32,128]{2,1,0:T(8,128)S(1)}, f32[1,32,128]{2,1,0:T(8,128)S(1)}, u32[]{:S(2)}, u32[]{:S(2)}) collective-permute-start(f32[1,32,128]{2,1,0:T(8,128)S(1)} %get-tuple-element.28), channel_id=1, source_target_pairs={{0,16},{16,32},{32,48},{48,64},{64,80},{80,96},{96,112},{112,128},... | collective-permute-start | bytes 49160 | tf_op jit(solution)/shard_map/ppermute | solution.py:14
  176.3 8.3 %collective-permute-start.22 = (f32[1,32,128]{2,1,0:T(8,128)S(1)}, f32[1,32,128]{2,1,0:T(8,128)S(1)}, u32[]{:S(2)}, u32[]{:S(2)}) collective-permute-start(f32[1,32,128]{2,1,0:T(8,128)S(1)} %get-tuple-element.29), channel_id=1, source_target_pairs={{16,0},{32,16},{48,32},{64,48},{80,64},{96,80},{112,96},{128,112},... | collective-permute-start | bytes 49160 | tf_op jit(solution)/shard_map/ppermute | solution.py:17
  193.0 8.3 %collective-permute-start.26 = (f32[6,34,1]{2,1,0:T(8,128)S(1)}, f32[6,34,1]{2,1,0:T(8,128)S(1)}, u32[]{:S(2)}, u32[]{:S(2)}) collective-permute-start(f32[6,34,1]{2,1,0:T(8,128)S(1)} %get-tuple-element.13), channel_id=1, source_target_pairs={{1,0},{3,2},{5,4},{7,6},{9,8},{11,10},{13,12},{15,14},{17,16},{19,... | collective-permute-start | bytes 2456 | tf_op jit(solution)/shard_map/ppermute | solution.py:17
  201.4 8.5 %collective-permute-start.27 = (f32[1,32,128]{2,1,0:T(8,128)S(1)}, f32[1,32,128]{2,1,0:T(8,128)S(1)}, u32[]{:S(2)}, u32[]{:S(2)}) collective-permute-start(f32[1,32,128]{2,1,0:T(8,128)S(1)} %get-tuple-element.26), channel_id=1, source_target_pairs={{0,16},{16,32},{32,48},{48,64},{64,80},{80,96},{96,112},{112,128},... | collective-permute-start | bytes 49160 | tf_op jit(solution)/shard_map/ppermute | solution.py:14
  203.3 7.9 %collective-permute-start.28 = (f32[1,32,128]{2,1,0:T(8,128)S(1)}, f32[1,32,128]{2,1,0:T(8,128)S(1)}, u32[]{:S(2)}, u32[]{:S(2)}) collective-permute-start(f32[1,32,128]{2,1,0:T(8,128)S(1)} %get-tuple-element.27), channel_id=1, source_target_pairs={{16,0},{32,16},{48,32},{64,48},{80,64},{96,80},{112,96},{128,112},... | collective-permute-start | bytes 49160 | tf_op jit(solution)/shard_map/ppermute | solution.py:17
  219.6 8.3 %collective-permute-start.32 = (f32[6,34,1]{2,1,0:T(8,128)S(1)}, f32[6,34,1]{2,1,0:T(8,128)S(1)}, u32[]{:S(2)}, u32[]{:S(2)}) collective-permute-start(f32[6,34,1]{2,1,0:T(8,128)S(1)} %get-tuple-element.11), channel_id=1, source_target_pairs={{1,0},{3,2},{5,4},{7,6},{9,8},{11,10},{13,12},{15,14},{17,16},{19,... | collective-permute-start | bytes 2456 | tf_op jit(solution)/shard_map/ppermute | solution.py:17
  (20 other events, 458.2 us)
where the time goes:
time: 233 us; the launch traced here: 229 us
  starting transfers between devices  98.3 us (42%)
  local copies, waits for them, and re-layouts  64.4 us (28%)
  waiting for transfers between devices  34.7 us (15%)
  matrix products  19.1 us (8%)
  other arithmetic  10.8 us (5%)
    ppermute x15, starting transfers between devices, extended(): lax.ppermute(lax.slice_in_dim(block, 0, width, axis=dim), axis, backward)  50.4 us
    ppermute x15, starting transfers between devices, extended(): lax.ppermute(lax.slice_in_dim(block, block.shape[dim] - width, None, axis...  38.5 us
    conv_general_dilated x5, local copies, waits for them, and re-layouts, affinities(): lax.conv_general_dilated(window[None], conv_weight, (1, 1, 1), 'VALID', d...  26.8 us
    ppermute x15, waiting for transfers between devices, extended(): lax.ppermute(lax.slice_in_dim(block, 0, width, axis=dim), axis, backward)  25.7 us
    conv_general_dilated x1, matrix products, affinities(): lax.conv_general_dilated(window[None], conv_weight, (1, 1, 1), 'VALID', d...  17.1 us
    ppermute x1, local copies, waits for them, and re-layouts, extended(): lax.ppermute(lax.slice_in_dim(block, 0, width, axis=dim), axis, backward)  9.75 us
    ppermute x1, local copies, waits for them, and re-layouts, extended(): lax.ppermute(lax.slice_in_dim(block, block.shape[dim] - width, None, axis...  9.69 us
    ppermute x3, starting transfers between devices, from_behind(): return lax.ppermute(x, axis, pairs)  9.45 us
  transfers between devices with their start and end apart: 33, of which 13 were waited for; matrix products, arithmetic and copies ran while one was open for 35% of the time, Pallas kernels for 0%

commit v1 on v0

v1 whole, which is shorter than its diff:
```python
import jax
import jax.numpy as jnp
from jax import lax
from jax.experimental import pallas as pl
from jax.experimental.pallas import tpu as pltpu
from jax.sharding import PartitionSpec as P

ROUNDS = 4
F32 = jnp.float32
BF16 = jnp.bfloat16
VMEM = pl.BlockSpec(memory_space=pltpu.VMEM)
SMEM = pl.BlockSpec(memory_space=pltpu.SMEM)
PARAMS = pltpu.CompilerParams(vmem_limit_bytes=48 * 2**20)


def swaps(axis):
    count = lax.axis_size(axis)

    def pairs(first):
        return [p for i in range(first, count - 1, 2) for p in ((i, i + 1), (i + 1, i))]

    return pairs(0), pairs(1)


def iota(shape, dim):
    return lax.broadcasted_iota(jnp.int32, shape, dim)


def pack_kernel(where_ref, x_ref, m_ref, s_ref, v_ref, zs_ref):
    gz = where_ref[2]
    for x in range(4):
        v_ref[x, 5:37] = jnp.swapaxes(x_ref[:, x], 0, 1)
    lane = iota((128, 128), 1)
    row = iota((128, 128), 0)
    base = jnp.where(gz == 0, 120, 0)
    hit = row == base + lane % 8
    acc = jnp.zeros((256, 128), F32)
    for y in range(16):
        sel = jnp.where(hit & (lane // 8 == y), 1.0, 0.0).astype(BF16)
        lhs = jnp.concatenate(
            [v_ref[x, 5 + 16 * half + y] for x in range(4) for half in range(2)], axis=0
        )
        acc = acc + jnp.dot(lhs, sel, preferred_element_type=F32)
    zs_ref[0:256] = acc.astype(BF16)
    lane = iota((32, 128), 1)
    edge = (lane >= jnp.where(gz == 0, 124, 0)) & (lane < jnp.where(gz == 0, 128, 4))
    packed = jnp.zeros((32, 128), F32)
    for x in range(4):
        mask = m_ref[x].astype(F32)
        seed = mask * s_ref[x].astype(F32)
        for slot, value in ((x, mask), (4 + x, seed)):
            value = jnp.where(edge, value, 0.0)
            packed = packed + (pltpu.roll(value, 8 * slot, 1) if slot else value)
    zs_ref[256:288] = packed.astype(BF16)


def unpack_ext(packed, slot, gz):
    lane = iota(packed.shape, 1)
    inside = (lane >= jnp.where(gz == 0, 0, 124)) & (lane < jnp.where(gz == 0, 4, 128))
    value = pltpu.roll(packed, (128 - 8 * slot) % 128, 1) if slot else packed
    return jnp.where(inside, value, 0.0)


def yface_kernel(where_ref, v_ref, zs_ref, zr_ref, m_ref, s_ref, pt_ref, ye_ref, yo_ref, ms_ref):
    odd = where_ref[1] % 2
    gz = where_ref[2]
    lane = iota((256, 128), 1) % 8
    own = pltpu.roll(zs_ref[0:256].astype(F32), jnp.where(gz == 0, 122, 5), 1)
    other = pltpu.roll(zr_ref[0:256].astype(F32), jnp.where(gz == 0, 2, 125), 1)
    own_from = jnp.where(gz == 0, 0, 5)
    other_from = jnp.where(gz == 0, 2, 0)
    packed = jnp.where((lane >= own_from) & (lane < own_from + 2), own, 0.0)
    packed = jnp.where((lane >= other_from) & (lane < other_from + 5), other, packed)
    packed = packed.astype(BF16).reshape(4, 2, 32, 128)
    pt_ref[...] = packed
    zmask = zr_ref[256:288].astype(F32)
    for x in range(4):
        mask = m_ref[x].astype(F32)
        seed = mask * s_ref[x].astype(F32)
        fields = (mask, seed, unpack_ext(zmask, x, gz), unpack_ext(zmask, 4 + x, gz))
        for f, value in enumerate(fields):
            ms_ref[0, x, 4 * f : 4 * f + 4] = value[28:32]
            ms_ref[1, x, 4 * f : 4 * f + 4] = value[0:4]

    def write(dst_ref, up):
        for x in range(4):
            first = 32 if up else 5
            for j in range(5):
                dst_ref[x, 32 * j : 32 * j + 32] = v_ref[x, first + j]
            dst_ref[x, 160:192] = pt_ref[x, 1 if up else 0]
            dst_ref[x, 192:208] = ms_ref[0 if up else 1, x].astype(BF16)

    @pl.when(odd == 0)
    def _():
        write(ye_ref, True)
        write(yo_ref, False)

    @pl.when(odd == 1)
    def _():
        write(ye_ref, False)
        write(yo_ref, True)


def xface_kernel(where_ref, v_in_ref, pt_ref, ye_ref, yo_ref, v_ref, xe_ref, xo_ref):
    odd_x = where_ref[0] % 2
    odd_y = where_ref[1] % 2

    def fill(low_ref, high_ref):
        for x in range(4):
            for j in range(5):
                v_ref[x, j] = low_ref[x, 32 * j : 32 * j + 32]
                v_ref[x, 37 + j] = high_ref[x, 32 * j : 32 * j + 32]
            v_ref[x, 42] = low_ref[x, 160:192]
            v_ref[x, 43] = pt_ref[x, 0]
            v_ref[x, 44] = pt_ref[x, 1]
            v_ref[x, 45] = high_ref[x, 160:192]

    @pl.when(odd_y == 0)
    def _():
        fill(yo_ref, ye_ref)

    @pl.when(odd_y == 1)
    def _():
        fill(ye_ref, yo_ref)

    even_face = jnp.where(odd_x == 0, 3, 0)
    xe_ref[...] = v_ref[even_face]
    xo_ref[...] = v_ref[3 - even_face]


def head(hidden, head_ref, head_bias):
    logits = jnp.dot(head_ref, hidden, preferred_element_type=F32) + head_bias
    return jax.nn.sigmoid(logits).astype(BF16).astype(F32)


def conv_slice(gz, refs, w, wp, bias, hw, hb, hwp, hbp, out_ref, ext_ref, x):
    lane = iota((32, 128), 1)

    def pair(t0, t1):
        cols = []
        for t in (t0, t1):
            cols.append(
                jnp.concatenate([r[pl.ds(t - 1, 3)].reshape(96, 128) for r in refs], axis=0)
            )
        part = jnp.dot(w, jnp.concatenate(cols, axis=1), preferred_element_type=F32)
        rows = []
        for i in range(2):
            one = part[:, 128 * i : 128 * i + 128]
            left = jnp.where(lane == 0, 0.0, pltpu.roll(one[0:32], 1, 1))
            right = jnp.where(lane == 127, 0.0, pltpu.roll(one[64:96], 127, 1))
            rows.append(jnp.maximum(one[32:64] + left + right + bias, 0.0).astype(BF16))
        return rows

    def group(starts, row):
        rows = []
        for t in starts:
            rows += pair(t, t + 1)
        value = head(jnp.concatenate(rows, axis=0), hw, hb)
        for c in range(3):
            out_ref[x, c, pl.ds(row, 8)] = value[8 * c : 8 * c + 8]

    @pl.loop(0, 4)
    def _(g):
        row = pl.multiple_of(8 * g, 8)
        group([row + 5 + 2 * i for i in range(4)], row)

    group([37, 39, 1, 3], 32)

    cols = [
        jnp.concatenate([r[42 + q] for r in refs], axis=0) for q in range(4)
    ]
    part = jnp.dot(wp, jnp.concatenate(cols, axis=1), preferred_element_type=F32)
    total = jnp.zeros((32, 512), F32)
    for dy in range(3):
        for dz in range(3):
            k = 3 * dy + dz
            shift = (-(8 * (dy - 1) + dz - 1)) % 512
            one = part[32 * k : 32 * k + 32]
            total = total + (pltpu.roll(one, shift, 1) if shift else one)
    hidden = jnp.maximum(total + bias[:, 0:1], 0.0).astype(BF16)
    value = head(hidden, hwp, hbp)
    row = iota((40, 512), 0)
    at = iota((40, 512), 1)
    mine = at // 8 - 16 == jnp.where(row < 36, row, row - 40)
    lhs = jnp.concatenate(
        [jnp.where(mine, jnp.broadcast_to(value[c : c + 1], (40, 512)), 0.0) for c in range(3)],
        axis=0,
    ).astype(BF16)
    k = iota((512, 128), 0) % 8
    to = iota((512, 128), 1)
    goal = jnp.where(gz == 0, (k + 126) % 128, (k + 123) % 128)
    first = jnp.where((k >= 1) & (k <= 5) & (to == goal), 1.0, 0.0).astype(BF16)
    spread = jnp.dot(lhs, first, preferred_element_type=F32)
    lane = iota((40, 128), 1)
    fixed = lane == jnp.where(gz == 0, 127, 0)
    for c in range(3):
        one = spread[40 * c : 40 * c + 40]
        out_ref[x, c] = jnp.where(fixed, one, out_ref[x, c])
        ext_ref[x, c] = jnp.where(fixed, 0.0, one)


def inner_kernel(where_ref, v_ref, w_ref, wp_ref, b_ref, hw_ref, hb_ref, hwp_ref, hbp_ref, out_ref, ext_ref):
    gz = where_ref[2]
    for x in range(2):
        refs = [v_ref.at[x + d] for d in range(3)]
        conv_slice(
            gz, refs, w_ref[...], wp_ref[...], b_ref[...], hw_ref[...], hb_ref[...], hwp_ref[...],
            hbp_ref[...], out_ref, ext_ref, x,
        )


def border_kernel(
    where_ref, v_ref, xe_ref, xo_ref, in_ref, in_ext_ref, ye_ref, yo_ref, zr_ref, m_ref, s_ref,
    w_ref, wp_ref, b_ref, hw_ref, hb_ref, hwp_ref, hbp_ref,
    aff_ref, e_ref, ext_ref, se_ref, so_ref,
    low_ref, high_ref, out_ref, oext_ref, mask_ref, mext_ref,
):
    odd_x = where_ref[0] % 2
    odd_y = where_ref[1] % 2
    gz = where_ref[2]

    @pl.when(odd_x == 0)
    def _():
        low_ref[...] = xo_ref[...]
        high_ref[...] = xe_ref[...]

    @pl.when(odd_x == 1)
    def _():
        low_ref[...] = xe_ref[...]
        high_ref[...] = xo_ref[...]

    for x, refs in (
        (0, [low_ref, v_ref.at[0], v_ref.at[1]]),
        (1, [v_ref.at[2], v_ref.at[3], high_ref]),
    ):
        conv_slice(
            gz, refs, w_ref[...], wp_ref[...], b_ref[...], hw_ref[...], hb_ref[...], hwp_ref[...],
            hbp_ref[...], out_ref, oext_ref, x,
        )

    zmask = zr_ref[256:288].astype(F32)
    for x in range(4):
        mask = m_ref[x].astype(F32)
        mask_ref[0, x, 0:32] = mask
        mask_ref[1, x, 0:32] = mask * s_ref[x].astype(F32)
        mext_ref[0, x, 0:32] = unpack_ext(zmask, x, gz)
        mext_ref[1, x, 0:32] = unpack_ext(zmask, 4 + x, gz)

    def fill(lower_ref, upper_ref):
        for x in range(4):
            lower = lower_ref[x, 192:208].astype(F32)
            upper = upper_ref[x, 192:208].astype(F32)
            for f in range(2):
                mask_ref[f, x, 32:36] = upper[4 * f : 4 * f + 4]
                mask_ref[f, x, 36:40] = lower[4 * f : 4 * f + 4]
                mext_ref[f, x, 32:36] = upper[8 + 4 * f : 12 + 4 * f]
                mext_ref[f, x, 36:40] = lower[8 + 4 * f : 12 + 4 * f]

    @pl.when(odd_y == 0)
    def _():
        fill(yo_ref, ye_ref)

    @pl.when(odd_y == 1)
    def _():
        fill(ye_ref, yo_ref)

    lane = iota((40, 128), 1)
    row = iota((40, 128), 0)

    def shift_y(value):
        return jnp.where(row == 36, 0.0, pltpu.roll(value, 1, 0))

    for x in range(4):
        main, ext = mask_ref[0, x], mext_ref[0, x]
        rolled, rolled_ext = pltpu.roll(main, 1, 1), pltpu.roll(ext, 1, 1)
        z_main = main * jnp.where(lane == 0, rolled_ext, rolled)
        z_ext = ext * jnp.where(lane == 0, rolled, rolled_ext)
        y_main, y_ext = main * shift_y(main), ext * shift_y(ext)
        x_main = main * mask_ref[0, x - 1] if x else main
        x_ext = ext * mext_ref[0, x - 1] if x else ext
        if 0 < x < 3:
            a = [in_ref[x - 1, c] for c in range(3)]
            aext = [in_ext_ref[x - 1, c] for c in range(3)]
        else:
            a = [out_ref[x // 3, c] for c in range(3)]
            aext = [oext_ref[x // 3, c] for c in range(3)]
        for c in range(3):
            aff_ref[c, x] = a[c][0:32].astype(BF16)
        slots = jnp.zeros((40, 128), F32)
        for f, (keep, keep_ext) in enumerate(((x_main, x_ext), (y_main, y_ext), (z_main, z_ext))):
            e_ref[x, f] = a[f] * keep
            ext_ref[x, f] = aext[f] * keep_ext
        e_ref[x, 3] = mask_ref[1, x]
        ext_ref[x, 3] = mext_ref[1, x]

    def send(dst_ref, order, last):
        packed = jnp.zeros((40, 128), F32)
        for j, x in enumerate(order):
            for f in range(4):
                value = ext_ref[x, f]
                slot = 4 * j + f
                packed = packed + (pltpu.roll(value, 8 * slot, 1) if slot else value)
                if j < 3:
                    dst_ref[slot] = e_ref[x, f].astype(BF16)
        dst_ref[12] = e_ref[order[3], 3].astype(BF16)
        dst_ref[13] = e_ref[order[3], 0].astype(BF16)
        dst_ref[14] = packed.astype(BF16)

    def send_up(dst_ref):
        send(dst_ref, (3, 2, 1, 0), None)

    def send_down(dst_ref):
        send(dst_ref, (0, 1, 2, 3), None)

    @pl.when(odd_x == 0)
    def _():
        send_up(se_ref)
        send_down(so_ref)

    @pl.when(odd_x == 1)
    def _():
        send_down(se_ref)
        send_up(so_ref)


def rounds_kernel(where_ref, e_ref, ext_ref, re_ref, ro_ref, m_ref, out_ref, all_ref, s_ref):
    odd_x = where_ref[0] % 2
    gz = where_ref[2]

    def place(src_ref, places, keep_last):
        packed = src_ref[14].astype(F32)
        for j, at in enumerate(places):
            for f in range(4):
                scale = (lambda v: v / 15.0) if f == 3 else (lambda v: v)
                ext = scale(unpack_ext(packed, 4 * j + f, gz))
                if j < 3:
                    main = scale(src_ref[4 * j + f].astype(F32))
                elif f == 3:
                    main = scale(src_ref[12].astype(F32))
                elif f == 0 and keep_last:
                    main = src_ref[13].astype(F32)
                else:
                    main, ext = jnp.zeros_like(packed), jnp.zeros_like(packed)
                if f == 3:
                    s_ref[0, at, 0] = main
                    s_ref[0, at, 1] = ext
                else:
                    all_ref[at, f, 0] = main
                    all_ref[at, f, 1] = ext

    @pl.when(odd_x == 0)
    def _():
        place(ro_ref, (3, 2, 1, 0), False)
        place(re_ref, (8, 9, 10, 11), True)

    @pl.when(odd_x == 1)
    def _():
        place(re_ref, (3, 2, 1, 0), False)
        place(ro_ref, (8, 9, 10, 11), True)

    for x in range(4):
        for f in range(3):
            all_ref[4 + x, f, 0] = e_ref[x, f]
            all_ref[4 + x, f, 1] = ext_ref[x, f]
        s_ref[0, 4 + x, 0] = e_ref[x, 3] / 15.0
        s_ref[0, 4 + x, 1] = ext_ref[x, 3] / 15.0

    lane = iota((40, 128), 1)

    def down(pair):
        a, b = pltpu.roll(pair[0], 1, 1), pltpu.roll(pair[1], 1, 1)
        return jnp.where(lane == 0, b, a), jnp.where(lane == 0, a, b)

    def up(pair):
        a, b = pltpu.roll(pair[0], 127, 1), pltpu.roll(pair[1], 127, 1)
        return jnp.where(lane == 127, b, a), jnp.where(lane == 127, a, b)

    for r in range(ROUNDS):
        src, dst = r % 2, (r + 1) % 2

        @pl.loop(r + 1, 11 - r)
        def _(x):
            here = (s_ref[src, x, 0], s_ref[src, x, 1])
            best = list(here)
            ez = (all_ref[x, 2, 0], all_ref[x, 2, 1])
            z_low = down(here)
            z_high = up(tuple(jnp.minimum(here[i], ez[i]) for i in range(2)))
            for i in range(2):
                ey = all_ref[x, 1, i]
                value = here[i]
                value = jnp.maximum(value, jnp.minimum(s_ref[src, x - 1, i], all_ref[x, 0, i]))
                value = jnp.maximum(value, jnp.minimum(s_ref[src, x + 1, i], all_ref[x + 1, 0, i]))
                value = jnp.maximum(value, jnp.minimum(pltpu.roll(here[i], 1, 0), ey))
                value = jnp.maximum(value, pltpu.roll(jnp.minimum(here[i], ey), 39, 0))
                value = jnp.maximum(value, jnp.minimum(z_low[i], ez[i]))
                value = jnp.maximum(value, z_high[i])
                s_ref[dst, x, i] = value

    for x in range(4):
        out_ref[x] = s_ref[ROUNDS % 2, 4 + x, 0, 0:32] * m_ref[x].astype(F32)


def call(kernel, shapes, args, scratch=(), aliases={}):
    return pl.pallas_call(
        kernel,
        out_shape=[jax.ShapeDtypeStruct(s, d) for s, d in shapes],
        in_specs=[SMEM] + [VMEM] * (len(args) - 1),
        out_specs=[VMEM] * len(shapes),
        scratch_shapes=[pltpu.VMEM(s, d) for s, d in scratch],
        input_output_aliases=aliases,
        compiler_params=PARAMS,
    )(*args)


def body(features, conv_weight, conv_bias, head_weight, head_bias, mask, seeds):
    where = jnp.stack([lax.axis_index(a) for a in ("gx", "gy", "gz")]).astype(jnp.int32)
    taps = jnp.transpose(conv_weight, (2, 3, 4, 0, 1))
    w = jnp.transpose(taps, (2, 3, 0, 1, 4)).reshape(96, 288)
    wp = jnp.transpose(taps, (1, 2, 3, 0, 4)).reshape(288, 96)
    bias = jnp.broadcast_to(conv_bias[:, None], (32, 128))
    eye = jnp.eye(8, dtype=BF16)
    hw = (head_weight[:, None, None, :] * eye[None, :, :, None]).reshape(24, 256)
    hb = jnp.broadcast_to(jnp.repeat(head_bias, 8)[:, None], (24, 128))
    hwp = jnp.zeros((8, 32), BF16).at[0:3].set(head_weight)
    hbp = jnp.zeros((8, 512), F32).at[0:3].set(jnp.broadcast_to(head_bias[:, None], (3, 512)))
    weights = (w, wp, bias, hw, hb, hwp, hbp)

    v, zs = call(
        pack_kernel, [((4, 46, 32, 128), BF16), ((288, 128), BF16)], (where, features, mask, seeds)
    )
    zr = lax.ppermute(zs, "gz", [(0, 1), (1, 0)])
    pt, ye, yo = call(
        yface_kernel,
        [((4, 2, 32, 128), BF16), ((4, 208, 128), BF16), ((4, 208, 128), BF16)],
        (where, v, zs, zr, mask, seeds),
        scratch=[((2, 4, 16, 128), F32)],
    )
    even, odd = swaps("gy")
    yo = lax.ppermute(yo, "gy", odd)
    ye = lax.ppermute(ye, "gy", even)
    v, xe, xo = call(
        xface_kernel,
        [((4, 46, 32, 128), BF16), ((46, 32, 128), BF16), ((46, 32, 128), BF16)],
        (where, v, pt, ye, yo),
        aliases={1: 0},
    )
    even, odd = swaps("gx")
    xo = lax.ppermute(xo, "gx", odd)
    xe = lax.ppermute(xe, "gx", even)
    inner, inner_ext = call(
        inner_kernel, [((2, 3, 40, 128), F32), ((2, 3, 40, 128), F32)], (where, v) + weights
    )
    affinity, e, ext, se, so = call(
        border_kernel,
        [
            ((3, 4, 32, 128), BF16),
            ((4, 4, 40, 128), F32),
            ((4, 4, 40, 128), F32),
            ((15, 40, 128), BF16),
            ((15, 40, 128), BF16),
        ],
        (where, v, xe, xo, inner, inner_ext, ye, yo, zr, mask, seeds) + weights,
        scratch=[
            ((46, 32, 128), BF16),
            ((46, 32, 128), BF16),
            ((2, 3, 40, 128), F32),
            ((2, 3, 40, 128), F32),
            ((2, 4, 40, 128), F32),
            ((2, 4, 40, 128), F32),
        ],
    )
    so = lax.ppermute(so, "gx", odd)
    se = lax.ppermute(se, "gx", even)
    (strength,) = call(
        rounds_kernel,
        [((4, 32, 128), F32)],
        (where, e, ext, se, so, mask),
        scratch=[((12, 3, 2, 40, 128), F32), ((2, 12, 2, 40, 128), F32)],
    )
    return (affinity, strength)


def solution(mesh):
    in_specs = (
        P(None, "gx", "gy", "gz"),
        P(),
        P(),
        P(),
        P(),
        P("gx", "gy", "gz"),
        P("gx", "gy", "gz"),
    )
    out_specs = (P(None, "gx", "gy", "gz"), P("gx", "gy", "gz"))
    return jax.shard_map(body, mesh=mesh, in_specs=in_specs, out_specs=out_specs, check_vma=False)
```

time: 233 us -> 62.8 us (0.27)
  the two profiles are of different devices: /device:TPU:14 before, /device:TPU:26 now
where the time goes in v1:
time: 62.8 us; the launch traced here: 62.4 us
  Pallas kernels  21.1 us (34%)
  starting transfers between devices  16.8 us (27%)
  waiting for transfers between devices  15.1 us (24%)
  local copies, waits for them, and re-layouts  8.44 us (13%)
  between operations  0.8 us (1%)
    pallas_call x6, Pallas kernels, call(): pl.pallas_call(kernel, out_shape=[jax.ShapeDtypeStruct(s, d) for s, d in...  21.1 us
    ppermute x1, starting transfers between devices, body(): xo = lax.ppermute(xo, 'gx', odd)  7.02 us
    ppermute x1, waiting for transfers between devices, body(): zr = lax.ppermute(zs, 'gz', [(0, 1), (1, 0)])  4.62 us
    ppermute x1, waiting for transfers between devices, body(): yo = lax.ppermute(yo, 'gy', odd)  4.61 us
    ppermute x1, waiting for transfers between devices, body(): so = lax.ppermute(so, 'gx', odd)  3.99 us
    ppermute x1, starting transfers between devices, body(): so = lax.ppermute(so, 'gx', odd)  3.91 us
    unnamed x18, local copies, waits for them, and re-layouts  2.93 us
    ppermute x1, starting transfers between devices, body(): yo = lax.ppermute(yo, 'gy', odd)  2.53 us
  transfers between devices with their start and end apart: 7, of which 4 were waited for; matrix products, arithmetic and copies ran while one was open for 9% of the time, Pallas kernels for 10%

profile of v1, /device:TPU:26, one launch (start us, length us, event | category | flops | bytes accessed | tf_op | source)
XLA Modules:
  0.0 62.4 jit_solution(11411981935799492983)
XLA Ops:
  0.7 1.2 %copy-done = bf16[32,4,32,128]{3,2,1,0:T(8,128)(2,1)S(1)} copy-done((bf16[32,4,32,128]{3,2,1,0:T(8,128)(2,1)S(1)}, bf16[32,4,32,128]{3,2,1,0:T(8,128)(2,1)}, u32[]{:S(2)}) %copy-start) | copy-done | bytes 1048600
  1.9 0.8 %copy-done.1 = s32[4,32,128]{2,1,0:T(8,128)S(1)} copy-done((s32[4,32,128]{2,1,0:T(8,128)S(1)}, s32[4,32,128]{2,1,0:T(8,128)}, u32[]{:S(2)}) %copy-start.1) | copy-done | bytes 65560
  2.8 0.8 %copy-done.3 = s32[4,32,128]{2,1,0:T(8,128)S(1)} copy-done((s32[4,32,128]{2,1,0:T(8,128)S(1)}, s32[4,32,128]{2,1,0:T(8,128)}, u32[]{:S(2)}) %copy-start.3) | copy-done | bytes 65560
  3.6 1.2 %shard_map.86 = (bf16[4,46,32,128]{3,2,1,0:T(8,128)(2,1)S(1)}, bf16[288,128]{1,0:T(8,128)(2,1)S(1)}) custom-call(s32[3]{0:T(128)S(1)} %pad_add_fusion.where_ref, bf16[32,4,32,128]{3,2,1,0:T(8,128)(2,1)S(1)} %copy-done, s32[4,32,128]{2,1,0:T(8,128)S(1)} %copy-done.1, s32[4,32,128]{2,1,0:T(8,128)S(1)} %copy-done.3), custom_call_target="tpu_custom_call" | custom-call | tf_op jit(solution)/shard_map/pallas_call | solution.py:404
  4.8 1.3 %collective-permute-start = (bf16[288,128]{1,0:T(8,128)(2,1)S(1)}, bf16[288,128]{1,0:T(8,128)(2,1)S(1)}, u32[]{:S(2)}, u32[]{:S(2)}) collective-permute-start(bf16[288,128]{1,0:T(8,128)(2,1)S(1)} %get-tuple-element.42.zs_ref), channel_id=1, source_target_pairs={{0,1},{1,0},{2,3},{3,2},{4,5},{5,4},{6,7},{7,6},{8,9},{9,8},{10,11... | collective-permute-start | bytes 221192 | tf_op jit(solution)/shard_map/ppermute | solution.py:431
  6.2 4.6 %collective-permute-done.zr_ref = bf16[288,128]{1,0:T(8,128)(2,1)S(1)} collective-permute-done((bf16[288,128]{1,0:T(8,128)(2,1)S(1)}, bf16[288,128]{1,0:T(8,128)(2,1)S(1)}, u32[]{:S(2)}, u32[]{:S(2)}) %collective-permute-start) | collective-permute-done | bytes 73760 | tf_op jit(solution)/shard_map/ppermute | solution.py:431
  10.8 0.7 %shard_map.87 = (bf16[4,2,32,128]{3,2,1,0:T(8,128)(2,1)S(1)}, bf16[4,208,128]{2,1,0:T(8,128)(2,1)S(1)}, bf16[4,208,128]{2,1,0:T(8,128)(2,1)S(1)}) custom-call(s32[3]{0:T(128)S(1)} %pad_add_fusion.where_ref, bf16[4,46,32,128]{3,2,1,0:T(8,128)(2,1)S(1)} %get-tuple-element.41.v_ref.v_in_ref, bf16[288,128]{1,0:T(8,128)(2,1)S(1)} %get-tuple-element.42.zs_ref, ...), custom_call_target="tpu_custom_call" | custom-call | tf_op jit(solution)/shard_map/pallas_call | solution.py:404
  11.5 0.1 collective-permute-start.1
  11.6 2.5 %collective-permute-start.2 = (bf16[4,208,128]{2,1,0:T(8,128)(2,1)S(1)}, bf16[4,208,128]{2,1,0:T(8,128)(2,1)S(1)}, u32[]{:S(2)}, u32[]{:S(2)}) collective-permute-start(bf16[4,208,128]{2,1,0:T(8,128)(2,1)S(1)} %get-tuple-element.45), channel_id=1, source_target_pairs={{2,4},{4,2},{6,8},{8,6},{10,12},{12,10},{3,5},{5,3},{7,9},{9,7},{1... | collective-permute-start | bytes 638984 | tf_op jit(solution)/shard_map/ppermute | solution.py:439
  14.1 4.6 %collective-permute-done.2.yo_ref = bf16[4,208,128]{2,1,0:T(8,128)(2,1)S(1)} collective-permute-done((bf16[4,208,128]{2,1,0:T(8,128)(2,1)S(1)}, bf16[4,208,128]{2,1,0:T(8,128)(2,1)S(1)}, u32[]{:S(2)}, u32[]{:S(2)}) %collective-permute-start.2) | collective-permute-done | bytes 213024 | tf_op jit(solution)/shard_map/ppermute | solution.py:439
  18.7 1.4 %shard_map.88 = (bf16[4,46,32,128]{3,2,1,0:T(8,128)(2,1)S(1)}, bf16[46,32,128]{2,1,0:T(8,128)(2,1)}, bf16[46,32,128]{2,1,0:T(8,128)(2,1)S(1)}) custom-call(s32[3]{0:T(128)S(1)} %pad_add_fusion.where_ref, bf16[4,46,32,128]{3,2,1,0:T(8,128)(2,1)S(1)} %get-tuple-element.41.v_ref.v_in_ref, ...), custom_call_target="tpu_custom_call", output_to_operand_aliasing={{0}: (1, {})} | custom-call | tf_op jit(solution)/shard_map/pallas_call | solution.py:404
  20.1 1.9 %collective-permute-start.3 = (bf16[46,32,128]{2,1,0:T(8,128)(2,1)}, bf16[46,32,128]{2,1,0:T(8,128)(2,1)S(1)}, u32[]{:S(2)}, u32[]{:S(2)}) collective-permute-start(bf16[46,32,128]{2,1,0:T(8,128)(2,1)} %get-tuple-element.47), channel_id=1, source_target_pairs={{0,16},{16,0},{32,48},{48,32},{64,80},{80,64},{96,112},{112,96},{1... | collective-permute-start | bytes 1130504 | tf_op jit(solution)/shard_map/ppermute | solution.py:449
  22.0 7.0 %collective-permute-start.4 = (bf16[46,32,128]{2,1,0:T(8,128)(2,1)S(1)}, bf16[46,32,128]{2,1,0:T(8,128)(2,1)S(1)}, u32[]{:S(2)}, u32[]{:S(2)}) collective-permute-start(bf16[46,32,128]{2,1,0:T(8,128)(2,1)S(1)} %get-tuple-element.48), channel_id=1, source_target_pairs={{16,32},{32,16},{48,64},{64,48},{80,96},{96,80},{112,128},{128,112... | collective-permute-start | bytes 1130504 | tf_op jit(solution)/shard_map/ppermute | solution.py:448
  29.1 0.9 %copy.12 = bf16[3,32,3,3,32]{4,3,2,1,0:T(4,128)(2,1)} copy(bf16[3,32,3,3,32]{4,1,0,3,2:T(8,128)(2,1)S(1)} %bitcast.8) | data formatting | bytes 110592 | tf_op jit(solution)/shard_map/transpose;transpose | solution.py:418
  29.9 1.2 %reshape.73.w_ref = bf16[96,288]{1,0:T(8,128)(2,1)S(1)} reshape(bf16[3,32,3,3,32]{4,3,2,1,0:T(4,128)(2,1)} %copy.12) | data formatting | bytes 110592 | tf_op jit(solution)/shard_map/reshape | solution.py:418
  31.2 1.8 %copy.13 = bf16[3,3,32,3,32]{4,3,2,1,0:T(4,128)(2,1)} copy(bf16[3,3,32,3,32]{4,2,1,0,3:T(8,128)(2,1)} %bitcast.7) | data formatting | bytes 110592 | tf_op jit(solution)/shard_map/transpose;transpose | solution.py:419
  33.0 1.1 %reshape.74.wp_ref = bf16[288,96]{1,0:T(8,128)(2,1)S(1)} reshape(bf16[3,3,32,3,32]{4,3,2,1,0:T(4,128)(2,1)} %copy.13) | data formatting | bytes 110592 | tf_op jit(solution)/shard_map/reshape | solution.py:419
  34.2 0.1 mul.20.hw_ref
  34.7 6.4 %shard_map.89 = (f32[2,3,40,128]{3,2,1,0:T(8,128)S(1)}, f32[2,3,40,128]{3,2,1,0:T(8,128)S(1)}) custom-call(s32[3]{0:T(128)S(1)} %pad_add_fusion.where_ref, bf16[4,46,32,128]{3,2,1,0:T(8,128)(2,1)S(1)} %get-tuple-element.46.v_ref, bf16[96,288]{1,0:T(8,128)(2,1)S(1)} %reshape.73.w_ref, bf16[288,96]{1,0:T(8,128)(2,1)S(1)} %reshape.74.wp_ref, ...), custom_call_target="tpu_custom_call" | custom-call | tf_op jit(solution)/shard_map/pallas_call | solution.py:404
  41.2 7.5 %shard_map.90 = (bf16[3,4,32,128]{3,2,1,0:T(8,128)(2,1)}, f32[4,4,40,128]{3,2,1,0:T(8,128)S(1)}, f32[4,4,40,128]{3,2,1,0:T(8,128)S(1)}, bf16[15,40,128]{2,1,0:T(8,128)(2,1)S(1)}, bf16[15,40,128]{2,1,0:T(8,128)(2,1)S(1)}) custom-call(s32[3]{0:T(128)S(1)} %pad_add_fusion.where_ref, bf16[4,46,32,128]{3,2,1,0:T(8,128)(2,1)S(1)} %get-tuple-element.46.v_ref, ...), custom_call_target="tpu_custom_call" | custom-call | tf_op jit(solution)/shard_map/pallas_call | solution.py:404
  48.7 3.9 %collective-permute-start.6 = (bf16[15,40,128]{2,1,0:T(8,128)(2,1)S(1)}, bf16[15,40,128]{2,1,0:T(8,128)(2,1)S(1)}, u32[]{:S(2)}, u32[]{:S(2)}) collective-permute-start(bf16[15,40,128]{2,1,0:T(8,128)(2,1)S(1)} %get-tuple-element.55), channel_id=1, source_target_pairs={{16,32},{32,16},{48,64},{64,48},{80,96},{96,80},{112,128},{128,112... | collective-permute-start | bytes 460808 | tf_op jit(solution)/shard_map/ppermute | solution.py:472
  52.6 1.9 %collective-permute-done.5.re_ref = bf16[15,40,128]{2,1,0:T(8,128)(2,1)S(1)} collective-permute-done((bf16[15,40,128]{2,1,0:T(8,128)(2,1)S(1)}, bf16[15,40,128]{2,1,0:T(8,128)(2,1)S(1)}, u32[]{:S(2)}, u32[]{:S(2)}) %collective-permute-start.5) | collective-permute-done | bytes 153632 | tf_op jit(solution)/shard_map/ppermute | solution.py:473
  54.5 4.0 %collective-permute-done.6.ro_ref = bf16[15,40,128]{2,1,0:T(8,128)(2,1)S(1)} collective-permute-done((bf16[15,40,128]{2,1,0:T(8,128)(2,1)S(1)}, bf16[15,40,128]{2,1,0:T(8,128)(2,1)S(1)}, u32[]{:S(2)}, u32[]{:S(2)}) %collective-permute-start.6) | collective-permute-done | bytes 153632 | tf_op jit(solution)/shard_map/ppermute | solution.py:472
  58.5 3.9 %shard_map.91 = f32[4,32,128]{2,1,0:T(8,128)} custom-call(s32[3]{0:T(128)S(1)} %pad_add_fusion.where_ref, f32[4,4,40,128]{3,2,1,0:T(8,128)S(1)} %get-tuple-element.52.e_ref, f32[4,4,40,128]{3,2,1,0:T(8,128)S(1)} %get-tuple-element.53.ext_ref, bf16[15,40,128]{2,1,0:T(8,128)(2,1)S(1)} %collective-permute-done.5.re_ref, ...), custom_call_target="tpu_custom_call" | custom-call | tf_op jit(solution)/shard_map/pallas_call | solution.py:404
  (29 shorter events, 0.6 us)
Async XLA Ops:
  0.7 1.2 %copy-start = (bf16[32,4,32,128]{3,2,1,0:T(8,128)(2,1)S(1)}, bf16[32,4,32,128]{3,2,1,0:T(8,128)(2,1)}, u32[]{:S(2)}) copy-start(bf16[32,4,32,128]{3,2,1,0:T(8,128)(2,1)} %x_ref.1) | copy-start | bytes 3145732
  1.9 0.8 %copy-start.1 = (s32[4,32,128]{2,1,0:T(8,128)S(1)}, s32[4,32,128]{2,1,0:T(8,128)}, u32[]{:S(2)}) copy-start(s32[4,32,128]{2,1,0:T(8,128)} %m_ref.7) | copy-start | bytes 196612
  2.8 0.8 %copy-start.3 = (s32[4,32,128]{2,1,0:T(8,128)S(1)}, s32[4,32,128]{2,1,0:T(8,128)}, u32[]{:S(2)}) copy-start(s32[4,32,128]{2,1,0:T(8,128)} %s_ref.5) | copy-start | bytes 196612
  4.8 5.9 %collective-permute-start = (bf16[288,128]{1,0:T(8,128)(2,1)S(1)}, bf16[288,128]{1,0:T(8,128)(2,1)S(1)}, u32[]{:S(2)}, u32[]{:S(2)}) collective-permute-start(bf16[288,128]{1,0:T(8,128)(2,1)S(1)} %get-tuple-element.42.zs_ref), channel_id=1, source_target_pairs={{0,1},{1,0},{2,3},{3,2},{4,5},{5,4},{6,7},{7,6},{8,9},{9,8},{10,11... | collective-permute-start | bytes 221192 | tf_op jit(solution)/shard_map/ppermute | solution.py:431
  10.8 18.3 %copy-start.5 = (bf16[32,32,3,3,3]{1,0,4,3,2:T(8,128)(2,1)S(1)}, bf16[32,32,3,3,3]{1,0,4,3,2:T(8,128)(2,1)}, u32[]{:S(2)}) copy-start(bf16[32,32,3,3,3]{1,0,4,3,2:T(8,128)(2,1)} %param.12) | copy-start | bytes 165892
  11.5 2.6 %collective-permute-start.1 = (bf16[4,208,128]{2,1,0:T(8,128)(2,1)S(1)}, bf16[4,208,128]{2,1,0:T(8,128)(2,1)S(1)}, u32[]{:S(2)}, u32[]{:S(2)}) collective-permute-start(bf16[4,208,128]{2,1,0:T(8,128)(2,1)S(1)} %get-tuple-element.44), channel_id=1, source_target_pairs={{0,2},{2,0},{4,6},{6,4},{8,10},{10,8},{12,14},{14,12},{1,3},{3,1},... | collective-permute-start | bytes 638984 | tf_op jit(solution)/shard_map/ppermute | solution.py:440
  11.6 7.2 %collective-permute-start.2 = (bf16[4,208,128]{2,1,0:T(8,128)(2,1)S(1)}, bf16[4,208,128]{2,1,0:T(8,128)(2,1)S(1)}, u32[]{:S(2)}, u32[]{:S(2)}) collective-permute-start(bf16[4,208,128]{2,1,0:T(8,128)(2,1)S(1)} %get-tuple-element.45), channel_id=1, source_target_pairs={{2,4},{4,2},{6,8},{8,6},{10,12},{12,10},{3,5},{5,3},{7,9},{9,7},{1... | collective-permute-start | bytes 638984 | tf_op jit(solution)/shard_map/ppermute | solution.py:439
  18.7 15.4 %copy-start.6 = (bf16[3,32]{1,0:T(4,128)(2,1)S(1)}, bf16[3,32]{1,0:T(4,128)(2,1)}, u32[]{:S(2)}) copy-start(bf16[3,32]{1,0:T(4,128)(2,1)} %param.14) | copy-start | bytes 580
  18.7 15.6 %copy-start.7 = (f32[3]{0:T(128)S(1)}, f32[3]{0:T(128)}, u32[]{:S(2)}) copy-start(f32[3]{0:T(128)} %param.15) | copy-start | bytes 40
  18.7 15.8 %copy-start.8 = (f32[32]{0:T(128)S(1)}, f32[32]{0:T(128)}, u32[]{:S(2)}) copy-start(f32[32]{0:T(128)} %param.13) | copy-start | bytes 388
  20.1 21.0 %collective-permute-start.3 = (bf16[46,32,128]{2,1,0:T(8,128)(2,1)}, bf16[46,32,128]{2,1,0:T(8,128)(2,1)S(1)}, u32[]{:S(2)}, u32[]{:S(2)}) collective-permute-start(bf16[46,32,128]{2,1,0:T(8,128)(2,1)} %get-tuple-element.47), channel_id=1, source_target_pairs={{0,16},{16,0},{32,48},{48,32},{64,80},{80,64},{96,112},{112,96},{1... | collective-permute-start | bytes 1130504 | tf_op jit(solution)/shard_map/ppermute | solution.py:449
  22.0 19.1 %collective-permute-start.4 = (bf16[46,32,128]{2,1,0:T(8,128)(2,1)S(1)}, bf16[46,32,128]{2,1,0:T(8,128)(2,1)S(1)}, u32[]{:S(2)}, u32[]{:S(2)}) collective-permute-start(bf16[46,32,128]{2,1,0:T(8,128)(2,1)S(1)} %get-tuple-element.48), channel_id=1, source_target_pairs={{16,32},{32,16},{48,64},{64,48},{80,96},{96,80},{112,128},{128,112... | collective-permute-start | bytes 1130504 | tf_op jit(solution)/shard_map/ppermute | solution.py:448
  29.9 11.2 %copy-start.2 = (s32[4,32,128]{2,1,0:T(8,128)S(1)}, s32[4,32,128]{2,1,0:T(8,128)}, u32[]{:S(2)}) copy-start(s32[4,32,128]{2,1,0:T(8,128)} %m_ref.7) | copy-start | bytes 196612
  29.9 11.2 %copy-start.4 = (s32[4,32,128]{2,1,0:T(8,128)S(1)}, s32[4,32,128]{2,1,0:T(8,128)}, u32[]{:S(2)}) copy-start(s32[4,32,128]{2,1,0:T(8,128)} %s_ref.5) | copy-start | bytes 196612
  48.7 5.8 %collective-permute-start.5 = (bf16[15,40,128]{2,1,0:T(8,128)(2,1)S(1)}, bf16[15,40,128]{2,1,0:T(8,128)(2,1)S(1)}, u32[]{:S(2)}, u32[]{:S(2)}) collective-permute-start(bf16[15,40,128]{2,1,0:T(8,128)(2,1)S(1)} %get-tuple-element.54), channel_id=1, source_target_pairs={{0,16},{16,0},{32,48},{48,32},{64,80},{80,64},{96,112},{112,96},{1... | collective-permute-start | bytes 460808 | tf_op jit(solution)/shard_map/ppermute | solution.py:473
  48.7 9.8 %collective-permute-start.6 = (bf16[15,40,128]{2,1,0:T(8,128)(2,1)S(1)}, bf16[15,40,128]{2,1,0:T(8,128)(2,1)S(1)}, u32[]{:S(2)}, u32[]{:S(2)}) collective-permute-start(bf16[15,40,128]{2,1,0:T(8,128)(2,1)S(1)} %get-tuple-element.55), channel_id=1, source_target_pairs={{16,32},{32,16},{48,64},{64,48},{80,96},{96,80},{112,128},{128,112... | collective-permute-start | bytes 460808 | tf_op jit(solution)/shard_map/ppermute | solution.py:472

commit v2 on v1

v2 whole, which is shorter than its diff:
```python
import jax
import jax.numpy as jnp
from jax import lax
from jax.experimental import pallas as pl
from jax.experimental.pallas import tpu as pltpu
from jax.sharding import PartitionSpec as P

ROUNDS = 4
F32 = jnp.float32
BF16 = jnp.bfloat16
VMEM = pl.BlockSpec(memory_space=pltpu.VMEM)
SMEM = pl.BlockSpec(memory_space=pltpu.SMEM)
HBM = pl.BlockSpec(memory_space=pltpu.HBM)
PARAMS = pltpu.CompilerParams(vmem_limit_bytes=12 * 2**20)


def swaps(axis):
    count = lax.axis_size(axis)

    def pairs(first):
        return [
            p
            for i in range(first, count + first, 2)
            for p in ((i % count, (i + 1) % count), ((i + 1) % count, i % count))
        ]

    return pairs(0), pairs(1)


def iota(shape, dim):
    return lax.broadcasted_iota(jnp.int32, shape, dim)


def pack_kernel(where_ref, x_hbm, m_hbm, s_hbm, v_ref, zs_ref, ms_ref, x_ref, m_ref, s_ref, sems):
    gz = where_ref[2]
    copies = [pltpu.make_async_copy(x_hbm.at[:, x], x_ref.at[x], sems.at[x]) for x in range(4)]
    copies += [
        pltpu.make_async_copy(m_hbm, m_ref, sems.at[4]),
        pltpu.make_async_copy(s_hbm, s_ref, sems.at[5]),
    ]
    for copy in copies:
        copy.start()
    lane = iota((128, 128), 1)
    row = iota((128, 128), 0)
    base = jnp.where(gz == 0, 120, 0)
    hit = row == base + lane % 8
    sels = [jnp.where(hit & (lane // 8 == y), 1.0, 0.0).astype(BF16) for y in range(16)]
    for x in range(4):
        copies[x].wait()
        v_ref[x, 5:37] = jnp.swapaxes(x_ref[x], 0, 1)
    acc = jnp.zeros((256, 128), F32)
    for y in range(16):
        lhs = jnp.concatenate(
            [v_ref[x, 5 + 16 * half + y] for x in range(4) for half in range(2)], axis=0
        )
        acc = acc + jnp.dot(lhs, sels[y], preferred_element_type=F32)
    zs_ref[0:256] = acc.astype(BF16)
    copies[4].wait()
    copies[5].wait()
    lane = iota((32, 128), 1)
    edge = (lane >= jnp.where(gz == 0, 124, 0)) & (lane < jnp.where(gz == 0, 128, 4))
    packed = jnp.zeros((32, 128), F32)
    for x in range(4):
        mask = m_ref[x].astype(F32)
        seed = mask * s_ref[x].astype(F32)
        ms_ref[0, x] = mask
        ms_ref[1, x] = seed
        for slot, value in ((x, mask), (4 + x, seed)):
            value = jnp.where(edge, value, 0.0)
            packed = packed + (pltpu.roll(value, 8 * slot, 1) if slot else value)
    zs_ref[256:288] = packed.astype(BF16)


def weights_kernel(
    t_hbm, b_hbm, h_hbm, hb_hbm, w_ref, wp_ref, bias_ref, hw_ref, hbias_ref, hwp_ref, hbp_ref,
    t_ref, b_ref, h_ref, hb_ref, sems,
):
    copies = [
        pltpu.make_async_copy(src, dst, sems.at[i])
        for i, (src, dst) in enumerate(
            ((t_hbm, t_ref), (b_hbm, b_ref), (h_hbm, h_ref), (hb_hbm, hb_ref))
        )
    ]
    for copy in copies:
        copy.start()
    for copy in copies:
        copy.wait()
    for dz in range(3):
        w_ref[32 * dz : 32 * dz + 32] = jnp.concatenate(
            [t_ref[3 * k + dz] for k in range(9)], axis=1
        )
    for k in range(9):
        wp_ref[32 * k : 32 * k + 32] = jnp.concatenate(
            [t_ref[9 * dx + k] for dx in range(3)], axis=1
        )
    across = jnp.broadcast_to(b_ref[...], (32, 32))
    diagonal = iota((32, 32), 0) == iota((32, 32), 1)
    column = jnp.sum(jnp.where(diagonal, across, 0.0), axis=1, keepdims=True)
    bias_ref[...] = jnp.broadcast_to(column, (32, 128))
    same = iota((8, 256), 0) == iota((8, 256), 1) // 32
    few = iota((8, 128), 0)
    hwp = jnp.zeros((8, 32), F32)
    hbp = jnp.zeros((8, 128), F32)
    heads = h_ref[...].astype(F32)
    for c in range(3):
        line = jnp.concatenate([heads[c : c + 1]] * 8, axis=1)
        hw_ref[8 * c : 8 * c + 8] = jnp.where(same, jnp.broadcast_to(line, (8, 256)), 0.0)
        hbias_ref[8 * c : 8 * c + 8] = jnp.full((8, 128), hb_ref[c], F32)
        hwp = jnp.where(few[:, 0:32] == c, jnp.broadcast_to(heads[c : c + 1], (8, 32)), hwp)
        hbp = jnp.where(few == c, hb_ref[c], hbp)
    hwp_ref[...] = hwp
    hbp_ref[...] = hbp


def unpack_ext(packed, slot, gz):
    lane = iota(packed.shape, 1)
    inside = (lane >= jnp.where(gz == 0, 0, 124)) & (lane < jnp.where(gz == 0, 4, 128))
    value = pltpu.roll(packed, (128 - 8 * slot) % 128, 1) if slot else packed
    return jnp.where(inside, value, 0.0)


def yface_kernel(where_ref, v_ref, zs_ref, zr_ref, ms_ref, pt_ref, ye_ref, yo_ref, block_ref):
    odd = where_ref[1] % 2
    gz = where_ref[2]
    lane = iota((256, 128), 1) % 8
    own = pltpu.roll(zs_ref[0:256].astype(F32), jnp.where(gz == 0, 122, 5), 1)
    other = pltpu.roll(zr_ref[0:256].astype(F32), jnp.where(gz == 0, 2, 125), 1)
    own_from = jnp.where(gz == 0, 0, 5)
    other_from = jnp.where(gz == 0, 2, 0)
    packed = jnp.where((lane >= own_from) & (lane < own_from + 2), own, 0.0)
    packed = jnp.where((lane >= other_from) & (lane < other_from + 5), other, packed)
    packed = packed.astype(BF16).reshape(4, 2, 32, 128)
    pt_ref[...] = packed
    zmask = zr_ref[256:288].astype(F32)
    for x in range(4):
        fields = (ms_ref[0, x], ms_ref[1, x], unpack_ext(zmask, x, gz), unpack_ext(zmask, 4 + x, gz))
        for f, value in enumerate(fields):
            block_ref[0, x, 4 * f : 4 * f + 4] = value[28:32]
            block_ref[1, x, 4 * f : 4 * f + 4] = value[0:4]

    def write(dst_ref, up):
        for x in range(4):
            first = 32 if up else 5
            for j in range(5):
                dst_ref[x, 32 * j : 32 * j + 32] = v_ref[x, first + j]
            dst_ref[x, 160:192] = pt_ref[x, 1 if up else 0]
            dst_ref[x, 192:208] = block_ref[0 if up else 1, x].astype(BF16)

    @pl.when(odd == 0)
    def _():
        write(ye_ref, True)
        write(yo_ref, False)

    @pl.when(odd == 1)
    def _():
        write(ye_ref, False)
        write(yo_ref, True)


def xface_kernel(where_ref, v_in_ref, pt_ref, ye_ref, yo_ref, v_ref, xe_ref, xo_ref):
    odd_x = where_ref[0] % 2
    odd_y = where_ref[1] % 2

    gy = where_ref[1]
    for x in range(4):
        v_ref[x, 5:37] = v_in_ref[x, 5:37]

    def fill(low_ref, high_ref):
        for x in range(4):
            for j in range(5):
                v_ref[x, j] = low_ref[x, 32 * j : 32 * j + 32]
                v_ref[x, 37 + j] = high_ref[x, 32 * j : 32 * j + 32]
            v_ref[x, 42] = low_ref[x, 160:192]
            v_ref[x, 43] = pt_ref[x, 0]
            v_ref[x, 44] = pt_ref[x, 1]
            v_ref[x, 45] = high_ref[x, 160:192]

    @pl.when(odd_y == 0)
    def _():
        fill(yo_ref, ye_ref)

    @pl.when(odd_y == 1)
    def _():
        fill(ye_ref, yo_ref)

    zero = jnp.zeros((32, 128), BF16)

    @pl.when(gy == 0)
    def _():
        for x in range(4):
            for tile in (0, 1, 2, 3, 4, 42):
                v_ref[x, tile] = zero

    @pl.when(gy == 7)
    def _():
        for x in range(4):
            for tile in (37, 38, 39, 40, 41, 45):
                v_ref[x, tile] = zero

    even_face = jnp.where(odd_x == 0, 3, 0)
    xe_ref[...] = v_ref[even_face]
    xo_ref[...] = v_ref[3 - even_face]


def head(hidden, head_ref, bias_ref):
    logits = jnp.dot(head_ref[...].astype(BF16), hidden, preferred_element_type=F32)
    logits = logits + jnp.tile(bias_ref[...], (1, logits.shape[1] // 128))
    return jax.nn.sigmoid(logits).astype(BF16).astype(F32)


def tile_of(row):
    return row + 5 if row < 36 else row - 35


def spread_matrix(gz):
    k = iota((512, 128), 0) % 8
    to = iota((512, 128), 1)
    goal = jnp.where(gz == 0, (k + 126) % 128, (k + 123) % 128)
    return jnp.where((k >= 1) & (k <= 5) & (to == goal), 1.0, 0.0).astype(BF16)


def conv_main(refs, weights, hid_ref, rows):
    lane = iota((32, 128), 1)
    first, last = lane == 0, lane == 127
    w, bias = weights[0][...], weights[2][...]
    for pair in zip(rows[0::2], rows[1::2]):
        cols = []
        for row in pair:
            t = tile_of(row)
            cols.append(
                jnp.concatenate([r[t - 1 : t + 2].reshape(96, 128) for r in refs], axis=0)
            )
        part = jnp.dot(w, jnp.concatenate(cols, axis=1), preferred_element_type=F32)
        for i, row in enumerate(pair):
            one = part[:, 128 * i : 128 * i + 128]
            left = jnp.where(first, 0.0, pltpu.roll(one[0:32], 1, 1))
            right = jnp.where(last, 0.0, pltpu.roll(one[64:96], 127, 1))
            hid = jnp.maximum(one[32:64] + left + right + bias, 0.0)
            hid_ref[32 * row : 32 * row + 32] = hid.astype(BF16)


def conv_packed(refs, weights, spread):
    _, wp_ref, b_ref, _, _, hwp_ref, hbp_ref = weights
    cols = [jnp.concatenate([r[42 + q] for r in refs], axis=0) for q in range(4)]
    part = jnp.dot(wp_ref[...], jnp.concatenate(cols, axis=1), preferred_element_type=F32)
    total = jnp.tile(b_ref[...], (1, 4))
    for dy in range(3):
        for dz in range(3):
            k = 3 * dy + dz
            shift = (-(8 * (dy - 1) + dz - 1)) % 512
            one = part[32 * k : 32 * k + 32]
            total = total + (pltpu.roll(one, shift, 1) if shift else one)
    value = head(jnp.maximum(total, 0.0).astype(BF16), hwp_ref, hbp_ref)
    row = iota((40, 512), 0)
    at = iota((40, 512), 1)
    mine = at // 8 - 16 == jnp.where(row < 36, row, row - 40)
    lhs = jnp.concatenate(
        [jnp.where(mine, jnp.broadcast_to(value[c : c + 1], (40, 512)), 0.0) for c in range(3)],
        axis=0,
    ).astype(BF16)
    return jnp.dot(lhs, spread, preferred_element_type=F32)


def conv_slice(gz, refs, weights, spread, hid_ref):
    conv_main(refs, weights, hid_ref, range(40))
    border = conv_packed(refs, weights, spread)
    hidden = jnp.concatenate([hid_ref[256 * g : 256 * g + 256] for g in range(5)], axis=1)
    value = head(hidden, weights[3], weights[4])
    fixed = iota((40, 128), 1) == jnp.where(gz == 0, 127, 0)
    out = []
    for c in range(3):
        main = jnp.concatenate(
            [value[8 * c : 8 * c + 8, 128 * g : 128 * g + 128] for g in range(5)], axis=0
        )
        one = border[40 * c : 40 * c + 40]
        out.append((jnp.where(fixed, one, main), jnp.where(fixed, 0.0, one)))
    return out


def inner_kernel(
    where_ref, v_ref, ye_ref, yo_ref, zr_ref, ms_ref, w_ref, wp_ref, b_ref, hw_ref, hb_ref, hwp_ref, hbp_ref,
    a_ref, e_ref, ext_ref, hid_ref, mask_ref, mext_ref,
):
    gy = where_ref[1]
    odd_y = gy % 2
    gz = where_ref[2]
    zmask = zr_ref[256:288].astype(F32)
    for x in range(4):
        for f in range(2):
            mask_ref[f, x, 0:32] = ms_ref[f, x]
            mext_ref[f, x, 0:32] = unpack_ext(zmask, 4 * f + x, gz)

    def fill(lower_ref, upper_ref):
        has_lower = jnp.where(gy == 0, 0.0, 1.0)
        has_upper = jnp.where(gy == 7, 0.0, 1.0)
        for x in range(4):
            lower = lower_ref[x, 192:208].astype(F32) * has_lower
            upper = upper_ref[x, 192:208].astype(F32) * has_upper
            for f in range(2):
                mask_ref[f, x, 32:36] = upper[4 * f : 4 * f + 4]
                mask_ref[f, x, 36:40] = lower[4 * f : 4 * f + 4]
                mext_ref[f, x, 32:36] = upper[8 + 4 * f : 12 + 4 * f]
                mext_ref[f, x, 36:40] = lower[8 + 4 * f : 12 + 4 * f]

    @pl.when(odd_y == 0)
    def _():
        fill(yo_ref, ye_ref)

    @pl.when(odd_y == 1)
    def _():
        fill(ye_ref, yo_ref)

    lane = iota((40, 128), 1)
    row = iota((40, 128), 0)

    def shift_y(value):
        return jnp.where(row == 36, 0.0, pltpu.roll(value, 1, 0))

    weights = (w_ref, wp_ref, b_ref, hw_ref, hb_ref, hwp_ref, hbp_ref)
    spread = spread_matrix(gz)
    for x in range(4):
        main, ext = mask_ref[0, x], mext_ref[0, x]
        rolled, rolled_ext = pltpu.roll(main, 1, 1), pltpu.roll(ext, 1, 1)
        z_main = main * jnp.where(lane == 0, rolled_ext, rolled)
        z_ext = ext * jnp.where(lane == 0, rolled, rolled_ext)
        y_main, y_ext = main * shift_y(main), ext * shift_y(ext)
        x_main = main * mask_ref[0, x - 1] if x else main
        x_ext = ext * mext_ref[0, x - 1] if x else ext
        keep = ((x_main, x_ext), (y_main, y_ext), (z_main, z_ext))
        if 0 < x < 3:
            refs = [v_ref.at[x - 1 + d] for d in range(3)]
            a = conv_slice(gz, refs, weights, spread, hid_ref.at[x - 1])
            for f in range(3):
                a_ref[f, x] = a[f][0][0:32].astype(BF16)
                e_ref[x, f] = a[f][0] * keep[f][0]
                ext_ref[x, f] = a[f][1] * keep[f][1]
        else:
            for f in range(3):
                e_ref[x, f] = keep[f][0]
                ext_ref[x, f] = keep[f][1]
        e_ref[x, 3] = mask_ref[1, x]
        ext_ref[x, 3] = mext_ref[1, x]


def border_kernel(
    where_ref, v_ref, xe_ref, xo_ref, a_in, e_in, ext_in, w_ref, wp_ref, b_ref, hw_ref, hb_ref, hwp_ref, hbp_ref,
    a_ref, e_ref, ext_ref, se_ref, so_ref, low_ref, high_ref, hid_ref,
):
    gx = where_ref[0]
    odd_x = gx % 2
    gz = where_ref[2]

    @pl.when(odd_x == 0)
    def _():
        low_ref[...] = xo_ref[...]
        high_ref[...] = xe_ref[...]

    @pl.when(odd_x == 1)
    def _():
        low_ref[...] = xe_ref[...]
        high_ref[...] = xo_ref[...]

    @pl.when(gx == 0)
    def _():
        low_ref[...] = jnp.zeros_like(low_ref)

    @pl.when(gx == 15)
    def _():
        high_ref[...] = jnp.zeros_like(high_ref)

    for x in (1, 2):
        a_ref[:, x] = a_in[:, x]
        e_ref[x] = e_in[x]
        ext_ref[x] = ext_in[x]
    for x in (0, 3):
        e_ref[x, 3] = e_in[x, 3]
        ext_ref[x, 3] = ext_in[x, 3]

    weights = (w_ref, wp_ref, b_ref, hw_ref, hb_ref, hwp_ref, hbp_ref)
    spread = spread_matrix(gz)
    for x, refs in (
        (0, [low_ref, v_ref.at[0], v_ref.at[1]]),
        (3, [v_ref.at[2], v_ref.at[3], high_ref]),
    ):
        a = conv_slice(gz, refs, weights, spread, hid_ref.at[x // 3])
        for f in range(3):
            a_ref[f, x] = a[f][0][0:32].astype(BF16)
            e_ref[x, f] = a[f][0] * e_in[x, f]
            ext_ref[x, f] = a[f][1] * ext_in[x, f]

    def send(dst_ref, order):
        packed = jnp.zeros((40, 128), F32)
        for j, x in enumerate(order):
            for f in range(4):
                value = ext_ref[x, f]
                slot = 4 * j + f
                packed = packed + (pltpu.roll(value, 8 * slot, 1) if slot else value)
                if j < 3:
                    dst_ref[slot] = e_ref[x, f].astype(BF16)
        dst_ref[12] = e_ref[order[3], 3].astype(BF16)
        dst_ref[13] = e_ref[order[3], 0].astype(BF16)
        dst_ref[14] = packed.astype(BF16)

    @pl.when(odd_x == 0)
    def _():
        send(se_ref, (3, 2, 1, 0))
        send(so_ref, (0, 1, 2, 3))

    @pl.when(odd_x == 1)
    def _():
        send(se_ref, (0, 1, 2, 3))
        send(so_ref, (3, 2, 1, 0))


def rounds_kernel(where_ref, e_ref, ext_ref, re_ref, ro_ref, ms_ref, out_ref, all_ref, s_ref):
    gx = where_ref[0]
    odd_x = gx % 2
    has_low = jnp.where(gx == 0, 0.0, 1.0)
    has_high = jnp.where(gx == 15, 0.0, 1.0)
    gz = where_ref[2]

    def place(src_ref, places, keep_last):
        has = has_high if keep_last else has_low
        packed = src_ref[14].astype(F32) * has
        for j, at in enumerate(places):
            for f in range(4):
                scale = (lambda v: v / 15.0) if f == 3 else (lambda v: v)
                ext = scale(unpack_ext(packed, 4 * j + f, gz))
                if j < 3:
                    main = scale(src_ref[4 * j + f].astype(F32) * has)
                elif f == 3:
                    main = scale(src_ref[12].astype(F32) * has)
                elif f == 0 and keep_last:
                    main = src_ref[13].astype(F32) * has
                else:
                    main, ext = jnp.zeros_like(packed), jnp.zeros_like(packed)
                if f == 3:
                    s_ref[0, at, 0] = main
                    s_ref[0, at, 1] = ext
                else:
                    all_ref[at, f, 0] = main
                    all_ref[at, f, 1] = ext

    @pl.when(odd_x == 0)
    def _():
        place(ro_ref, (3, 2, 1, 0), False)
        place(re_ref, (8, 9, 10, 11), True)

    @pl.when(odd_x == 1)
    def _():
        place(re_ref, (3, 2, 1, 0), False)
        place(ro_ref, (8, 9, 10, 11), True)

    for x in range(4):
        for f in range(3):
            all_ref[4 + x, f, 0] = e_ref[x, f]
            all_ref[4 + x, f, 1] = ext_ref[x, f]
        s_ref[0, 4 + x, 0] = e_ref[x, 3] / 15.0
        s_ref[0, 4 + x, 1] = ext_ref[x, 3] / 15.0

    lane = iota((40, 128), 1)

    def down(pair):
        a, b = pltpu.roll(pair[0], 1, 1), pltpu.roll(pair[1], 1, 1)
        return jnp.where(lane == 0, b, a), jnp.where(lane == 0, a, b)

    def up(pair):
        a, b = pltpu.roll(pair[0], 127, 1), pltpu.roll(pair[1], 127, 1)
        return jnp.where(lane == 127, b, a), jnp.where(lane == 127, a, b)

    for r in range(ROUNDS):
        src, dst = r % 2, (r + 1) % 2

        for x in range(r + 1, 11 - r):
            here = (s_ref[src, x, 0], s_ref[src, x, 1])
            best = list(here)
            ez = (all_ref[x, 2, 0], all_ref[x, 2, 1])
            z_low = down(here)
            z_high = up(tuple(jnp.minimum(here[i], ez[i]) for i in range(2)))
            for i in range(2):
                ey = all_ref[x, 1, i]
                value = here[i]
                value = jnp.maximum(value, jnp.minimum(s_ref[src, x - 1, i], all_ref[x, 0, i]))
                value = jnp.maximum(value, jnp.minimum(s_ref[src, x + 1, i], all_ref[x + 1, 0, i]))
                value = jnp.maximum(value, jnp.minimum(pltpu.roll(here[i], 1, 0), ey))
                value = jnp.maximum(value, pltpu.roll(jnp.minimum(here[i], ey), 39, 0))
                value = jnp.maximum(value, jnp.minimum(z_low[i], ez[i]))
                value = jnp.maximum(value, z_high[i])
                s_ref[dst, x, i] = value

    for x in range(4):
        out_ref[x] = s_ref[ROUNDS % 2, 4 + x, 0, 0:32] * ms_ref[0, x]


def stay(value):
    return pltpu.with_memory_space_constraint(value, pltpu.HBM)


def call(kernel, shapes, args, scratch=(), aliases={}, specs=None):
    return pl.pallas_call(
        kernel,
        out_shape=[jax.ShapeDtypeStruct(s, d) for s, d in shapes],
        in_specs=specs or [SMEM] + [VMEM] * (len(args) - 1),
        out_specs=[VMEM] * len(shapes),
        scratch_shapes=[pltpu.VMEM(*s) if isinstance(s[0], tuple) else s[0](*s[1:]) for s in scratch],
        input_output_aliases=aliases,
        compiler_params=PARAMS,
    )(*args)


def body(features, conv_weight, conv_bias, head_weight, head_bias, mask, seeds):
    where = jnp.stack([lax.axis_index(a) for a in ("gx", "gy", "gz")]).astype(jnp.int32)

    v, zs, ms = call(
        pack_kernel,
        [((4, 46, 32, 128), BF16), ((288, 128), BF16), ((2, 4, 32, 128), F32)],
        (where, *(stay(a) for a in (features, mask, seeds))),
        scratch=[
            ((4, 32, 32, 128), BF16),
            ((4, 32, 128), jnp.int32),
            ((4, 32, 128), jnp.int32),
            (pltpu.SemaphoreType.DMA, (6,)),
        ],
        specs=[SMEM, HBM, HBM, HBM],
    )
    zs, conv_weight, conv_bias, head_weight, head_bias = lax.optimization_barrier(
        (zs, conv_weight, conv_bias, head_weight, head_bias)
    )
    zr = lax.ppermute(zs, "gz", [(0, 1), (1, 0)])
    taps = jnp.transpose(conv_weight, (2, 3, 4, 0, 1)).reshape(27, 32, 32)
    forms = call(
        weights_kernel,
        [
            ((96, 288), BF16),
            ((288, 96), BF16),
            ((32, 128), F32),
            ((24, 256), F32),
            ((24, 128), F32),
            ((8, 32), F32),
            ((8, 128), F32),
        ],
        tuple(stay(a) for a in (taps, conv_bias.reshape(1, 32), head_weight, head_bias)),
        scratch=[
            ((27, 32, 32), BF16),
            ((1, 32), F32),
            ((3, 32), BF16),
            (pltpu.SMEM, (3,), F32),
            (pltpu.SemaphoreType.DMA, (4,)),
        ],
        specs=[HBM] * 4,
    )
    zr, *weights = lax.optimization_barrier((zr, *forms))
    weights = tuple(weights)
    pt, ye, yo = call(
        yface_kernel,
        [((4, 2, 32, 128), BF16), ((4, 208, 128), BF16), ((4, 208, 128), BF16)],
        (where, v, zs, zr, ms),
        scratch=[((2, 4, 16, 128), F32)],
    )
    even, odd = swaps("gy")
    yo = lax.ppermute(yo, "gy", odd)
    ye = lax.ppermute(ye, "gy", even)
    v, xe, xo = call(
        xface_kernel,
        [((4, 46, 32, 128), BF16), ((46, 32, 128), BF16), ((46, 32, 128), BF16)],
        (where, v, pt, ye, yo),
    )
    even, odd = swaps("gx")
    xo = lax.ppermute(xo, "gx", odd)
    xe = lax.ppermute(xe, "gx", even)
    affinity, e, ext = call(
        inner_kernel,
        [((3, 4, 32, 128), BF16), ((4, 4, 40, 128), F32), ((4, 4, 40, 128), F32)],
        (where, v, ye, yo, zr, ms) + weights,
        scratch=[((2, 1280, 128), BF16), ((2, 4, 40, 128), F32), ((2, 4, 40, 128), F32)],
    )
    affinity, e, ext, se, so = call(
        border_kernel,
        [
            ((3, 4, 32, 128), BF16),
            ((4, 4, 40, 128), F32),
            ((4, 4, 40, 128), F32),
            ((15, 40, 128), BF16),
            ((15, 40, 128), BF16),
        ],
        (where, v, xe, xo, affinity, e, ext) + weights,
        scratch=[((46, 32, 128), BF16), ((46, 32, 128), BF16), ((2, 1280, 128), BF16)],
    )
    so = lax.ppermute(so, "gx", odd)
    se = lax.ppermute(se, "gx", even)
    (strength,) = call(
        rounds_kernel,
        [((4, 32, 128), F32)],
        (where, e, ext, se, so, ms),
        scratch=[((12, 3, 2, 40, 128), F32), ((2, 12, 2, 40, 128), F32)],
    )
    return (affinity, strength)


def solution(mesh):
    in_specs = (
        P(None, "gx", "gy", "gz"),
        P(),
        P(),
        P(),
        P(),
        P("gx", "gy", "gz"),
        P("gx", "gy", "gz"),
    )
    out_specs = (P(None, "gx", "gy", "gz"), P("gx", "gy", "gz"))
    return jax.shard_map(body, mesh=mesh, in_specs=in_specs, out_specs=out_specs, check_vma=False)
```

time: 62.8 us -> 48.2 us (0.77)
  the two profiles are of different devices: /device:TPU:26 before, /device:TPU:6 now
where the time goes in v2:
time: 48.2 us; the launch traced here: 48.1 us
  starting transfers between devices  16.7 us (35%)
  waiting for transfers between devices  15.8 us (33%)
  Pallas kernels  14.8 us (31%)
  between operations  0.7 us (1%)
    pallas_call x7, Pallas kernels, call(): pl.pallas_call(kernel, out_shape=[jax.ShapeDtypeStruct(s, d) for s, d in...  14.8 us
    ppermute x1, starting transfers between devices, body(): xo = lax.ppermute(xo, 'gx', odd)  5.96 us
    ppermute x1, waiting for transfers between devices, body(): xo = lax.ppermute(xo, 'gx', odd)  5.61 us
    ppermute x1, starting transfers between devices, body(): so = lax.ppermute(so, 'gx', odd)  4.45 us
    ppermute x1, waiting for transfers between devices, body(): yo = lax.ppermute(yo, 'gy', odd)  3.91 us
    ppermute x1, starting transfers between devices, body(): zr = lax.ppermute(zs, 'gz', [(0, 1), (1, 0)])  3.28 us
    ppermute x1, waiting for transfers between devices, body(): so = lax.ppermute(so, 'gx', odd)  2.39 us
    ppermute x1, starting transfers between devices, body(): xe = lax.ppermute(xe, 'gx', even)  2.01 us
  transfers between devices with their start and end apart: 7, of which 6 were waited for; matrix products, arithmetic and copies ran while one was open for 0% of the time, Pallas kernels for 9%

profile of v2, /device:TPU:6, one launch (start us, length us, event | category | flops | bytes accessed | tf_op | source)
XLA Modules:
  0.0 48.1 jit_solution(4628455878127111007)
XLA Ops:
  0.6 0.1 pad_add_fusion.where_ref
  0.7 2.4 %shard_map.86 = (bf16[4,46,32,128]{3,2,1,0:T(8,128)(2,1)S(1)}, bf16[288,128]{1,0:T(8,128)(2,1)S(1)}, f32[2,4,32,128]{3,2,1,0:T(8,128)S(1)}) custom-call(s32[3]{0:T(128)S(1)} %pad_add_fusion.where_ref, bf16[32,4,32,128]{3,2,1,0:T(8,128)(2,1)} %x_hbm.1, s32[4,32,128]{2,1,0:T(8,128)} %m_hbm.1, s32[4,32,128]{2,1,0:T(8,128)} %s_hbm.1), custom_call_target="tpu_custom_call" | custom-call | tf_op jit(solution)/shard_map/pallas_call | solution.py:500
  3.1 3.3 %collective-permute-start = (bf16[288,128]{1,0:T(8,128)(2,1)S(1)}, bf16[288,128]{1,0:T(8,128)(2,1)S(1)}, u32[]{:S(2)}, u32[]{:S(2)}) collective-permute-start(bf16[288,128]{1,0:T(8,128)(2,1)S(1)} %get-tuple-element.41.zs_ref), channel_id=1, source_target_pairs={{0,1},{1,0},{2,3},{3,2},{4,5},{5,4},{6,7},{7,6},{8,9},{9,8},{10,11... | collective-permute-start | bytes 221192 | tf_op jit(solution)/shard_map/ppermute | solution.py:529
  6.4 1.2 %shard_map.87 = (bf16[96,288]{1,0:T(8,128)(2,1)S(1)}, bf16[288,96]{1,0:T(8,128)(2,1)S(1)}, f32[32,128]{1,0:T(8,128)S(1)}, f32[24,256]{1,0:T(8,128)S(1)}, f32[24,...) custom-call(bf16[27,32,32]{2,1,0:T(8,128)(2,1)} %bitcast.7, f32[1,32]{1,0:T(1,128)} %bitcast.8, ...), custom_call_target="tpu_custom_call" | custom-call | tf_op jit(solution)/shard_map/pallas_call | solution.py:500
  7.5 1.5 %collective-permute-done.zr_ref = bf16[288,128]{1,0:T(8,128)(2,1)S(1)} collective-permute-done((bf16[288,128]{1,0:T(8,128)(2,1)S(1)}, bf16[288,128]{1,0:T(8,128)(2,1)S(1)}, u32[]{:S(2)}, u32[]{:S(2)}) %collective-permute-start) | collective-permute-done | bytes 73760 | tf_op jit(solution)/shard_map/ppermute | solution.py:529
  9.0 0.7 %shard_map.88 = (bf16[4,2,32,128]{3,2,1,0:T(8,128)(2,1)S(1)}, bf16[4,208,128]{2,1,0:T(8,128)(2,1)S(1)}, bf16[4,208,128]{2,1,0:T(8,128)(2,1)S(1)}) custom-call(s32[3]{0:T(128)S(1)} %pad_add_fusion.where_ref, bf16[4,46,32,128]{3,2,1,0:T(8,128)(2,1)S(1)} %get-tuple-element.39.v_ref.v_in_ref, bf16[288,128]{1,0:T(8,128)(2,1)S(1)} %get-tuple-element.41.zs_ref, ...), custom_call_target="tpu_custom_call" | custom-call | tf_op jit(solution)/shard_map/pallas_call | solution.py:500
  9.7 0.1 collective-permute-start.1
  9.8 0.9 %collective-permute-start.2 = (bf16[4,208,128]{2,1,0:T(8,128)(2,1)S(1)}, bf16[4,208,128]{2,1,0:T(8,128)(2,1)S(1)}, u32[]{:S(2)}, u32[]{:S(2)}) collective-permute-start(bf16[4,208,128]{2,1,0:T(8,128)(2,1)S(1)} %get-tuple-element.57), channel_id=1, source_target_pairs={{2,4},{4,2},{6,8},{8,6},{10,12},{12,10},{14,0},{0,14},{3,5},{5,3},... | collective-permute-start | bytes 638984 | tf_op jit(solution)/shard_map/ppermute | solution.py:561
  10.7 0.5 %collective-permute-done.1.ye_ref = bf16[4,208,128]{2,1,0:T(8,128)(2,1)S(1)} collective-permute-done((bf16[4,208,128]{2,1,0:T(8,128)(2,1)S(1)}, bf16[4,208,128]{2,1,0:T(8,128)(2,1)S(1)}, u32[]{:S(2)}, u32[]{:S(2)}) %collective-permute-start.1) | collective-permute-done | bytes 213024 | tf_op jit(solution)/shard_map/ppermute | solution.py:562
  11.3 3.9 %collective-permute-done.2.yo_ref = bf16[4,208,128]{2,1,0:T(8,128)(2,1)S(1)} collective-permute-done((bf16[4,208,128]{2,1,0:T(8,128)(2,1)S(1)}, bf16[4,208,128]{2,1,0:T(8,128)(2,1)S(1)}, u32[]{:S(2)}, u32[]{:S(2)}) %collective-permute-start.2) | collective-permute-done | bytes 213024 | tf_op jit(solution)/shard_map/ppermute | solution.py:561
  15.2 0.7 %shard_map.89 = (bf16[4,46,32,128]{3,2,1,0:T(8,128)(2,1)S(1)}, bf16[46,32,128]{2,1,0:T(8,128)(2,1)S(1)}, bf16[46,32,128]{2,1,0:T(8,128)(2,1)S(1)}) custom-call(s32[3]{0:T(128)S(1)} %pad_add_fusion.where_ref, bf16[4,46,32,128]{3,2,1,0:T(8,128)(2,1)S(1)} %get-tuple-element.39.v_ref.v_in_ref, bf16[4,2,32,128]{3,2,1,0:T(8,128)(2,1)S(1)} %get-tuple-element.55.pt_ref, ...), custom_call_target="tpu_custom_call" | custom-call | tf_op jit(solution)/shard_map/pallas_call | solution.py:500
  15.9 2.0 %collective-permute-start.3 = (bf16[46,32,128]{2,1,0:T(8,128)(2,1)S(1)}, bf16[46,32,128]{2,1,0:T(8,128)(2,1)S(1)}, u32[]{:S(2)}, u32[]{:S(2)}) collective-permute-start(bf16[46,32,128]{2,1,0:T(8,128)(2,1)S(1)} %get-tuple-element.59), channel_id=1, source_target_pairs={{0,16},{16,0},{32,48},{48,32},{64,80},{80,64},{96,112},{112,96},{1... | collective-permute-start | bytes 1130504 | tf_op jit(solution)/shard_map/ppermute | solution.py:570
  17.9 6.0 %collective-permute-start.4 = (bf16[46,32,128]{2,1,0:T(8,128)(2,1)S(1)}, bf16[46,32,128]{2,1,0:T(8,128)(2,1)S(1)}, u32[]{:S(2)}, u32[]{:S(2)}) collective-permute-start(bf16[46,32,128]{2,1,0:T(8,128)(2,1)S(1)} %get-tuple-element.60), channel_id=1, source_target_pairs={{16,32},{32,16},{48,64},{64,48},{80,96},{96,80},{112,128},{128,112... | collective-permute-start | bytes 1130504 | tf_op jit(solution)/shard_map/ppermute | solution.py:569
  23.8 3.4 %shard_map.90 = (bf16[3,4,32,128]{3,2,1,0:T(8,128)(2,1)S(1)}, f32[4,4,40,128]{3,2,1,0:T(8,128)S(1)}, f32[4,4,40,128]{3,2,1,0:T(8,128)S(1)}) custom-call(s32[3]{0:T(128)S(1)} %pad_add_fusion.where_ref, bf16[4,46,32,128]{3,2,1,0:T(8,128)(2,1)S(1)} %get-tuple-element.58.v_ref, bf16[4,208,128]{2,1,0:T(8,128)(2,1)S(1)} %collective-permute-done.1.ye_ref, ...), custom_call_target="tpu_custom_call" | custom-call | tf_op jit(solution)/shard_map/pallas_call | solution.py:500
  27.2 0.0 collective-permute-done.3.xe_ref
  27.2 5.6 %collective-permute-done.4.xo_ref = bf16[46,32,128]{2,1,0:T(8,128)(2,1)S(1)} collective-permute-done((bf16[46,32,128]{2,1,0:T(8,128)(2,1)S(1)}, bf16[46,32,128]{2,1,0:T(8,128)(2,1)S(1)}, u32[]{:S(2)}, u32[]{:S(2)}) %collective-permute-start.4) | collective-permute-done | bytes 376864 | tf_op jit(solution)/shard_map/ppermute | solution.py:569
  32.8 4.3 %shard_map.91 = (bf16[3,4,32,128]{3,2,1,0:T(8,128)(2,1)}, f32[4,4,40,128]{3,2,1,0:T(8,128)S(1)}, f32[4,4,40,128]{3,2,1,0:T(8,128)S(1)}, bf16[15,40,128]{2,1,0:T(8,128)(2,1)S(1)}, bf16[15,40,128]{2,1,0:T(8,128)(2,1)S(1)}) custom-call(s32[3]{0:T(128)S(1)} %pad_add_fusion.where_ref, bf16[4,46,32,128]{3,2,1,0:T(8,128)(2,1)S(1)} %get-tuple-element.58.v_ref, ...), custom_call_target="tpu_custom_call" | custom-call | tf_op jit(solution)/shard_map/pallas_call | solution.py:500
  37.1 0.0 collective-permute-start.5
  37.1 4.4 %collective-permute-start.6 = (bf16[15,40,128]{2,1,0:T(8,128)(2,1)S(1)}, bf16[15,40,128]{2,1,0:T(8,128)(2,1)S(1)}, u32[]{:S(2)}, u32[]{:S(2)}) collective-permute-start(bf16[15,40,128]{2,1,0:T(8,128)(2,1)S(1)} %get-tuple-element.75), channel_id=1, source_target_pairs={{16,32},{32,16},{48,64},{64,48},{80,96},{96,80},{112,128},{128,112... | collective-permute-start | bytes 460808 | tf_op jit(solution)/shard_map/ppermute | solution.py:589
  41.6 1.9 %collective-permute-done.5.re_ref = bf16[15,40,128]{2,1,0:T(8,128)(2,1)S(1)} collective-permute-done((bf16[15,40,128]{2,1,0:T(8,128)(2,1)S(1)}, bf16[15,40,128]{2,1,0:T(8,128)(2,1)S(1)}, u32[]{:S(2)}, u32[]{:S(2)}) %collective-permute-start.5) | collective-permute-done | bytes 153632 | tf_op jit(solution)/shard_map/ppermute | solution.py:590
  43.5 2.4 %collective-permute-done.6.ro_ref = bf16[15,40,128]{2,1,0:T(8,128)(2,1)S(1)} collective-permute-done((bf16[15,40,128]{2,1,0:T(8,128)(2,1)S(1)}, bf16[15,40,128]{2,1,0:T(8,128)(2,1)S(1)}, u32[]{:S(2)}, u32[]{:S(2)}) %collective-permute-start.6) | collective-permute-done | bytes 153632 | tf_op jit(solution)/shard_map/ppermute | solution.py:589
  45.8 2.3 %shard_map.92 = f32[4,32,128]{2,1,0:T(8,128)} custom-call(s32[3]{0:T(128)S(1)} %pad_add_fusion.where_ref, f32[4,4,40,128]{3,2,1,0:T(8,128)S(1)} %get-tuple-element.72.e_ref, f32[4,4,40,128]{3,2,1,0:T(8,128)S(1)} %get-tuple-element.73.ext_ref, bf16[15,40,128]{2,1,0:T(8,128)(2,1)S(1)} %collective-permute-done.5.re_ref, ...), custom_call_target="tpu_custom_call" | custom-call | tf_op jit(solution)/shard_map/pallas_call | solution.py:500
Async XLA Ops:
  3.1 5.9 %collective-permute-start = (bf16[288,128]{1,0:T(8,128)(2,1)S(1)}, bf16[288,128]{1,0:T(8,128)(2,1)S(1)}, u32[]{:S(2)}, u32[]{:S(2)}) collective-permute-start(bf16[288,128]{1,0:T(8,128)(2,1)S(1)} %get-tuple-element.41.zs_ref), channel_id=1, source_target_pairs={{0,1},{1,0},{2,3},{3,2},{4,5},{5,4},{6,7},{7,6},{8,9},{9,8},{10,11... | collective-permute-start | bytes 221192 | tf_op jit(solution)/shard_map/ppermute | solution.py:529
  9.7 1.6 %collective-permute-start.1 = (bf16[4,208,128]{2,1,0:T(8,128)(2,1)S(1)}, bf16[4,208,128]{2,1,0:T(8,128)(2,1)S(1)}, u32[]{:S(2)}, u32[]{:S(2)}) collective-permute-start(bf16[4,208,128]{2,1,0:T(8,128)(2,1)S(1)} %get-tuple-element.56), channel_id=1, source_target_pairs={{0,2},{2,0},{4,6},{6,4},{8,10},{10,8},{12,14},{14,12},{1,3},{3,1},... | collective-permute-start | bytes 638984 | tf_op jit(solution)/shard_map/ppermute | solution.py:562
  9.8 5.4 %collective-permute-start.2 = (bf16[4,208,128]{2,1,0:T(8,128)(2,1)S(1)}, bf16[4,208,128]{2,1,0:T(8,128)(2,1)S(1)}, u32[]{:S(2)}, u32[]{:S(2)}) collective-permute-start(bf16[4,208,128]{2,1,0:T(8,128)(2,1)S(1)} %get-tuple-element.57), channel_id=1, source_target_pairs={{2,4},{4,2},{6,8},{8,6},{10,12},{12,10},{14,0},{0,14},{3,5},{5,3},... | collective-permute-start | bytes 638984 | tf_op jit(solution)/shard_map/ppermute | solution.py:561
  15.9 11.3 %collective-permute-start.3 = (bf16[46,32,128]{2,1,0:T(8,128)(2,1)S(1)}, bf16[46,32,128]{2,1,0:T(8,128)(2,1)S(1)}, u32[]{:S(2)}, u32[]{:S(2)}) collective-permute-start(bf16[46,32,128]{2,1,0:T(8,128)(2,1)S(1)} %get-tuple-element.59), channel_id=1, source_target_pairs={{0,16},{16,0},{32,48},{48,32},{64,80},{80,64},{96,112},{112,96},{1... | collective-permute-start | bytes 1130504 | tf_op jit(solution)/shard_map/ppermute | solution.py:570
  17.9 15.0 %collective-permute-start.4 = (bf16[46,32,128]{2,1,0:T(8,128)(2,1)S(1)}, bf16[46,32,128]{2,1,0:T(8,128)(2,1)S(1)}, u32[]{:S(2)}, u32[]{:S(2)}) collective-permute-start(bf16[46,32,128]{2,1,0:T(8,128)(2,1)S(1)} %get-tuple-element.60), channel_id=1, source_target_pairs={{16,32},{32,16},{48,64},{64,48},{80,96},{96,80},{112,128},{128,112... | collective-permute-start | bytes 1130504 | tf_op jit(solution)/shard_map/ppermute | solution.py:569
  37.1 6.3 %collective-permute-start.5 = (bf16[15,40,128]{2,1,0:T(8,128)(2,1)S(1)}, bf16[15,40,128]{2,1,0:T(8,128)(2,1)S(1)}, u32[]{:S(2)}, u32[]{:S(2)}) collective-permute-start(bf16[15,40,128]{2,1,0:T(8,128)(2,1)S(1)} %get-tuple-element.74), channel_id=1, source_target_pairs={{0,16},{16,0},{32,48},{48,32},{64,80},{80,64},{96,112},{112,96},{1... | collective-permute-start | bytes 460808 | tf_op jit(solution)/shard_map/ppermute | solution.py:590
  37.1 8.7 %collective-permute-start.6 = (bf16[15,40,128]{2,1,0:T(8,128)(2,1)S(1)}, bf16[15,40,128]{2,1,0:T(8,128)(2,1)S(1)}, u32[]{:S(2)}, u32[]{:S(2)}) collective-permute-start(bf16[15,40,128]{2,1,0:T(8,128)(2,1)S(1)} %get-tuple-element.75), channel_id=1, source_target_pairs={{16,32},{32,16},{48,64},{64,48},{80,96},{96,80},{112,128},{128,112... | collective-permute-start | bytes 460808 | tf_op jit(solution)/shard_map/ppermute | solution.py:589

commit v3 on v2

--- a/solution.py
+++ b/solution.py
@@ -9,7 +9,6 @@
 F32 = jnp.float32
 BF16 = jnp.bfloat16
 VMEM = pl.BlockSpec(memory_space=pltpu.VMEM)
-SMEM = pl.BlockSpec(memory_space=pltpu.SMEM)
 HBM = pl.BlockSpec(memory_space=pltpu.HBM)
 PARAMS = pltpu.CompilerParams(vmem_limit_bytes=12 * 2**20)
 
@@ -31,8 +30,8 @@
     return lax.broadcasted_iota(jnp.int32, shape, dim)
 
 
-def pack_kernel(where_ref, x_hbm, m_hbm, s_hbm, v_ref, zs_ref, ms_ref, x_ref, m_ref, s_ref, sems):
-    gz = where_ref[2]
+def pack_kernel(x_hbm, m_hbm, s_hbm, v_ref, zs_ref, ms_ref, x_ref, m_ref, s_ref, sems):
+    gz = lax.axis_index("gz")
     copies = [pltpu.make_async_copy(x_hbm.at[:, x], x_ref.at[x], sems.at[x]) for x in range(4)]
     copies += [
         pltpu.make_async_copy(m_hbm, m_ref, sems.at[4]),
@@ -119,9 +118,9 @@
     return jnp.where(inside, value, 0.0)
 
 
-def yface_kernel(where_ref, v_ref, zs_ref, zr_ref, ms_ref, pt_ref, ye_ref, yo_ref, block_ref):
-    odd = where_ref[1] % 2
-    gz = where_ref[2]
+def yface_kernel(v_ref, zs_ref, zr_ref, ms_ref, pt_ref, ye_ref, yo_ref, block_ref):
+    odd = lax.axis_index("gy") % 2
+    gz = lax.axis_index("gz")
     lane = iota((256, 128), 1) % 8
     own = pltpu.roll(zs_ref[0:256].astype(F32), jnp.where(gz == 0, 122, 5), 1)
     other = pltpu.roll(zr_ref[0:256].astype(F32), jnp.where(gz == 0, 2, 125), 1)
@@ -157,11 +156,11 @@
         write(yo_ref, True)
 
 
-def xface_kernel(where_ref, v_in_ref, pt_ref, ye_ref, yo_ref, v_ref, xe_ref, xo_ref):
-    odd_x = where_ref[0] % 2
-    odd_y = where_ref[1] % 2
-
-    gy = where_ref[1]
+def xface_kernel(v_in_ref, pt_ref, ye_ref, yo_ref, v_ref, xe_ref, xo_ref):
+    odd_x = lax.axis_index("gx") % 2
+    odd_y = lax.axis_index("gy") % 2
+
+    gy = lax.axis_index("gy")
     for x in range(4):
         v_ref[x, 5:37] = v_in_ref[x, 5:37]
 
@@ -278,12 +277,12 @@
 
 
 def inner_kernel(
-    where_ref, v_ref, ye_ref, yo_ref, zr_ref, ms_ref, w_ref, wp_ref, b_ref, hw_ref, hb_ref, hwp_ref, hbp_ref,
+    v_ref, ye_ref, yo_ref, zr_ref, ms_ref, w_ref, wp_ref, b_ref, hw_ref, hb_ref, hwp_ref, hbp_ref,
     a_ref, e_ref, ext_ref, hid_ref, mask_ref, mext_ref,
 ):
-    gy = where_ref[1]
+    gy = lax.axis_index("gy")
     odd_y = gy % 2
-    gz = where_ref[2]
+    gz = lax.axis_index("gz")
     zmask = zr_ref[256:288].astype(F32)
     for x in range(4):
         for f in range(2):
@@ -343,12 +342,12 @@
 
 
 def border_kernel(
-    where_ref, v_ref, xe_ref, xo_ref, a_in, e_in, ext_in, w_ref, wp_ref, b_ref, hw_ref, hb_ref, hwp_ref, hbp_ref,
+    v_ref, xe_ref, xo_ref, a_in, e_in, ext_in, w_ref, wp_ref, b_ref, hw_ref, hb_ref, hwp_ref, hbp_ref,
     a_ref, e_ref, ext_ref, se_ref, so_ref, low_ref, high_ref, hid_ref,
 ):
-    gx = where_ref[0]
+    gx = lax.axis_index("gx")
     odd_x = gx % 2
-    gz = where_ref[2]
+    gz = lax.axis_index("gz")
 
     @pl.when(odd_x == 0)
     def _():
@@ -412,12 +411,12 @@
         send(so_ref, (3, 2, 1, 0))
 
 
-def rounds_kernel(where_ref, e_ref, ext_ref, re_ref, ro_ref, ms_ref, out_ref, all_ref, s_ref):
-    gx = where_ref[0]
+def rounds_kernel(e_ref, ext_ref, re_ref, ro_ref, ms_ref, out_ref, all_ref, s_ref):
+    gx = lax.axis_index("gx")
     odd_x = gx % 2
     has_low = jnp.where(gx == 0, 0.0, 1.0)
     has_high = jnp.where(gx == 15, 0.0, 1.0)
-    gz = where_ref[2]
+    gz = lax.axis_index("gz")
 
     def place(src_ref, places, keep_last):
         has = has_high if keep_last else has_low
@@ -500,7 +499,7 @@
     return pl.pallas_call(
         kernel,
         out_shape=[jax.ShapeDtypeStruct(s, d) for s, d in shapes],
-        in_specs=specs or [SMEM] + [VMEM] * (len(args) - 1),
+        in_specs=specs or [VMEM] * len(args),
         out_specs=[VMEM] * len(shapes),
         scratch_shapes=[pltpu.VMEM(*s) if isinstance(s[0], tuple) else s[0](*s[1:]) for s in scratch],
         input_output_aliases=aliases,
@@ -509,19 +508,17 @@
 
 
 def body(features, conv_weight, conv_bias, head_weight, head_bias, mask, seeds):
-    where = jnp.stack([lax.axis_index(a) for a in ("gx", "gy", "gz")]).astype(jnp.int32)
-
     v, zs, ms = call(
         pack_kernel,
         [((4, 46, 32, 128), BF16), ((288, 128), BF16), ((2, 4, 32, 128), F32)],
-        (where, *(stay(a) for a in (features, mask, seeds))),
+        tuple(stay(a) for a in (features, mask, seeds)),
         scratch=[
             ((4, 32, 32, 128), BF16),
             ((4, 32, 128), jnp.int32),
             ((4, 32, 128), jnp.int32),
             (pltpu.SemaphoreType.DMA, (6,)),
         ],
-        specs=[SMEM, HBM, HBM, HBM],
+        specs=[HBM] * 3,
     )
     zs, conv_weight, conv_bias, head_weight, head_bias = lax.optimization_barrier(
         (zs, conv_weight, conv_bias, head_weight, head_bias)
@@ -554,7 +551,7 @@
     pt, ye, yo = call(
         yface_kernel,
         [((4, 2, 32, 128), BF16), ((4, 208, 128), BF16), ((4, 208, 128), BF16)],
-        (where, v, zs, zr, ms),
+        (v, zs, zr, ms),
         scratch=[((2, 4, 16, 128), F32)],
     )
     even, odd = swaps("gy")
@@ -563,7 +560,7 @@
     v, xe, xo = call(
         xface_kernel,
         [((4, 46, 32, 128), BF16), ((46, 32, 128), BF16), ((46, 32, 128), BF16)],
-        (where, v, pt, ye, yo),
+        (v, pt, ye, yo),
     )
     even, odd = swaps("gx")
     xo = lax.ppermute(xo, "gx", odd)
@@ -571,7 +568,7 @@
     affinity, e, ext = call(
         inner_kernel,
         [((3, 4, 32, 128), BF16), ((4, 4, 40, 128), F32), ((4, 4, 40, 128), F32)],
-        (where, v, ye, yo, zr, ms) + weights,
+        (v, ye, yo, zr, ms) + weights,
         scratch=[((2, 1280, 128), BF16), ((2, 4, 40, 128), F32), ((2, 4, 40, 128), F32)],
     )
     affinity, e, ext, se, so = call(
@@ -583,7 +580,7 @@
             ((15, 40, 128), BF16),
             ((15, 40, 128), BF16),
         ],
-        (where, v, xe, xo, affinity, e, ext) + weights,
+        (v, xe, xo, affinity, e, ext) + weights,
         scratch=[((46, 32, 128), BF16), ((46, 32, 128), BF16), ((2, 1280, 128), BF16)],
     )
     so = lax.ppermute(so, "gx", odd)
@@ -591,7 +588,7 @@
     (strength,) = call(
         rounds_kernel,
         [((4, 32, 128), F32)],
-        (where, e, ext, se, so, ms),
+        (e, ext, se, so, ms),
         scratch=[((12, 3, 2, 40, 128), F32), ((2, 12, 2, 40, 128), F32)],
     )
     return (affinity, strength)

time: 48.2 us -> 45.4 us (0.942)
  Pallas kernels: 14.8 us -> 11.6 us
  waiting for transfers between devices: 15.8 us -> 16.3 us
    pallas_call x7, Pallas kernels: 14.8 us -> 11.6 us  [call(): pl.pallas_call(kernel, out_shape=[jax.ShapeDtypeStruct(s, d) for s, d in...]
  transfers between devices with their start and end apart: 7 -> 7, of which waited for: 6 -> 7; matrix products, arithmetic and copies ran while one was open for 0% -> 0% of each run, Pallas kernels for 9% -> 9%
where the time goes in v3:
time: 45.4 us; the launch traced here: 45.3 us
  starting transfers between devices  16.7 us (37%)
  waiting for transfers between devices  16.3 us (36%)
  Pallas kernels  11.6 us (26%)
  between operations  0.68 us (1%)
    pallas_call x7, Pallas kernels, call(): pl.pallas_call(kernel, out_shape=[jax.ShapeDtypeStruct(s, d) for s, d in...  11.6 us
    ppermute x1, waiting for transfers between devices, body(): xo = lax.ppermute(xo, 'gx', odd)  6.05 us
    ppermute x1, starting transfers between devices, body(): xo = lax.ppermute(xo, 'gx', odd)  5.97 us
    ppermute x1, starting transfers between devices, body(): so = lax.ppermute(so, 'gx', odd)  4.44 us
    ppermute x1, waiting for transfers between devices, body(): yo = lax.ppermute(yo, 'gy', odd)  3.91 us
    ppermute x1, starting transfers between devices, body(): zr = lax.ppermute(zs, 'gz', [(0, 1), (1, 0)])  3.28 us
    ppermute x1, waiting for transfers between devices, body(): so = lax.ppermute(so, 'gx', odd)  2.39 us
    ppermute x1, starting transfers between devices, body(): xe = lax.ppermute(xe, 'gx', even)  2 us
  transfers between devices with their start and end apart: 7, of which 7 were waited for; matrix products, arithmetic and copies ran while one was open for 0% of the time, Pallas kernels for 9%

profile of v3, /device:TPU:6, one launch (start us, length us, event | category | flops | bytes accessed | tf_op | source)
XLA Modules:
  0.0 45.3 jit_solution(94894822306683604)
XLA Ops:
  0.6 1.8 %shard_map.86 = (bf16[4,46,32,128]{3,2,1,0:T(8,128)(2,1)S(1)}, bf16[288,128]{1,0:T(8,128)(2,1)S(1)}, f32[2,4,32,128]{3,2,1,0:T(8,128)S(1)}) custom-call(bf16[32,4,32,128]{3,2,1,0:T(8,128)(2,1)} %x_hbm.1, s32[4,32,128]{2,1,0:T(8,128)} %m_hbm.1, s32[4,32,128]{2,1,0:T(8,128)} %s_hbm.1), custom_call_target="tpu_custom_call" | custom-call | tf_op jit(solution)/shard_map/pallas_call | solution.py:499
  2.5 3.3 %collective-permute-start = (bf16[288,128]{1,0:T(8,128)(2,1)S(1)}, bf16[288,128]{1,0:T(8,128)(2,1)S(1)}, u32[]{:S(2)}, u32[]{:S(2)}) collective-permute-start(bf16[288,128]{1,0:T(8,128)(2,1)S(1)} %get-tuple-element.41.zs_ref), channel_id=1, source_target_pairs={{0,1},{1,0},{2,3},{3,2},{4,5},{5,4},{6,7},{7,6},{8,9},{9,8},{10,11... | collective-permute-start | bytes 221192 | tf_op jit(solution)/shard_map/ppermute | solution.py:526
  5.7 1.2 %shard_map.87 = (bf16[96,288]{1,0:T(8,128)(2,1)S(1)}, bf16[288,96]{1,0:T(8,128)(2,1)S(1)}, f32[32,128]{1,0:T(8,128)S(1)}, f32[24,256]{1,0:T(8,128)S(1)}, f32[24,...) custom-call(bf16[27,32,32]{2,1,0:T(8,128)(2,1)} %bitcast.4, f32[1,32]{1,0:T(1,128)} %bitcast.5, ...), custom_call_target="tpu_custom_call" | custom-call | tf_op jit(solution)/shard_map/pallas_call | solution.py:499
  6.9 1.5 %collective-permute-done.zr_ref = bf16[288,128]{1,0:T(8,128)(2,1)S(1)} collective-permute-done((bf16[288,128]{1,0:T(8,128)(2,1)S(1)}, bf16[288,128]{1,0:T(8,128)(2,1)S(1)}, u32[]{:S(2)}, u32[]{:S(2)}) %collective-permute-start) | collective-permute-done | bytes 73760 | tf_op jit(solution)/shard_map/ppermute | solution.py:526
  8.4 0.1 shard_map.88
  8.6 0.1 collective-permute-start.1
  8.7 0.9 %collective-permute-start.2 = (bf16[4,208,128]{2,1,0:T(8,128)(2,1)S(1)}, bf16[4,208,128]{2,1,0:T(8,128)(2,1)S(1)}, u32[]{:S(2)}, u32[]{:S(2)}) collective-permute-start(bf16[4,208,128]{2,1,0:T(8,128)(2,1)S(1)} %get-tuple-element.57), channel_id=1, source_target_pairs={{2,4},{4,2},{6,8},{8,6},{10,12},{12,10},{14,0},{0,14},{3,5},{5,3},... | collective-permute-start | bytes 638984 | tf_op jit(solution)/shard_map/ppermute | solution.py:558
  9.6 0.5 %collective-permute-done.1.ye_ref = bf16[4,208,128]{2,1,0:T(8,128)(2,1)S(1)} collective-permute-done((bf16[4,208,128]{2,1,0:T(8,128)(2,1)S(1)}, bf16[4,208,128]{2,1,0:T(8,128)(2,1)S(1)}, u32[]{:S(2)}, u32[]{:S(2)}) %collective-permute-start.1) | collective-permute-done | bytes 213024 | tf_op jit(solution)/shard_map/ppermute | solution.py:559
  10.1 3.9 %collective-permute-done.2.yo_ref = bf16[4,208,128]{2,1,0:T(8,128)(2,1)S(1)} collective-permute-done((bf16[4,208,128]{2,1,0:T(8,128)(2,1)S(1)}, bf16[4,208,128]{2,1,0:T(8,128)(2,1)S(1)}, u32[]{:S(2)}, u32[]{:S(2)}) %collective-permute-start.2) | collective-permute-done | bytes 213024 | tf_op jit(solution)/shard_map/ppermute | solution.py:558
  14.0 0.2 shard_map.89
  14.2 2.0 %collective-permute-start.3 = (bf16[46,32,128]{2,1,0:T(8,128)(2,1)S(1)}, bf16[46,32,128]{2,1,0:T(8,128)(2,1)S(1)}, u32[]{:S(2)}, u32[]{:S(2)}) collective-permute-start(bf16[46,32,128]{2,1,0:T(8,128)(2,1)S(1)} %get-tuple-element.59), channel_id=1, source_target_pairs={{0,16},{16,0},{32,48},{48,32},{64,80},{80,64},{96,112},{112,96},{1... | collective-permute-start | bytes 1130504 | tf_op jit(solution)/shard_map/ppermute | solution.py:567
  16.2 6.0 %collective-permute-start.4 = (bf16[46,32,128]{2,1,0:T(8,128)(2,1)S(1)}, bf16[46,32,128]{2,1,0:T(8,128)(2,1)S(1)}, u32[]{:S(2)}, u32[]{:S(2)}) collective-permute-start(bf16[46,32,128]{2,1,0:T(8,128)(2,1)S(1)} %get-tuple-element.60), channel_id=1, source_target_pairs={{16,32},{32,16},{48,64},{64,48},{80,96},{96,80},{112,128},{128,112... | collective-permute-start | bytes 1130504 | tf_op jit(solution)/shard_map/ppermute | solution.py:566
  22.2 2.8 %shard_map.90 = (bf16[3,4,32,128]{3,2,1,0:T(8,128)(2,1)S(1)}, f32[4,4,40,128]{3,2,1,0:T(8,128)S(1)}, f32[4,4,40,128]{3,2,1,0:T(8,128)S(1)}) custom-call(bf16[4,46,32,128]{3,2,1,0:T(8,128)(2,1)S(1)} %get-tuple-element.58.v_ref, bf16[4,208,128]{2,1,0:T(8,128)(2,1)S(1)} %collective-permute-done.1.ye_ref, ...), custom_call_target="tpu_custom_call" | custom-call | tf_op jit(solution)/shard_map/pallas_call | solution.py:499
  25.0 0.1 collective-permute-done.3.xe_ref
  25.1 6.0 %collective-permute-done.4.xo_ref = bf16[46,32,128]{2,1,0:T(8,128)(2,1)S(1)} collective-permute-done((bf16[46,32,128]{2,1,0:T(8,128)(2,1)S(1)}, bf16[46,32,128]{2,1,0:T(8,128)(2,1)S(1)}, u32[]{:S(2)}, u32[]{:S(2)}) %collective-permute-start.4) | collective-permute-done | bytes 376864 | tf_op jit(solution)/shard_map/ppermute | solution.py:566
  31.2 3.7 %shard_map.91 = (bf16[3,4,32,128]{3,2,1,0:T(8,128)(2,1)}, f32[4,4,40,128]{3,2,1,0:T(8,128)S(1)}, f32[4,4,40,128]{3,2,1,0:T(8,128)S(1)}, bf16[15,40,128]{2,1,0:T(8,128)(2,1)S(1)}, bf16[15,40,128]{2,1,0:T(8,128)(2,1)S(1)}) custom-call(bf16[4,46,32,128]{3,2,1,0:T(8,128)(2,1)S(1)} %get-tuple-element.58.v_ref, ...), custom_call_target="tpu_custom_call" | custom-call | tf_op jit(solution)/shard_map/pallas_call | solution.py:499
  34.9 0.0 collective-permute-start.5
  34.9 4.4 %collective-permute-start.6 = (bf16[15,40,128]{2,1,0:T(8,128)(2,1)S(1)}, bf16[15,40,128]{2,1,0:T(8,128)(2,1)S(1)}, u32[]{:S(2)}, u32[]{:S(2)}) collective-permute-start(bf16[15,40,128]{2,1,0:T(8,128)(2,1)S(1)} %get-tuple-element.75), channel_id=1, source_target_pairs={{16,32},{32,16},{48,64},{64,48},{80,96},{96,80},{112,128},{128,112... | collective-permute-start | bytes 460808 | tf_op jit(solution)/shard_map/ppermute | solution.py:586
  39.3 1.9 %collective-permute-done.5.re_ref = bf16[15,40,128]{2,1,0:T(8,128)(2,1)S(1)} collective-permute-done((bf16[15,40,128]{2,1,0:T(8,128)(2,1)S(1)}, bf16[15,40,128]{2,1,0:T(8,128)(2,1)S(1)}, u32[]{:S(2)}, u32[]{:S(2)}) %collective-permute-start.5) | collective-permute-done | bytes 153632 | tf_op jit(solution)/shard_map/ppermute | solution.py:587
  41.2 2.4 %collective-permute-done.6.ro_ref = bf16[15,40,128]{2,1,0:T(8,128)(2,1)S(1)} collective-permute-done((bf16[15,40,128]{2,1,0:T(8,128)(2,1)S(1)}, bf16[15,40,128]{2,1,0:T(8,128)(2,1)S(1)}, u32[]{:S(2)}, u32[]{:S(2)}) %collective-permute-start.6) | collective-permute-done | bytes 153632 | tf_op jit(solution)/shard_map/ppermute | solution.py:586
  43.6 1.7 %shard_map.92 = f32[4,32,128]{2,1,0:T(8,128)} custom-call(f32[4,4,40,128]{3,2,1,0:T(8,128)S(1)} %get-tuple-element.72.e_ref, f32[4,4,40,128]{3,2,1,0:T(8,128)S(1)} %get-tuple-element.73.ext_ref, bf16[15,40,128]{2,1,0:T(8,128)(2,1)S(1)} %collective-permute-done.5.re_ref, bf16[15,40,128]{2,1,0:T(8,128)(2,1)S(1)} %collective-permute-done.6.ro_ref, ...), custom_call_target="tpu_custom_call" | custom-call | tf_op jit(solution)/shard_map/pallas_call | solution.py:499
Async XLA Ops:
  2.5 5.9 %collective-permute-start = (bf16[288,128]{1,0:T(8,128)(2,1)S(1)}, bf16[288,128]{1,0:T(8,128)(2,1)S(1)}, u32[]{:S(2)}, u32[]{:S(2)}) collective-permute-start(bf16[288,128]{1,0:T(8,128)(2,1)S(1)} %get-tuple-element.41.zs_ref), channel_id=1, source_target_pairs={{0,1},{1,0},{2,3},{3,2},{4,5},{5,4},{6,7},{7,6},{8,9},{9,8},{10,11... | collective-permute-start | bytes 221192 | tf_op jit(solution)/shard_map/ppermute | solution.py:526
  8.6 1.6 %collective-permute-start.1 = (bf16[4,208,128]{2,1,0:T(8,128)(2,1)S(1)}, bf16[4,208,128]{2,1,0:T(8,128)(2,1)S(1)}, u32[]{:S(2)}, u32[]{:S(2)}) collective-permute-start(bf16[4,208,128]{2,1,0:T(8,128)(2,1)S(1)} %get-tuple-element.56), channel_id=1, source_target_pairs={{0,2},{2,0},{4,6},{6,4},{8,10},{10,8},{12,14},{14,12},{1,3},{3,1},... | collective-permute-start | bytes 638984 | tf_op jit(solution)/shard_map/ppermute | solution.py:559
  8.7 5.4 %collective-permute-start.2 = (bf16[4,208,128]{2,1,0:T(8,128)(2,1)S(1)}, bf16[4,208,128]{2,1,0:T(8,128)(2,1)S(1)}, u32[]{:S(2)}, u32[]{:S(2)}) collective-permute-start(bf16[4,208,128]{2,1,0:T(8,128)(2,1)S(1)} %get-tuple-element.57), channel_id=1, source_target_pairs={{2,4},{4,2},{6,8},{8,6},{10,12},{12,10},{14,0},{0,14},{3,5},{5,3},... | collective-permute-start | bytes 638984 | tf_op jit(solution)/shard_map/ppermute | solution.py:558
  14.2 10.9 %collective-permute-start.3 = (bf16[46,32,128]{2,1,0:T(8,128)(2,1)S(1)}, bf16[46,32,128]{2,1,0:T(8,128)(2,1)S(1)}, u32[]{:S(2)}, u32[]{:S(2)}) collective-permute-start(bf16[46,32,128]{2,1,0:T(8,128)(2,1)S(1)} %get-tuple-element.59), channel_id=1, source_target_pairs={{0,16},{16,0},{32,48},{48,32},{64,80},{80,64},{96,112},{112,96},{1... | collective-permute-start | bytes 1130504 | tf_op jit(solution)/shard_map/ppermute | solution.py:567
  16.2 15.0 %collective-permute-start.4 = (bf16[46,32,128]{2,1,0:T(8,128)(2,1)S(1)}, bf16[46,32,128]{2,1,0:T(8,128)(2,1)S(1)}, u32[]{:S(2)}, u32[]{:S(2)}) collective-permute-start(bf16[46,32,128]{2,1,0:T(8,128)(2,1)S(1)} %get-tuple-element.60), channel_id=1, source_target_pairs={{16,32},{32,16},{48,64},{64,48},{80,96},{96,80},{112,128},{128,112... | collective-permute-start | bytes 1130504 | tf_op jit(solution)/shard_map/ppermute | solution.py:566
  34.9 6.3 %collective-permute-start.5 = (bf16[15,40,128]{2,1,0:T(8,128)(2,1)S(1)}, bf16[15,40,128]{2,1,0:T(8,128)(2,1)S(1)}, u32[]{:S(2)}, u32[]{:S(2)}) collective-permute-start(bf16[15,40,128]{2,1,0:T(8,128)(2,1)S(1)} %get-tuple-element.74), channel_id=1, source_target_pairs={{0,16},{16,0},{32,48},{48,32},{64,80},{80,64},{96,112},{112,96},{1... | collective-permute-start | bytes 460808 | tf_op jit(solution)/shard_map/ppermute | solution.py:587
  34.9 8.7 %collective-permute-start.6 = (bf16[15,40,128]{2,1,0:T(8,128)(2,1)S(1)}, bf16[15,40,128]{2,1,0:T(8,128)(2,1)S(1)}, u32[]{:S(2)}, u32[]{:S(2)}) collective-permute-start(bf16[15,40,128]{2,1,0:T(8,128)(2,1)S(1)} %get-tuple-element.75), channel_id=1, source_target_pairs={{16,32},{32,16},{48,64},{64,48},{80,96},{96,80},{112,128},{128,112... | collective-permute-start | bytes 460808 | tf_op jit(solution)/shard_map/ppermute | solution.py:586

commit v4 on v3

--- a/solution.py
+++ b/solution.py
@@ -30,7 +30,7 @@
     return lax.broadcasted_iota(jnp.int32, shape, dim)
 
 
-def pack_kernel(x_hbm, m_hbm, s_hbm, v_ref, zs_ref, ms_ref, x_ref, m_ref, s_ref, sems):
+def pack_kernel(x_hbm, m_hbm, s_hbm, v_ref, zs_ref, ms_ref, xe_ref, xo_ref, x_ref, m_ref, s_ref, sems):
     gz = lax.axis_index("gz")
     copies = [pltpu.make_async_copy(x_hbm.at[:, x], x_ref.at[x], sems.at[x]) for x in range(4)]
     copies += [
@@ -47,6 +47,9 @@
     for x in range(4):
         copies[x].wait()
         v_ref[x, 5:37] = jnp.swapaxes(x_ref[x], 0, 1)
+    even_face = jnp.where(lax.axis_index("gx") % 2 == 0, 3, 0)
+    xe_ref[...] = v_ref[even_face, 5:37]
+    xo_ref[...] = v_ref[3 - even_face, 5:37]
     acc = jnp.zeros((256, 128), F32)
     for y in range(16):
         lhs = jnp.concatenate(
@@ -197,8 +200,9 @@
                 v_ref[x, tile] = zero
 
     even_face = jnp.where(odd_x == 0, 3, 0)
-    xe_ref[...] = v_ref[even_face]
-    xo_ref[...] = v_ref[3 - even_face]
+    for dst_ref, face in ((xe_ref, even_face), (xo_ref, 3 - even_face)):
+        dst_ref[0:5] = v_ref[face, 0:5]
+        dst_ref[5:14] = v_ref[face, 37:46]
 
 
 def head(hidden, head_ref, bias_ref):
@@ -216,6 +220,10 @@
     to = iota((512, 128), 1)
     goal = jnp.where(gz == 0, (k + 126) % 128, (k + 123) % 128)
     return jnp.where((k >= 1) & (k <= 5) & (to == goal), 1.0, 0.0).astype(BF16)
+
+
+INTERIOR = tuple(range(1, 31))
+OTHERS = (31, 32, 33, 34, 35, 36, 37, 38, 39, 0)
 
 
 def conv_main(refs, weights, hid_ref, rows):
@@ -260,11 +268,17 @@
     return jnp.dot(lhs, spread, preferred_element_type=F32)
 
 
-def conv_slice(gz, refs, weights, spread, hid_ref):
-    conv_main(refs, weights, hid_ref, range(40))
+def conv_slice(gz, refs, weights, spread, interior_ref, hid_ref):
+    conv_main(refs, weights, hid_ref, OTHERS)
     border = conv_packed(refs, weights, spread)
-    hidden = jnp.concatenate([hid_ref[256 * g : 256 * g + 256] for g in range(5)], axis=1)
-    value = head(hidden, weights[3], weights[4])
+
+    def hidden(row):
+        return (interior_ref if row in INTERIOR else hid_ref)[32 * row : 32 * row + 32]
+
+    hid = jnp.concatenate(
+        [jnp.concatenate([hidden(8 * g + i) for i in range(8)], axis=0) for g in range(5)], axis=1
+    )
+    value = head(hid, weights[3], weights[4])
     fixed = iota((40, 128), 1) == jnp.where(gz == 0, 127, 0)
     out = []
     for c in range(3):
@@ -276,8 +290,52 @@
     return out
 
 
+def inner_rows_kernel(v_ref, w_ref, b_ref, hid_ref):
+    for x in (1, 2):
+        refs = [v_ref.at[x - 1 + d] for d in range(3)]
+        conv_main(refs, (w_ref, None, b_ref), hid_ref.at[x - 1], INTERIOR)
+
+
+def by_side(even_ref, odd_ref, fill):
+    gx = lax.axis_index("gx")
+
+    @pl.when(gx % 2 == 0)
+    def _():
+        fill(odd_ref, even_ref)
+
+    @pl.when(gx % 2 == 1)
+    def _():
+        fill(even_ref, odd_ref)
+
+
+def border_rows_kernel(v_ref, xe_ref, xo_ref, w_ref, b_ref, hid_ref, face_ref):
+    gx = lax.axis_index("gx")
+
+    def fill(low_ref, high_ref):
+        face_ref[0, 5:37] = low_ref[...]
+        face_ref[1, 5:37] = high_ref[...]
+
+    by_side(xe_ref, xo_ref, fill)
+
+    @pl.when(gx == 0)
+    def _():
+        face_ref[0, 5:37] = jnp.zeros((32, 32, 128), BF16)
+
+    @pl.when(gx == 15)
+    def _():
+        face_ref[1, 5:37] = jnp.zeros((32, 32, 128), BF16)
+
+    for i, refs in enumerate(
+        (
+            [face_ref.at[0], v_ref.at[0], v_ref.at[1]],
+            [v_ref.at[2], v_ref.at[3], face_ref.at[1]],
+        )
+    ):
+        conv_main(refs, (w_ref, None, b_ref), hid_ref.at[i], INTERIOR)
+
+
 def inner_kernel(
-    v_ref, ye_ref, yo_ref, zr_ref, ms_ref, w_ref, wp_ref, b_ref, hw_ref, hb_ref, hwp_ref, hbp_ref,
+    v_ref, rows_ref, ye_ref, yo_ref, zr_ref, ms_ref, w_ref, wp_ref, b_ref, hw_ref, hb_ref, hwp_ref, hbp_ref,
     a_ref, e_ref, ext_ref, hid_ref, mask_ref, mext_ref,
 ):
     gy = lax.axis_index("gy")
@@ -328,7 +386,7 @@
         keep = ((x_main, x_ext), (y_main, y_ext), (z_main, z_ext))
         if 0 < x < 3:
             refs = [v_ref.at[x - 1 + d] for d in range(3)]
-            a = conv_slice(gz, refs, weights, spread, hid_ref.at[x - 1])
+            a = conv_slice(gz, refs, weights, spread, rows_ref.at[x - 1], hid_ref.at[x - 1])
             for f in range(3):
                 a_ref[f, x] = a[f][0][0:32].astype(BF16)
                 e_ref[x, f] = a[f][0] * keep[f][0]
@@ -342,30 +400,27 @@
 
 
 def border_kernel(
-    v_ref, xe_ref, xo_ref, a_in, e_in, ext_in, w_ref, wp_ref, b_ref, hw_ref, hb_ref, hwp_ref, hbp_ref,
-    a_ref, e_ref, ext_ref, se_ref, so_ref, low_ref, high_ref, hid_ref,
+    v_ref, face_ref, rows_ref, xe_ref, xo_ref, a_in, e_in, ext_in, w_ref, wp_ref, b_ref, hw_ref, hb_ref, hwp_ref, hbp_ref,
+    a_ref, e_ref, ext_ref, se_ref, so_ref, side_ref, hid_ref,
 ):
     gx = lax.axis_index("gx")
     odd_x = gx % 2
     gz = lax.axis_index("gz")
 
-    @pl.when(odd_x == 0)
-    def _():
-        low_ref[...] = xo_ref[...]
-        high_ref[...] = xe_ref[...]
-
-    @pl.when(odd_x == 1)
-    def _():
-        low_ref[...] = xe_ref[...]
-        high_ref[...] = xo_ref[...]
-
-    @pl.when(gx == 0)
-    def _():
-        low_ref[...] = jnp.zeros_like(low_ref)
-
-    @pl.when(gx == 15)
-    def _():
-        high_ref[...] = jnp.zeros_like(high_ref)
+    def fill(low_ref, high_ref):
+        for i, ref in enumerate((low_ref, high_ref)):
+            side_ref[i, 0:5] = ref[0:5]
+            side_ref[i, 37:46] = ref[5:14]
+
+    by_side(xe_ref, xo_ref, fill)
+    for i, end in ((0, 0), (1, 15)):
+        for at in (5, 6, 35, 36):
+            side_ref[i, at] = face_ref[i, at]
+
+        @pl.when(gx == end)
+        def _():
+            side_ref[i, 0:5] = jnp.zeros((5, 32, 128), BF16)
+            side_ref[i, 37:46] = jnp.zeros((9, 32, 128), BF16)
 
     for x in (1, 2):
         a_ref[:, x] = a_in[:, x]
@@ -378,10 +433,10 @@
     weights = (w_ref, wp_ref, b_ref, hw_ref, hb_ref, hwp_ref, hbp_ref)
     spread = spread_matrix(gz)
     for x, refs in (
-        (0, [low_ref, v_ref.at[0], v_ref.at[1]]),
-        (3, [v_ref.at[2], v_ref.at[3], high_ref]),
+        (0, [side_ref.at[0], v_ref.at[0], v_ref.at[1]]),
+        (3, [v_ref.at[2], v_ref.at[3], side_ref.at[1]]),
     ):
-        a = conv_slice(gz, refs, weights, spread, hid_ref.at[x // 3])
+        a = conv_slice(gz, refs, weights, spread, rows_ref.at[x // 3], hid_ref.at[x // 3])
         for f in range(3):
             a_ref[f, x] = a[f][0][0:32].astype(BF16)
             e_ref[x, f] = a[f][0] * e_in[x, f]
@@ -390,12 +445,11 @@
     def send(dst_ref, order):
         packed = jnp.zeros((40, 128), F32)
         for j, x in enumerate(order):
-            for f in range(4):
+            for f in range(4 if j < 3 else 0):
                 value = ext_ref[x, f]
                 slot = 4 * j + f
                 packed = packed + (pltpu.roll(value, 8 * slot, 1) if slot else value)
-                if j < 3:
-                    dst_ref[slot] = e_ref[x, f].astype(BF16)
+                dst_ref[slot] = e_ref[x, f].astype(BF16)
         dst_ref[12] = e_ref[order[3], 3].astype(BF16)
         dst_ref[13] = e_ref[order[3], 0].astype(BF16)
         dst_ref[14] = packed.astype(BF16)
@@ -411,7 +465,9 @@
         send(so_ref, (3, 2, 1, 0))
 
 
-def rounds_kernel(e_ref, ext_ref, re_ref, ro_ref, ms_ref, out_ref, all_ref, s_ref):
+def rounds_kernel(a_ref, e_ref, ext_ref, re_ref, ro_ref, ms_ref, a_hbm, out_hbm, all_ref, s_ref, out_ref, sems):
+    affinity_copy = pltpu.make_async_copy(a_ref, a_hbm, sems.at[4])
+    affinity_copy.start()
     gx = lax.axis_index("gx")
     odd_x = gx % 2
     has_low = jnp.where(gx == 0, 0.0, 1.0)
@@ -424,7 +480,7 @@
         for j, at in enumerate(places):
             for f in range(4):
                 scale = (lambda v: v / 15.0) if f == 3 else (lambda v: v)
-                ext = scale(unpack_ext(packed, 4 * j + f, gz))
+                ext = scale(unpack_ext(packed, 4 * j + f, gz)) if j < 3 else jnp.zeros_like(packed)
                 if j < 3:
                     main = scale(src_ref[4 * j + f].astype(F32) * has)
                 elif f == 3:
@@ -432,7 +488,7 @@
                 elif f == 0 and keep_last:
                     main = src_ref[13].astype(F32) * has
                 else:
-                    main, ext = jnp.zeros_like(packed), jnp.zeros_like(packed)
+                    main = jnp.zeros_like(packed)
                 if f == 3:
                     s_ref[0, at, 0] = main
                     s_ref[0, at, 1] = ext
@@ -487,30 +543,40 @@
                 value = jnp.maximum(value, z_high[i])
                 s_ref[dst, x, i] = value
 
+    copies = [affinity_copy]
     for x in range(4):
         out_ref[x] = s_ref[ROUNDS % 2, 4 + x, 0, 0:32] * ms_ref[0, x]
+        copies.append(pltpu.make_async_copy(out_ref.at[x], out_hbm.at[x], sems.at[x]))
+        copies[-1].start()
+    for copy in copies:
+        copy.wait()
 
 
 def stay(value):
     return pltpu.with_memory_space_constraint(value, pltpu.HBM)
 
 
-def call(kernel, shapes, args, scratch=(), aliases={}, specs=None):
+def call(kernel, shapes, args, scratch=(), specs=None, out_specs=None):
     return pl.pallas_call(
         kernel,
         out_shape=[jax.ShapeDtypeStruct(s, d) for s, d in shapes],
         in_specs=specs or [VMEM] * len(args),
-        out_specs=[VMEM] * len(shapes),
+        out_specs=out_specs or [VMEM] * len(shapes),
         scratch_shapes=[pltpu.VMEM(*s) if isinstance(s[0], tuple) else s[0](*s[1:]) for s in scratch],
-        input_output_aliases=aliases,
         compiler_params=PARAMS,
     )(*args)
 
 
 def body(features, conv_weight, conv_bias, head_weight, head_bias, mask, seeds):
-    v, zs, ms = call(
+    v, zs, ms, fe, fo = call(
         pack_kernel,
-        [((4, 46, 32, 128), BF16), ((288, 128), BF16), ((2, 4, 32, 128), F32)],
+        [
+            ((4, 46, 32, 128), BF16),
+            ((288, 128), BF16),
+            ((2, 4, 32, 128), F32),
+            ((32, 32, 128), BF16),
+            ((32, 32, 128), BF16),
+        ],
         tuple(stay(a) for a in (features, mask, seeds)),
         scratch=[
             ((4, 32, 32, 128), BF16),
@@ -520,10 +586,19 @@
         ],
         specs=[HBM] * 3,
     )
-    zs, conv_weight, conv_bias, head_weight, head_bias = lax.optimization_barrier(
-        (zs, conv_weight, conv_bias, head_weight, head_bias)
-    )
     zr = lax.ppermute(zs, "gz", [(0, 1), (1, 0)])
+    even_x, odd_x = swaps("gx")
+    fo = lax.ppermute(fo, "gx", odd_x)
+    fe = lax.ppermute(fe, "gx", even_x)
+    pt, ye, yo = call(
+        yface_kernel,
+        [((4, 2, 32, 128), BF16), ((4, 208, 128), BF16), ((4, 208, 128), BF16)],
+        (v, zs, zr, ms),
+        scratch=[((2, 4, 16, 128), F32)],
+    )
+    ye, yo, vy, conv_weight, conv_bias, head_weight, head_bias = lax.optimization_barrier(
+        (ye, yo, v, conv_weight, conv_bias, head_weight, head_bias)
+    )
     taps = jnp.transpose(conv_weight, (2, 3, 4, 0, 1)).reshape(27, 32, 32)
     forms = call(
         weights_kernel,
@@ -546,30 +621,34 @@
         ],
         specs=[HBM] * 4,
     )
-    zr, *weights = lax.optimization_barrier((zr, *forms))
-    weights = tuple(weights)
-    pt, ye, yo = call(
-        yface_kernel,
-        [((4, 2, 32, 128), BF16), ((4, 208, 128), BF16), ((4, 208, 128), BF16)],
-        (v, zs, zr, ms),
-        scratch=[((2, 4, 16, 128), F32)],
-    )
+    weights = tuple(forms)
+    rows_shape = [((2, 1280, 128), BF16)]
+    (inner_rows,) = call(inner_rows_kernel, rows_shape, (vy, weights[0], weights[2]))
     even, odd = swaps("gy")
     yo = lax.ppermute(yo, "gy", odd)
     ye = lax.ppermute(ye, "gy", even)
+    ye, yo, inner_rows = lax.optimization_barrier((ye, yo, inner_rows))
     v, xe, xo = call(
         xface_kernel,
-        [((4, 46, 32, 128), BF16), ((46, 32, 128), BF16), ((46, 32, 128), BF16)],
+        [((4, 46, 32, 128), BF16), ((14, 32, 128), BF16), ((14, 32, 128), BF16)],
         (v, pt, ye, yo),
     )
-    even, odd = swaps("gx")
-    xo = lax.ppermute(xo, "gx", odd)
-    xe = lax.ppermute(xe, "gx", even)
+    xe, xo, v, fe, fo = lax.optimization_barrier((xe, xo, v, fe, fo))
+    xo = lax.ppermute(xo, "gx", odd_x)
+    xe = lax.ppermute(xe, "gx", even_x)
     affinity, e, ext = call(
         inner_kernel,
         [((3, 4, 32, 128), BF16), ((4, 4, 40, 128), F32), ((4, 4, 40, 128), F32)],
-        (v, ye, yo, zr, ms) + weights,
+        (v, inner_rows, ye, yo, zr, ms) + weights,
         scratch=[((2, 1280, 128), BF16), ((2, 4, 40, 128), F32), ((2, 4, 40, 128), F32)],
+    )
+    border_rows, faces = call(
+        border_rows_kernel,
+        rows_shape + [((2, 46, 32, 128), BF16)],
+        (v, fe, fo, weights[0], weights[2]),
+    )
+    xe, xo, affinity, e, ext, border_rows, faces = lax.optimization_barrier(
+        (xe, xo, affinity, e, ext, border_rows, faces)
     )
     affinity, e, ext, se, so = call(
         border_kernel,
@@ -580,16 +659,22 @@
             ((15, 40, 128), BF16),
             ((15, 40, 128), BF16),
         ],
-        (v, xe, xo, affinity, e, ext) + weights,
-        scratch=[((46, 32, 128), BF16), ((46, 32, 128), BF16), ((2, 1280, 128), BF16)],
-    )
-    so = lax.ppermute(so, "gx", odd)
-    se = lax.ppermute(se, "gx", even)
-    (strength,) = call(
+        (v, faces, border_rows, xe, xo, affinity, e, ext) + weights,
+        scratch=[((2, 46, 32, 128), BF16), ((2, 1280, 128), BF16)],
+    )
+    so = lax.ppermute(so, "gx", odd_x)
+    se = lax.ppermute(se, "gx", even_x)
+    affinity, strength = call(
         rounds_kernel,
-        [((4, 32, 128), F32)],
-        (e, ext, se, so, ms),
-        scratch=[((12, 3, 2, 40, 128), F32), ((2, 12, 2, 40, 128), F32)],
+        [((3, 4, 32, 128), BF16), ((4, 32, 128), F32)],
+        (affinity, e, ext, se, so, ms),
+        scratch=[
+            ((12, 3, 2, 40, 128), F32),
+            ((2, 12, 2, 40, 128), F32),
+            ((4, 32, 128), F32),
+            (pltpu.SemaphoreType.DMA, (5,)),
+        ],
+        out_specs=[HBM, HBM],
     )
     return (affinity, strength)
 

time: 45.4 us -> 38.6 us (0.85)
  the two profiles are of different devices: /device:TPU:6 before, /device:TPU:14 now
where the time goes in v4:
time: 38.6 us; the launch traced here: 38.2 us
  starting transfers between devices  18.6 us (48%)
  Pallas kernels  11.2 us (29%)
  waiting for transfers between devices  7.61 us (20%)
  between operations  0.74 us (2%)
    pallas_call x9, Pallas kernels, call(): pl.pallas_call(kernel, out_shape=[jax.ShapeDtypeStruct(s, d) for s, d in...  11.2 us
    ppermute x1, starting transfers between devices, body(): fo = lax.ppermute(fo, 'gx', odd_x)  5.74 us
    ppermute x1, starting transfers between devices, body(): xo = lax.ppermute(xo, 'gx', odd_x)  3.73 us
    ppermute x1, starting transfers between devices, body(): so = lax.ppermute(so, 'gx', odd_x)  3.53 us
    ppermute x1, waiting for transfers between devices, body(): se = lax.ppermute(se, 'gx', even_x)  2.67 us
    ppermute x1, starting transfers between devices, body(): zr = lax.ppermute(zs, 'gz', [(0, 1), (1, 0)])  2.38 us
    ppermute x1, waiting for transfers between devices, body(): so = lax.ppermute(so, 'gx', odd_x)  2.22 us
    ppermute x1, waiting for transfers between devices, body(): yo = lax.ppermute(yo, 'gy', odd)  1.91 us
  transfers between devices with their start and end apart: 9, of which 4 were waited for; matrix products, arithmetic and copies ran while one was open for 0% of the time, Pallas kernels for 15%

profile of v4, /device:TPU:14, one launch (start us, length us, event | category | flops | bytes accessed | tf_op | source)
XLA Modules:
  0.0 38.2 jit_solution(2049005766494896574)
XLA Ops:
  0.6 1.9 %shard_map.86 = (bf16[4,46,32,128]{3,2,1,0:T(8,128)(2,1)S(1)}, bf16[288,128]{1,0:T(8,128)(2,1)S(1)}, f32[2,4,32,128]{3,2,1,0:T(8,128)S(1)}, bf16[32,32,128]{2,1,0:T(8,128)(2,1)S(1)}, bf16[32,32,128]{2,1,0:T(8,128)(2,1)S(1)}) custom-call(bf16[32,4,32,128]{3,2,1,0:T(8,128)(2,1)} %x_hbm.1, s32[4,32,128]{2,1,0:T(8,128)} %m_hbm.1, s32[4,32,128]{2,1,0:T(8,128)} %s_hbm.1), custom_call_target="tpu_custom_call" | custom-call | tf_op jit(solution)/shard_map/pallas_call | solution.py:560
  2.5 2.4 %collective-permute-start = (bf16[288,128]{1,0:T(8,128)(2,1)S(1)}, bf16[288,128]{1,0:T(8,128)(2,1)S(1)}, u32[]{:S(2)}, u32[]{:S(2)}) collective-permute-start(bf16[288,128]{1,0:T(8,128)(2,1)S(1)} %get-tuple-element.53.zs_ref), channel_id=1, source_target_pairs={{0,1},{1,0},{2,3},{3,2},{4,5},{5,4},{6,7},{7,6},{8,9},{9,8},{10,11... | collective-permute-start | bytes 221192 | tf_op jit(solution)/shard_map/ppermute | solution.py:589
  4.9 1.9 %collective-permute-start.3 = (bf16[32,32,128]{2,1,0:T(8,128)(2,1)S(1)}, bf16[32,32,128]{2,1,0:T(8,128)(2,1)S(1)}, u32[]{:S(2)}, u32[]{:S(2)}) collective-permute-start(bf16[32,32,128]{2,1,0:T(8,128)(2,1)S(1)} %get-tuple-element.72), channel_id=1, source_target_pairs={{0,16},{16,0},{32,48},{48,32},{64,80},{80,64},{96,112},{112,96},{1... | collective-permute-start | bytes 786440 | tf_op jit(solution)/shard_map/ppermute | solution.py:592
  6.8 5.7 %collective-permute-start.4 = (bf16[32,32,128]{2,1,0:T(8,128)(2,1)S(1)}, bf16[32,32,128]{2,1,0:T(8,128)(2,1)S(1)}, u32[]{:S(2)}, u32[]{:S(2)}) collective-permute-start(bf16[32,32,128]{2,1,0:T(8,128)(2,1)S(1)} %get-tuple-element.73), channel_id=1, source_target_pairs={{16,32},{32,16},{48,64},{64,48},{80,96},{96,80},{112,128},{128,112... | collective-permute-start | bytes 786440 | tf_op jit(solution)/shard_map/ppermute | solution.py:591
  12.5 0.0 collective-permute-done.zr_ref
  12.5 0.1 shard_map.87
  12.7 0.1 collective-permute-start.1
  12.8 0.9 %collective-permute-start.2 = (bf16[4,208,128]{2,1,0:T(8,128)(2,1)S(1)}, bf16[4,208,128]{2,1,0:T(8,128)(2,1)S(1)}, u32[]{:S(2)}, u32[]{:S(2)}) collective-permute-start(bf16[4,208,128]{2,1,0:T(8,128)(2,1)S(1)} %get-tuple-element.59), channel_id=1, source_target_pairs={{2,4},{4,2},{6,8},{8,6},{10,12},{12,10},{14,0},{0,14},{3,5},{5,3},... | collective-permute-start | bytes 638984 | tf_op jit(solution)/shard_map/ppermute | solution.py:628
  13.7 1.2 %shard_map.88 = (bf16[96,288]{1,0:T(8,128)(2,1)S(1)}, bf16[288,96]{1,0:T(8,128)(2,1)S(1)}, f32[32,128]{1,0:T(8,128)S(1)}, f32[24,256]{1,0:T(8,128)S(1)}, f32[24,...) custom-call(bf16[27,32,32]{2,1,0:T(8,128)(2,1)} %bitcast.4, f32[1,32]{1,0:T(1,128)} %bitcast.5, ...), custom_call_target="tpu_custom_call" | custom-call | tf_op jit(solution)/shard_map/pallas_call | solution.py:560
  14.9 1.3 %shard_map.89.rows_ref = bf16[2,1280,128]{2,1,0:T(8,128)(2,1)S(1)} custom-call(bf16[4,46,32,128]{3,2,1,0:T(8,128)(2,1)S(1)} %get-tuple-element.60.v_ref.v_in_ref, bf16[96,288]{1,0:T(8,128)(2,1)S(1)} %get-tuple-element.65.w_ref, f32[32,128]{1,0:T(8,128)S(1)} %get-tuple-element.66.b_ref), custom_call_target="tpu_custom_call" | custom-call | tf_op jit(solution)/shard_map/pallas_call | solution.py:560
  16.2 1.9 %collective-permute-done.2.yo_ref = bf16[4,208,128]{2,1,0:T(8,128)(2,1)S(1)} collective-permute-done((bf16[4,208,128]{2,1,0:T(8,128)(2,1)S(1)}, bf16[4,208,128]{2,1,0:T(8,128)(2,1)S(1)}, u32[]{:S(2)}, u32[]{:S(2)}) %collective-permute-start.2) | collective-permute-done | bytes 213024 | tf_op jit(solution)/shard_map/ppermute | solution.py:628
  18.2 0.1 shard_map.90
  18.3 0.0 collective-permute-done.3.xe_ref
  18.3 0.1 collective-permute-start.5
  18.4 3.7 %collective-permute-start.6 = (bf16[14,32,128]{2,1,0:T(8,128)(2,1)S(1)}, bf16[14,32,128]{2,1,0:T(8,128)(2,1)S(1)}, u32[]{:S(2)}, u32[]{:S(2)}) collective-permute-start(bf16[14,32,128]{2,1,0:T(8,128)(2,1)S(1)} %get-tuple-element.76), channel_id=1, source_target_pairs={{16,32},{32,16},{48,64},{64,48},{80,96},{96,80},{112,128},{128,112... | collective-permute-start | bytes 344072 | tf_op jit(solution)/shard_map/ppermute | solution.py:637
  22.1 1.4 %shard_map.92 = (bf16[2,1280,128]{2,1,0:T(8,128)(2,1)S(1)}, bf16[2,46,32,128]{3,2,1,0:T(8,128)(2,1)S(1)}) custom-call(bf16[4,46,32,128]{3,2,1,0:T(8,128)(2,1)S(1)} %get-tuple-element.74.v_ref, bf16[32,32,128]{2,1,0:T(8,128)(2,1)S(1)} %collective-permute-done.3.xe_ref, bf16[32,32,128]{2,1,0:T(8,128)(2,1)S(1)} %collective-permute-done.4.xo_ref, ...), custom_call_target="tpu_custom_call" | custom-call | tf_op jit(solution)/shard_map/pallas_call | solution.py:560
  23.5 1.7 %shard_map.91 = (bf16[3,4,32,128]{3,2,1,0:T(8,128)(2,1)S(1)}, f32[4,4,40,128]{3,2,1,0:T(8,128)S(1)}, f32[4,4,40,128]{3,2,1,0:T(8,128)S(1)}) custom-call(bf16[4,46,32,128]{3,2,1,0:T(8,128)(2,1)S(1)} %get-tuple-element.74.v_ref, bf16[2,1280,128]{2,1,0:T(8,128)(2,1)S(1)} %shard_map.89.rows_ref, bf16[4,208,128]{2,1,0:T(8,128)(2,1)S(1)} %collective-permute-done.1.ye_ref, ...), custom_call_target="tpu_custom_call" | custom-call | tf_op jit(solution)/shard_map/pallas_call | solution.py:560
  25.2 0.8 %collective-permute-done.6.xo_ref = bf16[14,32,128]{2,1,0:T(8,128)(2,1)S(1)} collective-permute-done((bf16[14,32,128]{2,1,0:T(8,128)(2,1)S(1)}, bf16[14,32,128]{2,1,0:T(8,128)(2,1)S(1)}, u32[]{:S(2)}, u32[]{:S(2)}) %collective-permute-start.6) | collective-permute-done | bytes 114720 | tf_op jit(solution)/shard_map/ppermute | solution.py:637
  26.0 1.8 %shard_map.93 = (bf16[3,4,32,128]{3,2,1,0:T(8,128)(2,1)S(1)}, f32[4,4,40,128]{3,2,1,0:T(8,128)S(1)}, f32[4,4,40,128]{3,2,1,0:T(8,128)S(1)}, bf16[15,40,128]{2,1,0:T(8,128)(2,1)S(1)}, bf16[15,40,128]{2,1,0:T(8,128)(2,1)S(1)}) custom-call(bf16[4,46,32,128]{3,2,1,0:T(8,128)(2,1)S(1)} %get-tuple-element.74.v_ref, ...), custom_call_target="tpu_custom_call" | custom-call | tf_op jit(solution)/shard_map/pallas_call | solution.py:560
  27.8 0.2 collective-permute-start.7
  28.0 3.5 %collective-permute-start.8 = (bf16[15,40,128]{2,1,0:T(8,128)(2,1)S(1)}, bf16[15,40,128]{2,1,0:T(8,128)(2,1)S(1)}, u32[]{:S(2)}, u32[]{:S(2)}) collective-permute-start(bf16[15,40,128]{2,1,0:T(8,128)(2,1)S(1)} %get-tuple-element.101), channel_id=1, source_target_pairs={{16,32},{32,16},{48,64},{64,48},{80,96},{96,80},{112,128},{128,112... | collective-permute-start | bytes 460808 | tf_op jit(solution)/shard_map/ppermute | solution.py:665
  31.6 2.7 %collective-permute-done.7.re_ref = bf16[15,40,128]{2,1,0:T(8,128)(2,1)S(1)} collective-permute-done((bf16[15,40,128]{2,1,0:T(8,128)(2,1)S(1)}, bf16[15,40,128]{2,1,0:T(8,128)(2,1)S(1)}, u32[]{:S(2)}, u32[]{:S(2)}) %collective-permute-start.7) | collective-permute-done | bytes 153632 | tf_op jit(solution)/shard_map/ppermute | solution.py:666
  34.3 2.2 %collective-permute-done.8.ro_ref = bf16[15,40,128]{2,1,0:T(8,128)(2,1)S(1)} collective-permute-done((bf16[15,40,128]{2,1,0:T(8,128)(2,1)S(1)}, bf16[15,40,128]{2,1,0:T(8,128)(2,1)S(1)}, u32[]{:S(2)}, u32[]{:S(2)}) %collective-permute-start.8) | collective-permute-done | bytes 153632 | tf_op jit(solution)/shard_map/ppermute | solution.py:665
  36.5 1.7 %shard_map.94 = (bf16[3,4,32,128]{3,2,1,0:T(8,128)(2,1)}, f32[4,32,128]{2,1,0:T(8,128)}) custom-call(bf16[3,4,32,128]{3,2,1,0:T(8,128)(2,1)S(1)} %get-tuple-element.97.a_ref, f32[4,4,40,128]{3,2,1,0:T(8,128)S(1)} %get-tuple-element.98.e_ref, f32[4,4,40,128]{3,2,1,0:T(8,128)S(1)} %get-tuple-element.99.ext_ref, ...), custom_call_target="tpu_custom_call" | custom-call | tf_op jit(solution)/shard_map/pallas_call | solution.py:560
  (3 shorter events, 0.0 us)
Async XLA Ops:
  2.5 10.0 %collective-permute-start = (bf16[288,128]{1,0:T(8,128)(2,1)S(1)}, bf16[288,128]{1,0:T(8,128)(2,1)S(1)}, u32[]{:S(2)}, u32[]{:S(2)}) collective-permute-start(bf16[288,128]{1,0:T(8,128)(2,1)S(1)} %get-tuple-element.53.zs_ref), channel_id=1, source_target_pairs={{0,1},{1,0},{2,3},{3,2},{4,5},{5,4},{6,7},{7,6},{8,9},{9,8},{10,11... | collective-permute-start | bytes 221192 | tf_op jit(solution)/shard_map/ppermute | solution.py:589
  4.9 13.4 %collective-permute-start.3 = (bf16[32,32,128]{2,1,0:T(8,128)(2,1)S(1)}, bf16[32,32,128]{2,1,0:T(8,128)(2,1)S(1)}, u32[]{:S(2)}, u32[]{:S(2)}) collective-permute-start(bf16[32,32,128]{2,1,0:T(8,128)(2,1)S(1)} %get-tuple-element.72), channel_id=1, source_target_pairs={{0,16},{16,0},{32,48},{48,32},{64,80},{80,64},{96,112},{112,96},{1... | collective-permute-start | bytes 786440 | tf_op jit(solution)/shard_map/ppermute | solution.py:592
  6.8 11.5 %collective-permute-start.4 = (bf16[32,32,128]{2,1,0:T(8,128)(2,1)S(1)}, bf16[32,32,128]{2,1,0:T(8,128)(2,1)S(1)}, u32[]{:S(2)}, u32[]{:S(2)}) collective-permute-start(bf16[32,32,128]{2,1,0:T(8,128)(2,1)S(1)} %get-tuple-element.73), channel_id=1, source_target_pairs={{16,32},{32,16},{48,64},{64,48},{80,96},{96,80},{112,128},{128,112... | collective-permute-start | bytes 786440 | tf_op jit(solution)/shard_map/ppermute | solution.py:591
  12.7 3.5 %collective-permute-start.1 = (bf16[4,208,128]{2,1,0:T(8,128)(2,1)S(1)}, bf16[4,208,128]{2,1,0:T(8,128)(2,1)S(1)}, u32[]{:S(2)}, u32[]{:S(2)}) collective-permute-start(bf16[4,208,128]{2,1,0:T(8,128)(2,1)S(1)} %get-tuple-element.58), channel_id=1, source_target_pairs={{0,2},{2,0},{4,6},{6,4},{8,10},{10,8},{12,14},{14,12},{1,3},{3,1},... | collective-permute-start | bytes 638984 | tf_op jit(solution)/shard_map/ppermute | solution.py:629
  12.8 5.4 %collective-permute-start.2 = (bf16[4,208,128]{2,1,0:T(8,128)(2,1)S(1)}, bf16[4,208,128]{2,1,0:T(8,128)(2,1)S(1)}, u32[]{:S(2)}, u32[]{:S(2)}) collective-permute-start(bf16[4,208,128]{2,1,0:T(8,128)(2,1)S(1)} %get-tuple-element.59), channel_id=1, source_target_pairs={{2,4},{4,2},{6,8},{8,6},{10,12},{12,10},{14,0},{0,14},{3,5},{5,3},... | collective-permute-start | bytes 638984 | tf_op jit(solution)/shard_map/ppermute | solution.py:628
  18.3 6.9 %collective-permute-start.5 = (bf16[14,32,128]{2,1,0:T(8,128)(2,1)S(1)}, bf16[14,32,128]{2,1,0:T(8,128)(2,1)S(1)}, u32[]{:S(2)}, u32[]{:S(2)}) collective-permute-start(bf16[14,32,128]{2,1,0:T(8,128)(2,1)S(1)} %get-tuple-element.75), channel_id=1, source_target_pairs={{0,16},{16,0},{32,48},{48,32},{64,80},{80,64},{96,112},{112,96},{1... | collective-permute-start | bytes 344072 | tf_op jit(solution)/shard_map/ppermute | solution.py:638
  18.4 7.6 %collective-permute-start.6 = (bf16[14,32,128]{2,1,0:T(8,128)(2,1)S(1)}, bf16[14,32,128]{2,1,0:T(8,128)(2,1)S(1)}, u32[]{:S(2)}, u32[]{:S(2)}) collective-permute-start(bf16[14,32,128]{2,1,0:T(8,128)(2,1)S(1)} %get-tuple-element.76), channel_id=1, source_target_pairs={{16,32},{32,16},{48,64},{64,48},{80,96},{96,80},{112,128},{128,112... | collective-permute-start | bytes 344072 | tf_op jit(solution)/shard_map/ppermute | solution.py:637
  27.8 6.4 %collective-permute-start.7 = (bf16[15,40,128]{2,1,0:T(8,128)(2,1)S(1)}, bf16[15,40,128]{2,1,0:T(8,128)(2,1)S(1)}, u32[]{:S(2)}, u32[]{:S(2)}) collective-permute-start(bf16[15,40,128]{2,1,0:T(8,128)(2,1)S(1)} %get-tuple-element.100), channel_id=1, source_target_pairs={{0,16},{16,0},{32,48},{48,32},{64,80},{80,64},{96,112},{112,96},{1... | collective-permute-start | bytes 460808 | tf_op jit(solution)/shard_map/ppermute | solution.py:666
  28.0 8.4 %collective-permute-start.8 = (bf16[15,40,128]{2,1,0:T(8,128)(2,1)S(1)}, bf16[15,40,128]{2,1,0:T(8,128)(2,1)S(1)}, u32[]{:S(2)}, u32[]{:S(2)}) collective-permute-start(bf16[15,40,128]{2,1,0:T(8,128)(2,1)S(1)} %get-tuple-element.101), channel_id=1, source_target_pairs={{16,32},{32,16},{48,64},{64,48},{80,96},{96,80},{112,128},{128,112... | collective-permute-start | bytes 460808 | tf_op jit(solution)/shard_map/ppermute | solution.py:665

commit v5 on v4

--- a/solution.py
+++ b/solution.py
@@ -13,9 +13,7 @@
 PARAMS = pltpu.CompilerParams(vmem_limit_bytes=12 * 2**20)
 
 
-def swaps(axis):
-    count = lax.axis_size(axis)
-
+def swaps(count):
     def pairs(first):
         return [
             p
@@ -26,6 +24,24 @@
     return pairs(0), pairs(1)
 
 
+def swaps_gx():
+    nx, ny = lax.axis_size("gx"), lax.axis_size("gy")
+
+    def partner(x, y, first):
+        other = x + 1 if x % 2 == first else x - 1
+        return (other, y) if 0 <= other < nx else (x, y ^ 1)
+
+    def pairs(first):
+        out = []
+        for x in range(nx):
+            for y in range(ny):
+                px, py = partner(x, y, first)
+                out.append((x * ny + y, px * ny + py))
+        return out
+
+    return pairs(0), pairs(1)
+
+
 def iota(shape, dim):
     return lax.broadcasted_iota(jnp.int32, shape, dim)
 
@@ -33,32 +49,19 @@
 def pack_kernel(x_hbm, m_hbm, s_hbm, v_ref, zs_ref, ms_ref, xe_ref, xo_ref, x_ref, m_ref, s_ref, sems):
     gz = lax.axis_index("gz")
     copies = [pltpu.make_async_copy(x_hbm.at[:, x], x_ref.at[x], sems.at[x]) for x in range(4)]
-    copies += [
+    small = [
         pltpu.make_async_copy(m_hbm, m_ref, sems.at[4]),
         pltpu.make_async_copy(s_hbm, s_ref, sems.at[5]),
     ]
-    for copy in copies:
+    for copy in small + copies:
         copy.start()
     lane = iota((128, 128), 1)
     row = iota((128, 128), 0)
     base = jnp.where(gz == 0, 120, 0)
     hit = row == base + lane % 8
     sels = [jnp.where(hit & (lane // 8 == y), 1.0, 0.0).astype(BF16) for y in range(16)]
-    for x in range(4):
-        copies[x].wait()
-        v_ref[x, 5:37] = jnp.swapaxes(x_ref[x], 0, 1)
-    even_face = jnp.where(lax.axis_index("gx") % 2 == 0, 3, 0)
-    xe_ref[...] = v_ref[even_face, 5:37]
-    xo_ref[...] = v_ref[3 - even_face, 5:37]
-    acc = jnp.zeros((256, 128), F32)
-    for y in range(16):
-        lhs = jnp.concatenate(
-            [v_ref[x, 5 + 16 * half + y] for x in range(4) for half in range(2)], axis=0
-        )
-        acc = acc + jnp.dot(lhs, sels[y], preferred_element_type=F32)
-    zs_ref[0:256] = acc.astype(BF16)
-    copies[4].wait()
-    copies[5].wait()
+    for copy in small:
+        copy.wait()
     lane = iota((32, 128), 1)
     edge = (lane >= jnp.where(gz == 0, 124, 0)) & (lane < jnp.where(gz == 0, 128, 4))
     packed = jnp.zeros((32, 128), F32)
@@ -67,10 +70,26 @@
         seed = mask * s_ref[x].astype(F32)
         ms_ref[0, x] = mask
         ms_ref[1, x] = seed
+        xe_ref[32 + x] = seed.astype(BF16)
+        xo_ref[32 + x] = seed.astype(BF16)
         for slot, value in ((x, mask), (4 + x, seed)):
             value = jnp.where(edge, value, 0.0)
             packed = packed + (pltpu.roll(value, 8 * slot, 1) if slot else value)
     zs_ref[256:288] = packed.astype(BF16)
+    for x in range(4):
+        copies[x].wait()
+        v_ref[x, 5:37] = jnp.swapaxes(x_ref[x], 0, 1)
+    acc = jnp.zeros((256, 128), F32)
+    for y in range(16):
+        lhs = jnp.concatenate(
+            [v_ref[x, 5 + 16 * half + y] for x in range(4) for half in range(2)], axis=0
+        )
+        acc = acc + jnp.dot(lhs, sels[y], preferred_element_type=F32)
+    zs_ref[0:256] = acc.astype(BF16)
+    zs_ref[288:320] = jnp.zeros((32, 128), BF16)
+    even_face = jnp.where(lax.axis_index("gx") % 2 == 0, 3, 0)
+    xe_ref[0:32] = v_ref[even_face, 5:37]
+    xo_ref[0:32] = v_ref[3 - even_face, 5:37]
 
 
 def weights_kernel(
@@ -201,8 +220,8 @@
 
     even_face = jnp.where(odd_x == 0, 3, 0)
     for dst_ref, face in ((xe_ref, even_face), (xo_ref, 3 - even_face)):
-        dst_ref[0:5] = v_ref[face, 0:5]
-        dst_ref[5:14] = v_ref[face, 37:46]
+        dst_ref[0:4] = v_ref[face, 1:5]
+        dst_ref[4:13] = v_ref[face, 37:46]
 
 
 def head(hidden, head_ref, bias_ref):
@@ -308,12 +327,14 @@
         fill(even_ref, odd_ref)
 
 
-def border_rows_kernel(v_ref, xe_ref, xo_ref, w_ref, b_ref, hid_ref, face_ref):
+def border_rows_kernel(v_ref, xe_ref, xo_ref, w_ref, b_ref, hid_ref, face_ref, seeds_ref):
     gx = lax.axis_index("gx")
 
     def fill(low_ref, high_ref):
-        face_ref[0, 5:37] = low_ref[...]
-        face_ref[1, 5:37] = high_ref[...]
+        face_ref[0, 5:37] = low_ref[0:32]
+        face_ref[1, 5:37] = high_ref[0:32]
+        seeds_ref[0] = low_ref[32:36]
+        seeds_ref[1] = high_ref[32:36]
 
     by_side(xe_ref, xo_ref, fill)
 
@@ -336,7 +357,7 @@
 
 def inner_kernel(
     v_ref, rows_ref, ye_ref, yo_ref, zr_ref, ms_ref, w_ref, wp_ref, b_ref, hw_ref, hb_ref, hwp_ref, hbp_ref,
-    a_ref, e_ref, ext_ref, hid_ref, mask_ref, mext_ref,
+    a_ref, e_ref, ext_ref, tile_ref, slots_ref, hid_ref, mask_ref, mext_ref,
 ):
     gy = lax.axis_index("gy")
     odd_y = gy % 2
@@ -388,19 +409,26 @@
             refs = [v_ref.at[x - 1 + d] for d in range(3)]
             a = conv_slice(gz, refs, weights, spread, rows_ref.at[x - 1], hid_ref.at[x - 1])
             for f in range(3):
-                a_ref[f, x] = a[f][0][0:32].astype(BF16)
+                a_ref[f, x - 1] = a[f][0][0:32].astype(BF16)
                 e_ref[x, f] = a[f][0] * keep[f][0]
                 ext_ref[x, f] = a[f][1] * keep[f][1]
+                tile_ref[x - 1, f] = e_ref[x, f].astype(BF16)
         else:
             for f in range(3):
                 e_ref[x, f] = keep[f][0]
                 ext_ref[x, f] = keep[f][1]
         e_ref[x, 3] = mask_ref[1, x]
         ext_ref[x, 3] = mext_ref[1, x]
+    for way, order in enumerate(((2, 1), (1, 2))):
+        packed = jnp.zeros((40, 128), F32)
+        for j, x in enumerate(order):
+            for f in range(4):
+                packed = packed + pltpu.roll(ext_ref[x, f], 8 * (4 * (j + 1) + f), 1)
+        slots_ref[way] = packed
 
 
 def border_kernel(
-    v_ref, face_ref, rows_ref, xe_ref, xo_ref, a_in, e_in, ext_in, w_ref, wp_ref, b_ref, hw_ref, hb_ref, hwp_ref, hbp_ref,
+    v_ref, face_ref, rows_ref, xe_ref, xo_ref, e_in, ext_in, tile_ref, slots_ref, w_ref, wp_ref, b_ref, hw_ref, hb_ref, hwp_ref, hbp_ref,
     a_ref, e_ref, ext_ref, se_ref, so_ref, side_ref, hid_ref,
 ):
     gx = lax.axis_index("gx")
@@ -409,8 +437,9 @@
 
     def fill(low_ref, high_ref):
         for i, ref in enumerate((low_ref, high_ref)):
-            side_ref[i, 0:5] = ref[0:5]
-            side_ref[i, 37:46] = ref[5:14]
+            side_ref[i, 0] = jnp.zeros((32, 128), BF16)
+            side_ref[i, 1:5] = ref[0:4]
+            side_ref[i, 37:46] = ref[4:13]
 
     by_side(xe_ref, xo_ref, fill)
     for i, end in ((0, 0), (1, 15)):
@@ -421,14 +450,6 @@
         def _():
             side_ref[i, 0:5] = jnp.zeros((5, 32, 128), BF16)
             side_ref[i, 37:46] = jnp.zeros((9, 32, 128), BF16)
-
-    for x in (1, 2):
-        a_ref[:, x] = a_in[:, x]
-        e_ref[x] = e_in[x]
-        ext_ref[x] = ext_in[x]
-    for x in (0, 3):
-        e_ref[x, 3] = e_in[x, 3]
-        ext_ref[x, 3] = ext_in[x, 3]
 
     weights = (w_ref, wp_ref, b_ref, hw_ref, hb_ref, hwp_ref, hbp_ref)
     spread = spread_matrix(gz)
@@ -438,80 +459,89 @@
     ):
         a = conv_slice(gz, refs, weights, spread, rows_ref.at[x // 3], hid_ref.at[x // 3])
         for f in range(3):
-            a_ref[f, x] = a[f][0][0:32].astype(BF16)
-            e_ref[x, f] = a[f][0] * e_in[x, f]
-            ext_ref[x, f] = a[f][1] * ext_in[x, f]
-
-    def send(dst_ref, order):
-        packed = jnp.zeros((40, 128), F32)
-        for j, x in enumerate(order):
-            for f in range(4 if j < 3 else 0):
-                value = ext_ref[x, f]
-                slot = 4 * j + f
-                packed = packed + (pltpu.roll(value, 8 * slot, 1) if slot else value)
-                dst_ref[slot] = e_ref[x, f].astype(BF16)
-        dst_ref[12] = e_ref[order[3], 3].astype(BF16)
-        dst_ref[13] = e_ref[order[3], 0].astype(BF16)
-        dst_ref[14] = packed.astype(BF16)
+            a_ref[f, x // 3] = a[f][0][0:32].astype(BF16)
+            e_ref[x // 3, f] = a[f][0] * e_in[x, f]
+            ext_ref[x // 3, f] = a[f][1] * ext_in[x, f]
+
+    def send(dst_ref, way, order):
+        packed = slots_ref[way]
+        for f in range(4):
+            x = order[0]
+            value = ext_ref[x // 3, f] if f < 3 else ext_in[x, 3]
+            packed = packed + (pltpu.roll(value, 8 * f, 1) if f else value)
+        for f in range(3):
+            dst_ref[f] = e_ref[order[0] // 3, f].astype(BF16)
+            dst_ref[3 + f] = tile_ref[order[1] - 1, f]
+            dst_ref[6 + f] = tile_ref[order[2] - 1, f]
+            dst_ref[11, 8 * f : 8 * f + 8] = e_in[order[f], 3, 32:40].astype(BF16)
+        dst_ref[9] = e_ref[order[3] // 3, 0].astype(BF16)
+        dst_ref[10] = packed.astype(BF16)
+
+    up, down = (0, (3, 2, 1, 0)), (1, (0, 1, 2, 3))
 
     @pl.when(odd_x == 0)
     def _():
-        send(se_ref, (3, 2, 1, 0))
-        send(so_ref, (0, 1, 2, 3))
+        send(se_ref, *up)
+        send(so_ref, *down)
 
     @pl.when(odd_x == 1)
     def _():
-        send(se_ref, (0, 1, 2, 3))
-        send(so_ref, (3, 2, 1, 0))
-
-
-def rounds_kernel(a_ref, e_ref, ext_ref, re_ref, ro_ref, ms_ref, a_hbm, out_hbm, all_ref, s_ref, out_ref, sems):
-    affinity_copy = pltpu.make_async_copy(a_ref, a_hbm, sems.at[4])
-    affinity_copy.start()
+        send(se_ref, *down)
+        send(so_ref, *up)
+
+
+def rounds_kernel(
+    ai_ref, ab_ref, ei_ref, exti_ref, eb_ref, extb_ref, seeds_ref, re_ref, ro_ref, ms_ref,
+    a_hbm, out_hbm, all_ref, s_ref, out_ref, sems,
+):
     gx = lax.axis_index("gx")
-    odd_x = gx % 2
+    gz = lax.axis_index("gz")
+    copies = [
+        pltpu.make_async_copy(ai_ref, a_hbm.at[:, 1:3], sems.at[4]),
+        pltpu.make_async_copy(ab_ref.at[:, 0:1], a_hbm.at[:, 0:1], sems.at[5]),
+        pltpu.make_async_copy(ab_ref.at[:, 1:2], a_hbm.at[:, 3:4], sems.at[6]),
+    ]
+    for copy in copies:
+        copy.start()
     has_low = jnp.where(gx == 0, 0.0, 1.0)
     has_high = jnp.where(gx == 15, 0.0, 1.0)
-    gz = lax.axis_index("gz")
-
-    def place(src_ref, places, keep_last):
-        has = has_high if keep_last else has_low
-        packed = src_ref[14].astype(F32) * has
+    zero = jnp.zeros((40, 128), F32)
+
+    def place(src_ref, places, has):
+        packed = src_ref[10].astype(F32) * has
+        high = places[0] == 8
         for j, at in enumerate(places):
-            for f in range(4):
-                scale = (lambda v: v / 15.0) if f == 3 else (lambda v: v)
-                ext = scale(unpack_ext(packed, 4 * j + f, gz)) if j < 3 else jnp.zeros_like(packed)
-                if j < 3:
-                    main = scale(src_ref[4 * j + f].astype(F32) * has)
-                elif f == 3:
-                    main = scale(src_ref[12].astype(F32) * has)
-                elif f == 0 and keep_last:
-                    main = src_ref[13].astype(F32) * has
-                else:
-                    main = jnp.zeros_like(packed)
-                if f == 3:
-                    s_ref[0, at, 0] = main
-                    s_ref[0, at, 1] = ext
-                else:
-                    all_ref[at, f, 0] = main
-                    all_ref[at, f, 1] = ext
-
-    @pl.when(odd_x == 0)
-    def _():
-        place(ro_ref, (3, 2, 1, 0), False)
-        place(re_ref, (8, 9, 10, 11), True)
-
-    @pl.when(odd_x == 1)
-    def _():
-        place(re_ref, (3, 2, 1, 0), False)
-        place(ro_ref, (8, 9, 10, 11), True)
+            seeds = seeds_ref[1, j] if high else seeds_ref[0, 3 - j]
+            s_ref[0, at, 0, 0:32] = seeds.astype(F32) * has / 15.0
+            if j == 3:
+                s_ref[0, at, 0, 32:40] = zero[0:8]
+                s_ref[0, at, 1] = zero
+                all_ref[at % 8 if high else 4 + at, 0, 0] = src_ref[9].astype(F32) * has
+                all_ref[at % 8 if high else 4 + at, 0, 1] = zero
+                continue
+            s_ref[0, at, 0, 32:40] = src_ref[11, 8 * j : 8 * j + 8].astype(F32) * has / 15.0
+            s_ref[0, at, 1] = unpack_ext(packed, 4 * j + 3, gz) / 15.0
+            for f in range(3):
+                where = at % 8 if high else 4 + at
+                all_ref[where, f, 0] = src_ref[3 * j + f].astype(F32) * has
+                all_ref[where, f, 1] = unpack_ext(packed, 4 * j + f, gz)
+
+    def fill(low_ref, high_ref):
+        place(low_ref, (3, 2, 1, 0), has_low)
+        place(high_ref, (8, 9, 10, 11), has_high)
+
+    by_side(re_ref, ro_ref, fill)
 
     for x in range(4):
-        for f in range(3):
-            all_ref[4 + x, f, 0] = e_ref[x, f]
-            all_ref[4 + x, f, 1] = ext_ref[x, f]
-        s_ref[0, 4 + x, 0] = e_ref[x, 3] / 15.0
-        s_ref[0, 4 + x, 1] = ext_ref[x, 3] / 15.0
+        s_ref[0, 4 + x, 0] = ei_ref[x, 3] / 15.0
+        s_ref[0, 4 + x, 1] = exti_ref[x, 3] / 15.0
+
+    def edge(at, f, i):
+        if at < 4 or at > 7:
+            return all_ref[4 + at if at < 4 else at - 8, f, i]
+        if at in (5, 6):
+            return (ei_ref, exti_ref)[i][at - 4, f]
+        return (eb_ref, extb_ref)[i][(at - 4) // 3, f]
 
     lane = iota((40, 128), 1)
 
@@ -525,29 +555,28 @@
 
     for r in range(ROUNDS):
         src, dst = r % 2, (r + 1) % 2
-
         for x in range(r + 1, 11 - r):
             here = (s_ref[src, x, 0], s_ref[src, x, 1])
-            best = list(here)
-            ez = (all_ref[x, 2, 0], all_ref[x, 2, 1])
+            ez = (edge(x, 2, 0), edge(x, 2, 1))
             z_low = down(here)
             z_high = up(tuple(jnp.minimum(here[i], ez[i]) for i in range(2)))
-            for i in range(2):
-                ey = all_ref[x, 1, i]
+            for i in range(1 if r == ROUNDS - 1 else 2):
+                ey = edge(x, 1, i)
                 value = here[i]
-                value = jnp.maximum(value, jnp.minimum(s_ref[src, x - 1, i], all_ref[x, 0, i]))
-                value = jnp.maximum(value, jnp.minimum(s_ref[src, x + 1, i], all_ref[x + 1, 0, i]))
+                value = jnp.maximum(value, jnp.minimum(s_ref[src, x - 1, i], edge(x, 0, i)))
+                value = jnp.maximum(value, jnp.minimum(s_ref[src, x + 1, i], edge(x + 1, 0, i)))
                 value = jnp.maximum(value, jnp.minimum(pltpu.roll(here[i], 1, 0), ey))
                 value = jnp.maximum(value, pltpu.roll(jnp.minimum(here[i], ey), 39, 0))
                 value = jnp.maximum(value, jnp.minimum(z_low[i], ez[i]))
                 value = jnp.maximum(value, z_high[i])
-                s_ref[dst, x, i] = value
-
-    copies = [affinity_copy]
-    for x in range(4):
-        out_ref[x] = s_ref[ROUNDS % 2, 4 + x, 0, 0:32] * ms_ref[0, x]
-        copies.append(pltpu.make_async_copy(out_ref.at[x], out_hbm.at[x], sems.at[x]))
-        copies[-1].start()
+                if r < ROUNDS - 1:
+                    s_ref[dst, x, i] = value
+                else:
+                    out_ref[x - 4] = value[0:32] * ms_ref[0, x - 4]
+                    copies.append(
+                        pltpu.make_async_copy(out_ref.at[x - 4], out_hbm.at[x - 4], sems.at[x - 4])
+                    )
+                    copies[-1].start()
     for copy in copies:
         copy.wait()
 
@@ -572,10 +601,10 @@
         pack_kernel,
         [
             ((4, 46, 32, 128), BF16),
-            ((288, 128), BF16),
+            ((320, 128), BF16),
             ((2, 4, 32, 128), F32),
-            ((32, 32, 128), BF16),
-            ((32, 32, 128), BF16),
+            ((36, 32, 128), BF16),
+            ((36, 32, 128), BF16),
         ],
         tuple(stay(a) for a in (features, mask, seeds)),
         scratch=[
@@ -587,9 +616,10 @@
         specs=[HBM] * 3,
     )
     zr = lax.ppermute(zs, "gz", [(0, 1), (1, 0)])
-    even_x, odd_x = swaps("gx")
-    fo = lax.ppermute(fo, "gx", odd_x)
-    fe = lax.ppermute(fe, "gx", even_x)
+    even_x, odd_x = swaps_gx()
+    axes = ("gx", "gy")
+    fo = lax.ppermute(fo, axes, odd_x)
+    fe = lax.ppermute(fe, axes, even_x)
     pt, ye, yo = call(
         yface_kernel,
         [((4, 2, 32, 128), BF16), ((4, 208, 128), BF16), ((4, 208, 128), BF16)],
@@ -624,55 +654,61 @@
     weights = tuple(forms)
     rows_shape = [((2, 1280, 128), BF16)]
     (inner_rows,) = call(inner_rows_kernel, rows_shape, (vy, weights[0], weights[2]))
-    even, odd = swaps("gy")
+    even, odd = swaps(lax.axis_size("gy"))
     yo = lax.ppermute(yo, "gy", odd)
     ye = lax.ppermute(ye, "gy", even)
     ye, yo, inner_rows = lax.optimization_barrier((ye, yo, inner_rows))
     v, xe, xo = call(
         xface_kernel,
-        [((4, 46, 32, 128), BF16), ((14, 32, 128), BF16), ((14, 32, 128), BF16)],
+        [((4, 46, 32, 128), BF16), ((13, 32, 128), BF16), ((13, 32, 128), BF16)],
         (v, pt, ye, yo),
     )
     xe, xo, v, fe, fo = lax.optimization_barrier((xe, xo, v, fe, fo))
-    xo = lax.ppermute(xo, "gx", odd_x)
-    xe = lax.ppermute(xe, "gx", even_x)
-    affinity, e, ext = call(
+    xo = lax.ppermute(xo, axes, odd_x)
+    xe = lax.ppermute(xe, axes, even_x)
+    inner_a, e, ext, tiles, slots = call(
         inner_kernel,
-        [((3, 4, 32, 128), BF16), ((4, 4, 40, 128), F32), ((4, 4, 40, 128), F32)],
+        [
+            ((3, 2, 32, 128), BF16),
+            ((4, 4, 40, 128), F32),
+            ((4, 4, 40, 128), F32),
+            ((2, 3, 40, 128), BF16),
+            ((2, 40, 128), F32),
+        ],
         (v, inner_rows, ye, yo, zr, ms) + weights,
         scratch=[((2, 1280, 128), BF16), ((2, 4, 40, 128), F32), ((2, 4, 40, 128), F32)],
     )
-    border_rows, faces = call(
+    border_rows, faces, side_seeds = call(
         border_rows_kernel,
-        rows_shape + [((2, 46, 32, 128), BF16)],
+        rows_shape + [((2, 46, 32, 128), BF16), ((2, 4, 32, 128), BF16)],
         (v, fe, fo, weights[0], weights[2]),
     )
-    xe, xo, affinity, e, ext, border_rows, faces = lax.optimization_barrier(
-        (xe, xo, affinity, e, ext, border_rows, faces)
-    )
-    affinity, e, ext, se, so = call(
+    xe, xo, e, ext, border_rows, faces = lax.optimization_barrier(
+        (xe, xo, e, ext, border_rows, faces)
+    )
+    border_a, border_e, border_ext, se, so = call(
         border_kernel,
         [
-            ((3, 4, 32, 128), BF16),
-            ((4, 4, 40, 128), F32),
-            ((4, 4, 40, 128), F32),
-            ((15, 40, 128), BF16),
-            ((15, 40, 128), BF16),
+            ((3, 2, 32, 128), BF16),
+            ((2, 3, 40, 128), F32),
+            ((2, 3, 40, 128), F32),
+            ((12, 40, 128), BF16),
+            ((12, 40, 128), BF16),
         ],
-        (v, faces, border_rows, xe, xo, affinity, e, ext) + weights,
+        (v, faces, border_rows, xe, xo, e, ext, tiles, slots) + weights,
         scratch=[((2, 46, 32, 128), BF16), ((2, 1280, 128), BF16)],
     )
-    so = lax.ppermute(so, "gx", odd_x)
-    se = lax.ppermute(se, "gx", even_x)
+    so = lax.ppermute(so, axes, odd_x)
+    se = lax.ppermute(se, axes, even_x)
     affinity, strength = call(
         rounds_kernel,
         [((3, 4, 32, 128), BF16), ((4, 32, 128), F32)],
-        (affinity, e, ext, se, so, ms),
+        (inner_a, border_a, e, ext, border_e, border_ext, side_seeds, se, so, ms),
         scratch=[
-            ((12, 3, 2, 40, 128), F32),
+            ((8, 3, 2, 40, 128), F32),
             ((2, 12, 2, 40, 128), F32),
             ((4, 32, 128), F32),
-            (pltpu.SemaphoreType.DMA, (5,)),
+            (pltpu.SemaphoreType.DMA, (7,)),
         ],
         out_specs=[HBM, HBM],
     )

time: 38.6 us -> 38 us (0.984)
  starting transfers between devices: 18.6 us -> 18 us
  waiting for transfers between devices: 7.61 us -> 8.01 us
    ppermute x6, starting transfers between devices: 15.2 us -> 14.6 us  [the longest x1 5.73 us: body(): fo = lax.ppermute(fo, axes, odd_x)]
    ppermute x6, waiting for transfers between devices: 5.69 us -> 6.08 us  [the longest x1 2.36 us: body(): se = lax.ppermute(se, axes, even_x)]
  transfers between devices with their start and end apart: 9 -> 9, of which waited for: 4 -> 5; matrix products, arithmetic and copies ran while one was open for 0% -> 0% of each run, Pallas kernels for 15% -> 15%
where the time goes in v5:
time: 38 us; the launch traced here: 37.8 us
  starting transfers between devices  18 us (47%)
  Pallas kernels  11.1 us (29%)
  waiting for transfers between devices  8.01 us (21%)
  between operations  0.73 us (2%)
    pallas_call x9, Pallas kernels, call(): pl.pallas_call(kernel, out_shape=[jax.ShapeDtypeStruct(s, d) for s, d in...  11.1 us
    ppermute x1, starting transfers between devices, body(): fo = lax.ppermute(fo, axes, odd_x)  5.73 us
    ppermute x1, starting transfers between devices, body(): xo = lax.ppermute(xo, axes, odd_x)  3.85 us
    ppermute x1, starting transfers between devices, body(): so = lax.ppermute(so, axes, odd_x)  2.97 us
    ppermute x1, starting transfers between devices, body(): zr = lax.ppermute(zs, 'gz', [(0, 1), (1, 0)])  2.38 us
    ppermute x1, waiting for transfers between devices, body(): se = lax.ppermute(se, axes, even_x)  2.36 us
    ppermute x1, waiting for transfers between devices, body(): so = lax.ppermute(so, axes, odd_x)  2.21 us
    ppermute x1, waiting for transfers between devices, body(): yo = lax.ppermute(yo, 'gy', odd)  1.92 us
  transfers between devices with their start and end apart: 9, of which 5 were waited for; matrix products, arithmetic and copies ran while one was open for 0% of the time, Pallas kernels for 15%

profile of v5, /device:TPU:14, one launch (start us, length us, event | category | flops | bytes accessed | tf_op | source)
XLA Modules:
  0.0 37.8 jit_solution(5488424767332524122)
XLA Ops:
  0.6 1.8 %shard_map.86 = (bf16[4,46,32,128]{3,2,1,0:T(8,128)(2,1)S(1)}, bf16[320,128]{1,0:T(8,128)(2,1)S(1)}, f32[2,4,32,128]{3,2,1,0:T(8,128)S(1)}, bf16[36,32,128]{2,1,0:T(8,128)(2,1)S(1)}, bf16[36,32,128]{2,1,0:T(8,128)(2,1)S(1)}) custom-call(bf16[32,4,32,128]{3,2,1,0:T(8,128)(2,1)} %x_hbm.1, s32[4,32,128]{2,1,0:T(8,128)} %m_hbm.1, s32[4,32,128]{2,1,0:T(8,128)} %s_hbm.1), custom_call_target="tpu_custom_call" | custom-call | tf_op jit(solution)/shard_map/pallas_call | solution.py:589
  2.5 2.4 %collective-permute-start = (bf16[320,128]{1,0:T(8,128)(2,1)S(1)}, bf16[320,128]{1,0:T(8,128)(2,1)S(1)}, u32[]{:S(2)}, u32[]{:S(2)}) collective-permute-start(bf16[320,128]{1,0:T(8,128)(2,1)S(1)} %get-tuple-element.55.zs_ref), channel_id=1, source_target_pairs={{0,1},{1,0},{2,3},{3,2},{4,5},{5,4},{6,7},{7,6},{8,9},{9,8},{10,11... | collective-permute-start | bytes 245768 | tf_op jit(solution)/shard_map/ppermute | solution.py:618
  4.9 1.9 %collective-permute-start.3 = (bf16[36,32,128]{2,1,0:T(8,128)(2,1)S(1)}, bf16[36,32,128]{2,1,0:T(8,128)(2,1)S(1)}, u32[]{:S(2)}, u32[]{:S(2)}) collective-permute-start(bf16[36,32,128]{2,1,0:T(8,128)(2,1)S(1)} %get-tuple-element.74), channel_id=1, source_target_pairs={{0,16},{2,18},{4,20},{6,22},{8,24},{10,26},{12,28},{14,30},{16,0},... | collective-permute-start | bytes 884744 | tf_op jit(solution)/shard_map/ppermute | solution.py:622
  6.8 5.7 %collective-permute-start.4 = (bf16[36,32,128]{2,1,0:T(8,128)(2,1)S(1)}, bf16[36,32,128]{2,1,0:T(8,128)(2,1)S(1)}, u32[]{:S(2)}, u32[]{:S(2)}) collective-permute-start(bf16[36,32,128]{2,1,0:T(8,128)(2,1)S(1)} %get-tuple-element.75), channel_id=1, source_target_pairs={{0,2},{2,0},{4,6},{6,4},{8,10},{10,8},{12,14},{14,12},{16,32},{18,... | collective-permute-start | bytes 884744 | tf_op jit(solution)/shard_map/ppermute | solution.py:621
  12.5 0.0 collective-permute-done.zr_ref
  12.5 0.1 shard_map.87
  12.7 0.1 collective-permute-start.1
  12.8 0.9 %collective-permute-start.2 = (bf16[4,208,128]{2,1,0:T(8,128)(2,1)S(1)}, bf16[4,208,128]{2,1,0:T(8,128)(2,1)S(1)}, u32[]{:S(2)}, u32[]{:S(2)}) collective-permute-start(bf16[4,208,128]{2,1,0:T(8,128)(2,1)S(1)} %get-tuple-element.61), channel_id=1, source_target_pairs={{2,4},{4,2},{6,8},{8,6},{10,12},{12,10},{14,0},{0,14},{3,5},{5,3},... | collective-permute-start | bytes 638984 | tf_op jit(solution)/shard_map/ppermute | solution.py:658
  13.7 1.2 %shard_map.88 = (bf16[96,288]{1,0:T(8,128)(2,1)S(1)}, bf16[288,96]{1,0:T(8,128)(2,1)S(1)}, f32[32,128]{1,0:T(8,128)S(1)}, f32[24,256]{1,0:T(8,128)S(1)}, f32[24,...) custom-call(bf16[27,32,32]{2,1,0:T(8,128)(2,1)} %bitcast.4, f32[1,32]{1,0:T(1,128)} %bitcast.5, ...), custom_call_target="tpu_custom_call" | custom-call | tf_op jit(solution)/shard_map/pallas_call | solution.py:589
  14.9 1.3 %shard_map.89.rows_ref = bf16[2,1280,128]{2,1,0:T(8,128)(2,1)S(1)} custom-call(bf16[4,46,32,128]{3,2,1,0:T(8,128)(2,1)S(1)} %get-tuple-element.62.v_ref.v_in_ref, bf16[96,288]{1,0:T(8,128)(2,1)S(1)} %get-tuple-element.67.w_ref, f32[32,128]{1,0:T(8,128)S(1)} %get-tuple-element.68.b_ref), custom_call_target="tpu_custom_call" | custom-call | tf_op jit(solution)/shard_map/pallas_call | solution.py:589
  16.2 0.0 collective-permute-done.1.ye_ref
  16.2 1.9 %collective-permute-done.2.yo_ref = bf16[4,208,128]{2,1,0:T(8,128)(2,1)S(1)} collective-permute-done((bf16[4,208,128]{2,1,0:T(8,128)(2,1)S(1)}, bf16[4,208,128]{2,1,0:T(8,128)(2,1)S(1)}, u32[]{:S(2)}, u32[]{:S(2)}) %collective-permute-start.2) | collective-permute-done | bytes 213024 | tf_op jit(solution)/shard_map/ppermute | solution.py:658
  18.1 0.1 shard_map.90
  18.3 0.7 %collective-permute-done.4.xo_ref = bf16[36,32,128]{2,1,0:T(8,128)(2,1)S(1)} collective-permute-done((bf16[36,32,128]{2,1,0:T(8,128)(2,1)S(1)}, bf16[36,32,128]{2,1,0:T(8,128)(2,1)S(1)}, u32[]{:S(2)}, u32[]{:S(2)}) %collective-permute-start.4) | collective-permute-done | bytes 294944 | tf_op jit(solution)/shard_map/ppermute | solution.py:621
  19.0 3.9 %collective-permute-start.6 = (bf16[13,32,128]{2,1,0:T(8,128)(2,1)S(1)}, bf16[13,32,128]{2,1,0:T(8,128)(2,1)S(1)}, u32[]{:S(2)}, u32[]{:S(2)}) collective-permute-start(bf16[13,32,128]{2,1,0:T(8,128)(2,1)S(1)} %get-tuple-element.85), channel_id=1, source_target_pairs={{0,2},{2,0},{4,6},{6,4},{8,10},{10,8},{12,14},{14,12},{16,32},{18,... | collective-permute-start | bytes 319496 | tf_op jit(solution)/shard_map/ppermute | solution.py:667
  22.8 1.4 %shard_map.92 = (bf16[2,1280,128]{2,1,0:T(8,128)(2,1)S(1)}, bf16[2,46,32,128]{3,2,1,0:T(8,128)(2,1)S(1)}, bf16[2,4,32,128]{3,2,1,0:T(8,128)(2,1)S(1)}) custom-call(bf16[4,46,32,128]{3,2,1,0:T(8,128)(2,1)S(1)} %get-tuple-element.76.v_ref, bf16[36,32,128]{2,1,0:T(8,128)(2,1)S(1)} %collective-permute-done.3.xe_ref, ...), custom_call_target="tpu_custom_call" | custom-call | tf_op jit(solution)/shard_map/pallas_call | solution.py:589
  24.2 1.7 %shard_map.91 = (bf16[3,2,32,128]{3,2,1,0:T(8,128)(2,1)S(1)}, f32[4,4,40,128]{3,2,1,0:T(8,128)S(1)}, f32[4,4,40,128]{3,2,1,0:T(8,128)S(1)}, bf16[2,3,40,128]{3,2,1,0:T(8,128)(2,1)S(1)}, f32[2,40,128]{2,1,0:T(8,128)S(1)}) custom-call(bf16[4,46,32,128]{3,2,1,0:T(8,128)(2,1)S(1)} %get-tuple-element.76.v_ref, bf16[2,1280,128]{2,1,0:T(8,128)(2,1)S(1)} %shard_map.89.rows_ref, ...), custom_call_target="tpu_custom_call" | custom-call | tf_op jit(solution)/shard_map/pallas_call | solution.py:589
  25.9 0.8 %collective-permute-done.6.xo_ref = bf16[13,32,128]{2,1,0:T(8,128)(2,1)S(1)} collective-permute-done((bf16[13,32,128]{2,1,0:T(8,128)(2,1)S(1)}, bf16[13,32,128]{2,1,0:T(8,128)(2,1)S(1)}, u32[]{:S(2)}, u32[]{:S(2)}) %collective-permute-start.6) | collective-permute-done | bytes 106528 | tf_op jit(solution)/shard_map/ppermute | solution.py:667
  26.7 1.7 %shard_map.93 = (bf16[3,2,32,128]{3,2,1,0:T(8,128)(2,1)S(1)}, f32[2,3,40,128]{3,2,1,0:T(8,128)S(1)}, f32[2,3,40,128]{3,2,1,0:T(8,128)S(1)}, bf16[12,40,128]{2,1,0:T(8,128)(2,1)S(1)}, bf16[12,40,128]{2,1,0:T(8,128)(2,1)S(1)}) custom-call(bf16[4,46,32,128]{3,2,1,0:T(8,128)(2,1)S(1)} %get-tuple-element.76.v_ref, ...), custom_call_target="tpu_custom_call" | custom-call | tf_op jit(solution)/shard_map/pallas_call | solution.py:589
  28.4 0.1 collective-permute-start.7
  28.5 3.0 %collective-permute-start.8 = (bf16[12,40,128]{2,1,0:T(8,128)(2,1)S(1)}, bf16[12,40,128]{2,1,0:T(8,128)(2,1)S(1)}, u32[]{:S(2)}, u32[]{:S(2)}) collective-permute-start(bf16[12,40,128]{2,1,0:T(8,128)(2,1)S(1)} %get-tuple-element.105), channel_id=1, source_target_pairs={{0,2},{2,0},{4,6},{6,4},{8,10},{10,8},{12,14},{14,12},{16,32},{18,... | collective-permute-start | bytes 368648 | tf_op jit(solution)/shard_map/ppermute | solution.py:701
  31.5 2.4 %collective-permute-done.7.re_ref = bf16[12,40,128]{2,1,0:T(8,128)(2,1)S(1)} collective-permute-done((bf16[12,40,128]{2,1,0:T(8,128)(2,1)S(1)}, bf16[12,40,128]{2,1,0:T(8,128)(2,1)S(1)}, u32[]{:S(2)}, u32[]{:S(2)}) %collective-permute-start.7) | collective-permute-done | bytes 122912 | tf_op jit(solution)/shard_map/ppermute | solution.py:702
  33.9 2.2 %collective-permute-done.8.ro_ref = bf16[12,40,128]{2,1,0:T(8,128)(2,1)S(1)} collective-permute-done((bf16[12,40,128]{2,1,0:T(8,128)(2,1)S(1)}, bf16[12,40,128]{2,1,0:T(8,128)(2,1)S(1)}, u32[]{:S(2)}, u32[]{:S(2)}) %collective-permute-start.8) | collective-permute-done | bytes 122912 | tf_op jit(solution)/shard_map/ppermute | solution.py:701
  36.1 1.8 %shard_map.94 = (bf16[3,4,32,128]{3,2,1,0:T(8,128)(2,1)}, f32[4,32,128]{2,1,0:T(8,128)}) custom-call(bf16[3,2,32,128]{3,2,1,0:T(8,128)(2,1)S(1)} %get-tuple-element.83.ai_ref, bf16[3,2,32,128]{3,2,1,0:T(8,128)(2,1)S(1)} %get-tuple-element.100.ab_ref, f32[4,4,40,128]{3,2,1,0:T(8,128)S(1)} %get-tuple-element.96.e_in.ei_ref, ...), custom_call_target="tpu_custom_call" | custom-call | tf_op jit(solution)/shard_map/pallas_call | solution.py:589
  (3 shorter events, 0.0 us)
Async XLA Ops:
  2.5 10.0 %collective-permute-start = (bf16[320,128]{1,0:T(8,128)(2,1)S(1)}, bf16[320,128]{1,0:T(8,128)(2,1)S(1)}, u32[]{:S(2)}, u32[]{:S(2)}) collective-permute-start(bf16[320,128]{1,0:T(8,128)(2,1)S(1)} %get-tuple-element.55.zs_ref), channel_id=1, source_target_pairs={{0,1},{1,0},{2,3},{3,2},{4,5},{5,4},{6,7},{7,6},{8,9},{9,8},{10,11... | collective-permute-start | bytes 245768 | tf_op jit(solution)/shard_map/ppermute | solution.py:618
  4.9 13.4 %collective-permute-start.3 = (bf16[36,32,128]{2,1,0:T(8,128)(2,1)S(1)}, bf16[36,32,128]{2,1,0:T(8,128)(2,1)S(1)}, u32[]{:S(2)}, u32[]{:S(2)}) collective-permute-start(bf16[36,32,128]{2,1,0:T(8,128)(2,1)S(1)} %get-tuple-element.74), channel_id=1, source_target_pairs={{0,16},{2,18},{4,20},{6,22},{8,24},{10,26},{12,28},{14,30},{16,0},... | collective-permute-start | bytes 884744 | tf_op jit(solution)/shard_map/ppermute | solution.py:622
  6.8 12.2 %collective-permute-start.4 = (bf16[36,32,128]{2,1,0:T(8,128)(2,1)S(1)}, bf16[36,32,128]{2,1,0:T(8,128)(2,1)S(1)}, u32[]{:S(2)}, u32[]{:S(2)}) collective-permute-start(bf16[36,32,128]{2,1,0:T(8,128)(2,1)S(1)} %get-tuple-element.75), channel_id=1, source_target_pairs={{0,2},{2,0},{4,6},{6,4},{8,10},{10,8},{12,14},{14,12},{16,32},{18,... | collective-permute-start | bytes 884744 | tf_op jit(solution)/shard_map/ppermute | solution.py:621
  12.7 3.5 %collective-permute-start.1 = (bf16[4,208,128]{2,1,0:T(8,128)(2,1)S(1)}, bf16[4,208,128]{2,1,0:T(8,128)(2,1)S(1)}, u32[]{:S(2)}, u32[]{:S(2)}) collective-permute-start(bf16[4,208,128]{2,1,0:T(8,128)(2,1)S(1)} %get-tuple-element.60), channel_id=1, source_target_pairs={{0,2},{2,0},{4,6},{6,4},{8,10},{10,8},{12,14},{14,12},{1,3},{3,1},... | collective-permute-start | bytes 638984 | tf_op jit(solution)/shard_map/ppermute | solution.py:659
  12.8 5.4 %collective-permute-start.2 = (bf16[4,208,128]{2,1,0:T(8,128)(2,1)S(1)}, bf16[4,208,128]{2,1,0:T(8,128)(2,1)S(1)}, u32[]{:S(2)}, u32[]{:S(2)}) collective-permute-start(bf16[4,208,128]{2,1,0:T(8,128)(2,1)S(1)} %get-tuple-element.61), channel_id=1, source_target_pairs={{2,4},{4,2},{6,8},{8,6},{10,12},{12,10},{14,0},{0,14},{3,5},{5,3},... | collective-permute-start | bytes 638984 | tf_op jit(solution)/shard_map/ppermute | solution.py:658
  18.9 7.0 %collective-permute-start.5 = (bf16[13,32,128]{2,1,0:T(8,128)(2,1)S(1)}, bf16[13,32,128]{2,1,0:T(8,128)(2,1)S(1)}, u32[]{:S(2)}, u32[]{:S(2)}) collective-permute-start(bf16[13,32,128]{2,1,0:T(8,128)(2,1)S(1)} %get-tuple-element.84), channel_id=1, source_target_pairs={{0,16},{2,18},{4,20},{6,22},{8,24},{10,26},{12,28},{14,30},{16,0},... | collective-permute-start | bytes 319496 | tf_op jit(solution)/shard_map/ppermute | solution.py:668
  19.0 7.8 %collective-permute-start.6 = (bf16[13,32,128]{2,1,0:T(8,128)(2,1)S(1)}, bf16[13,32,128]{2,1,0:T(8,128)(2,1)S(1)}, u32[]{:S(2)}, u32[]{:S(2)}) collective-permute-start(bf16[13,32,128]{2,1,0:T(8,128)(2,1)S(1)} %get-tuple-element.85), channel_id=1, source_target_pairs={{0,2},{2,0},{4,6},{6,4},{8,10},{10,8},{12,14},{14,12},{16,32},{18,... | collective-permute-start | bytes 319496 | tf_op jit(solution)/shard_map/ppermute | solution.py:667
  28.4 5.4 %collective-permute-start.7 = (bf16[12,40,128]{2,1,0:T(8,128)(2,1)S(1)}, bf16[12,40,128]{2,1,0:T(8,128)(2,1)S(1)}, u32[]{:S(2)}, u32[]{:S(2)}) collective-permute-start(bf16[12,40,128]{2,1,0:T(8,128)(2,1)S(1)} %get-tuple-element.104), channel_id=1, source_target_pairs={{0,16},{2,18},{4,20},{6,22},{8,24},{10,26},{12,28},{14,30},{16,0},... | collective-permute-start | bytes 368648 | tf_op jit(solution)/shard_map/ppermute | solution.py:702
  28.5 7.5 %collective-permute-start.8 = (bf16[12,40,128]{2,1,0:T(8,128)(2,1)S(1)}, bf16[12,40,128]{2,1,0:T(8,128)(2,1)S(1)}, u32[]{:S(2)}, u32[]{:S(2)}) collective-permute-start(bf16[12,40,128]{2,1,0:T(8,128)(2,1)S(1)} %get-tuple-element.105), channel_id=1, source_target_pairs={{0,2},{2,0},{4,6},{6,4},{8,10},{10,8},{12,14},{14,12},{16,32},{18,... | collective-permute-start | bytes 368648 | tf_op jit(solution)/shard_map/ppermute | solution.py:701

commit v6 on v5

--- a/solution.py
+++ b/solution.py
@@ -13,23 +13,16 @@
 PARAMS = pltpu.CompilerParams(vmem_limit_bytes=12 * 2**20)
 
 
-def swaps(count):
-    def pairs(first):
-        return [
-            p
-            for i in range(first, count + first, 2)
-            for p in ((i % count, (i + 1) % count), ((i + 1) % count, i % count))
-        ]
-
-    return pairs(0), pairs(1)
-
-
-def swaps_gx():
+def swaps(axis):
     nx, ny = lax.axis_size("gx"), lax.axis_size("gy")
 
     def partner(x, y, first):
-        other = x + 1 if x % 2 == first else x - 1
-        return (other, y) if 0 <= other < nx else (x, y ^ 1)
+        at, count = (x, nx) if axis == "gx" else (y, ny)
+        other = at + 1 if at % 2 == first else at - 1
+        inside = 0 <= other < count
+        if axis == "gx":
+            return (other, y) if inside else (x, y ^ 1)
+        return (x, other) if inside else (x ^ 1, y)
 
     def pairs(first):
         out = []
@@ -79,13 +72,17 @@
     for x in range(4):
         copies[x].wait()
         v_ref[x, 5:37] = jnp.swapaxes(x_ref[x], 0, 1)
-    acc = jnp.zeros((256, 128), F32)
-    for y in range(16):
-        lhs = jnp.concatenate(
-            [v_ref[x, 5 + 16 * half + y] for x in range(4) for half in range(2)], axis=0
-        )
-        acc = acc + jnp.dot(lhs, sels[y], preferred_element_type=F32)
-    zs_ref[0:256] = acc.astype(BF16)
+    lhs = jnp.concatenate(
+        [
+            jnp.concatenate(
+                [v_ref[x, 5 + 16 * half + y] for x in range(4) for half in range(2)], axis=0
+            )
+            for y in range(16)
+        ],
+        axis=1,
+    )
+    edges = jnp.dot(lhs, jnp.concatenate(sels, axis=0), preferred_element_type=F32)
+    zs_ref[0:256] = edges.astype(BF16)
     zs_ref[288:320] = jnp.zeros((32, 128), BF16)
     even_face = jnp.where(lax.axis_index("gx") % 2 == 0, 3, 0)
     xe_ref[0:32] = v_ref[even_face, 5:37]
@@ -333,8 +330,8 @@
     def fill(low_ref, high_ref):
         face_ref[0, 5:37] = low_ref[0:32]
         face_ref[1, 5:37] = high_ref[0:32]
-        seeds_ref[0] = low_ref[32:36]
-        seeds_ref[1] = high_ref[32:36]
+        seeds_ref[0] = low_ref[32:36].astype(F32) / 15.0
+        seeds_ref[1] = high_ref[32:36].astype(F32) / 15.0
 
     by_side(xe_ref, xo_ref, fill)
 
@@ -357,7 +354,7 @@
 
 def inner_kernel(
     v_ref, rows_ref, ye_ref, yo_ref, zr_ref, ms_ref, w_ref, wp_ref, b_ref, hw_ref, hb_ref, hwp_ref, hbp_ref,
-    a_ref, e_ref, ext_ref, tile_ref, slots_ref, hid_ref, mask_ref, mext_ref,
+    a_ref, e_ref, ext_ref, tile_ref, slots_ref, start_ref, hid_ref, mask_ref, mext_ref,
 ):
     gy = lax.axis_index("gy")
     odd_y = gy % 2
@@ -419,6 +416,8 @@
                 ext_ref[x, f] = keep[f][1]
         e_ref[x, 3] = mask_ref[1, x]
         ext_ref[x, 3] = mext_ref[1, x]
+        start_ref[x, 0] = mask_ref[1, x] / 15.0
+        start_ref[x, 1] = mext_ref[1, x] / 15.0
     for way, order in enumerate(((2, 1), (1, 2))):
         packed = jnp.zeros((40, 128), F32)
         for j, x in enumerate(order):
@@ -491,7 +490,7 @@
 
 
 def rounds_kernel(
-    ai_ref, ab_ref, ei_ref, exti_ref, eb_ref, extb_ref, seeds_ref, re_ref, ro_ref, ms_ref,
+    ai_ref, ab_ref, ei_ref, exti_ref, eb_ref, extb_ref, start_ref, seeds_ref, re_ref, ro_ref, ms_ref,
     a_hbm, out_hbm, all_ref, s_ref, out_ref, sems,
 ):
     gx = lax.axis_index("gx")
@@ -512,7 +511,7 @@
         high = places[0] == 8
         for j, at in enumerate(places):
             seeds = seeds_ref[1, j] if high else seeds_ref[0, 3 - j]
-            s_ref[0, at, 0, 0:32] = seeds.astype(F32) * has / 15.0
+            s_ref[0, at, 0, 0:32] = seeds * has
             if j == 3:
                 s_ref[0, at, 0, 32:40] = zero[0:8]
                 s_ref[0, at, 1] = zero
@@ -533,8 +532,7 @@
     by_side(re_ref, ro_ref, fill)
 
     for x in range(4):
-        s_ref[0, 4 + x, 0] = ei_ref[x, 3] / 15.0
-        s_ref[0, 4 + x, 1] = exti_ref[x, 3] / 15.0
+        s_ref[0, 4 + x] = start_ref[x]
 
     def edge(at, f, i):
         if at < 4 or at > 7:
@@ -616,7 +614,7 @@
         specs=[HBM] * 3,
     )
     zr = lax.ppermute(zs, "gz", [(0, 1), (1, 0)])
-    even_x, odd_x = swaps_gx()
+    even_x, odd_x = swaps("gx")
     axes = ("gx", "gy")
     fo = lax.ppermute(fo, axes, odd_x)
     fe = lax.ppermute(fe, axes, even_x)
@@ -654,9 +652,9 @@
     weights = tuple(forms)
     rows_shape = [((2, 1280, 128), BF16)]
     (inner_rows,) = call(inner_rows_kernel, rows_shape, (vy, weights[0], weights[2]))
-    even, odd = swaps(lax.axis_size("gy"))
-    yo = lax.ppermute(yo, "gy", odd)
-    ye = lax.ppermute(ye, "gy", even)
+    even, odd = swaps("gy")
+    yo = lax.ppermute(yo, axes, odd)
+    ye = lax.ppermute(ye, axes, even)
     ye, yo, inner_rows = lax.optimization_barrier((ye, yo, inner_rows))
     v, xe, xo = call(
         xface_kernel,
@@ -666,7 +664,7 @@
     xe, xo, v, fe, fo = lax.optimization_barrier((xe, xo, v, fe, fo))
     xo = lax.ppermute(xo, axes, odd_x)
     xe = lax.ppermute(xe, axes, even_x)
-    inner_a, e, ext, tiles, slots = call(
+    inner_a, e, ext, tiles, slots, start = call(
         inner_kernel,
         [
             ((3, 2, 32, 128), BF16),
@@ -674,13 +672,14 @@
             ((4, 4, 40, 128), F32),
             ((2, 3, 40, 128), BF16),
             ((2, 40, 128), F32),
+            ((4, 2, 40, 128), F32),
         ],
         (v, inner_rows, ye, yo, zr, ms) + weights,
         scratch=[((2, 1280, 128), BF16), ((2, 4, 40, 128), F32), ((2, 4, 40, 128), F32)],
     )
     border_rows, faces, side_seeds = call(
         border_rows_kernel,
-        rows_shape + [((2, 46, 32, 128), BF16), ((2, 4, 32, 128), BF16)],
+        rows_shape + [((2, 46, 32, 128), BF16), ((2, 4, 32, 128), F32)],
         (v, fe, fo, weights[0], weights[2]),
     )
     xe, xo, e, ext, border_rows, faces = lax.optimization_barrier(
@@ -703,7 +702,7 @@
     affinity, strength = call(
         rounds_kernel,
         [((3, 4, 32, 128), BF16), ((4, 32, 128), F32)],
-        (inner_a, border_a, e, ext, border_e, border_ext, side_seeds, se, so, ms),
+        (inner_a, border_a, e, ext, border_e, border_ext, start, side_seeds, se, so, ms),
         scratch=[
             ((8, 3, 2, 40, 128), F32),
             ((2, 12, 2, 40, 128), F32),

time: 38 us -> 37.4 us (0.984)
  waiting for transfers between devices: 8.01 us -> 6.13 us
  starting transfers between devices: 18 us -> 18.9 us
    ppermute x1, waiting for transfers between devices: 2.36 us -> 1.02 us  [body(): se = lax.ppermute(se, axes, even_x)]
    ppermute x1, starting transfers between devices: 2.97 us -> 3.92 us  [body(): so = lax.ppermute(so, axes, odd_x)]
    ppermute x1, waiting for transfers between devices: 0.82 us -> 0.27 us  [body(): xo = lax.ppermute(xo, axes, odd_x)]
  transfers between devices with their start and end apart: 9 -> 9, of which waited for: 5 -> 5; matrix products, arithmetic and copies ran while one was open for 0% -> 0% of each run, Pallas kernels for 15% -> 16%
where the time goes in v6:
time: 37.4 us; the launch traced here: 36.9 us
  starting transfers between devices  18.9 us (51%)
  Pallas kernels  11.1 us (30%)
  waiting for transfers between devices  6.13 us (16%)
  between operations  0.73 us (2%)
    pallas_call x9, Pallas kernels, call(): pl.pallas_call(kernel, out_shape=[jax.ShapeDtypeStruct(s, d) for s, d in...  11.1 us
    ppermute x1, starting transfers between devices, body(): fo = lax.ppermute(fo, axes, odd_x)  5.74 us
    ppermute x1, starting transfers between devices, body(): so = lax.ppermute(so, axes, odd_x)  3.92 us
    ppermute x1, starting transfers between devices, body(): xo = lax.ppermute(xo, axes, odd_x)  3.85 us
    ppermute x1, starting transfers between devices, body(): zr = lax.ppermute(zs, 'gz', [(0, 1), (1, 0)])  2.38 us
    ppermute x1, waiting for transfers between devices, body(): so = lax.ppermute(so, axes, odd_x)  2.21 us
    ppermute x1, waiting for transfers between devices, body(): yo = lax.ppermute(yo, axes, odd)  1.93 us
    ppermute x1, starting transfers between devices, body(): fe = lax.ppermute(fe, axes, even_x)  1.91 us
  transfers between devices with their start and end apart: 9, of which 5 were waited for; matrix products, arithmetic and copies ran while one was open for 0% of the time, Pallas kernels for 16%

profile of v6, /device:TPU:14, one launch (start us, length us, event | category | flops | bytes accessed | tf_op | source)
XLA Modules:
  0.0 36.9 jit_solution(2932533413758291138)
XLA Ops:
  0.6 1.8 %shard_map.86 = (bf16[4,46,32,128]{3,2,1,0:T(8,128)(2,1)S(1)}, bf16[320,128]{1,0:T(8,128)(2,1)S(1)}, f32[2,4,32,128]{3,2,1,0:T(8,128)S(1)}, bf16[36,32,128]{2,1,0:T(8,128)(2,1)S(1)}, bf16[36,32,128]{2,1,0:T(8,128)(2,1)S(1)}) custom-call(bf16[32,4,32,128]{3,2,1,0:T(8,128)(2,1)} %x_hbm.1, s32[4,32,128]{2,1,0:T(8,128)} %m_hbm.1, s32[4,32,128]{2,1,0:T(8,128)} %s_hbm.1), custom_call_target="tpu_custom_call" | custom-call | tf_op jit(solution)/shard_map/pallas_call | solution.py:587
  2.4 2.4 %collective-permute-start = (bf16[320,128]{1,0:T(8,128)(2,1)S(1)}, bf16[320,128]{1,0:T(8,128)(2,1)S(1)}, u32[]{:S(2)}, u32[]{:S(2)}) collective-permute-start(bf16[320,128]{1,0:T(8,128)(2,1)S(1)} %get-tuple-element.56.zs_ref), channel_id=1, source_target_pairs={{0,1},{1,0},{2,3},{3,2},{4,5},{5,4},{6,7},{7,6},{8,9},{9,8},{10,11... | collective-permute-start | bytes 245768 | tf_op jit(solution)/shard_map/ppermute | solution.py:616
  4.8 1.9 %collective-permute-start.3 = (bf16[36,32,128]{2,1,0:T(8,128)(2,1)S(1)}, bf16[36,32,128]{2,1,0:T(8,128)(2,1)S(1)}, u32[]{:S(2)}, u32[]{:S(2)}) collective-permute-start(bf16[36,32,128]{2,1,0:T(8,128)(2,1)S(1)} %get-tuple-element.75), channel_id=1, source_target_pairs={{0,16},{2,18},{4,20},{6,22},{8,24},{10,26},{12,28},{14,30},{16,0},... | collective-permute-start | bytes 884744 | tf_op jit(solution)/shard_map/ppermute | solution.py:620
  6.7 5.7 %collective-permute-start.4 = (bf16[36,32,128]{2,1,0:T(8,128)(2,1)S(1)}, bf16[36,32,128]{2,1,0:T(8,128)(2,1)S(1)}, u32[]{:S(2)}, u32[]{:S(2)}) collective-permute-start(bf16[36,32,128]{2,1,0:T(8,128)(2,1)S(1)} %get-tuple-element.76), channel_id=1, source_target_pairs={{0,2},{2,0},{4,6},{6,4},{8,10},{10,8},{12,14},{14,12},{16,32},{18,... | collective-permute-start | bytes 884744 | tf_op jit(solution)/shard_map/ppermute | solution.py:619
  12.5 0.0 collective-permute-done.zr_ref
  12.5 0.1 shard_map.87
  12.6 0.1 collective-permute-start.1
  12.7 0.9 %collective-permute-start.2 = (bf16[4,208,128]{2,1,0:T(8,128)(2,1)S(1)}, bf16[4,208,128]{2,1,0:T(8,128)(2,1)S(1)}, u32[]{:S(2)}, u32[]{:S(2)}) collective-permute-start(bf16[4,208,128]{2,1,0:T(8,128)(2,1)S(1)} %get-tuple-element.62), channel_id=1, source_target_pairs={{0,16},{2,4},{4,2},{6,8},{8,6},{10,12},{12,10},{14,30},{16,0},{18,... | collective-permute-start | bytes 638984 | tf_op jit(solution)/shard_map/ppermute | solution.py:656
  13.7 1.2 %shard_map.88 = (bf16[96,288]{1,0:T(8,128)(2,1)S(1)}, bf16[288,96]{1,0:T(8,128)(2,1)S(1)}, f32[32,128]{1,0:T(8,128)S(1)}, f32[24,256]{1,0:T(8,128)S(1)}, f32[24,...) custom-call(bf16[27,32,32]{2,1,0:T(8,128)(2,1)} %bitcast.4, f32[1,32]{1,0:T(1,128)} %bitcast.5, ...), custom_call_target="tpu_custom_call" | custom-call | tf_op jit(solution)/shard_map/pallas_call | solution.py:587
  14.8 1.3 %shard_map.89.rows_ref = bf16[2,1280,128]{2,1,0:T(8,128)(2,1)S(1)} custom-call(bf16[4,46,32,128]{3,2,1,0:T(8,128)(2,1)S(1)} %get-tuple-element.63.v_ref.v_in_ref, bf16[96,288]{1,0:T(8,128)(2,1)S(1)} %get-tuple-element.68.w_ref, f32[32,128]{1,0:T(8,128)S(1)} %get-tuple-element.69.b_ref), custom_call_target="tpu_custom_call" | custom-call | tf_op jit(solution)/shard_map/pallas_call | solution.py:587
  16.2 0.0 collective-permute-done.1.ye_ref
  16.2 1.9 %collective-permute-done.2.yo_ref = bf16[4,208,128]{2,1,0:T(8,128)(2,1)S(1)} collective-permute-done((bf16[4,208,128]{2,1,0:T(8,128)(2,1)S(1)}, bf16[4,208,128]{2,1,0:T(8,128)(2,1)S(1)}, u32[]{:S(2)}, u32[]{:S(2)}) %collective-permute-start.2) | collective-permute-done | bytes 213024 | tf_op jit(solution)/shard_map/ppermute | solution.py:656
  18.1 0.1 shard_map.90
  18.2 0.7 %collective-permute-done.4.xo_ref = bf16[36,32,128]{2,1,0:T(8,128)(2,1)S(1)} collective-permute-done((bf16[36,32,128]{2,1,0:T(8,128)(2,1)S(1)}, bf16[36,32,128]{2,1,0:T(8,128)(2,1)S(1)}, u32[]{:S(2)}, u32[]{:S(2)}) %collective-permute-start.4) | collective-permute-done | bytes 294944 | tf_op jit(solution)/shard_map/ppermute | solution.py:619
  18.9 3.9 %collective-permute-start.6 = (bf16[13,32,128]{2,1,0:T(8,128)(2,1)S(1)}, bf16[13,32,128]{2,1,0:T(8,128)(2,1)S(1)}, u32[]{:S(2)}, u32[]{:S(2)}) collective-permute-start(bf16[13,32,128]{2,1,0:T(8,128)(2,1)S(1)} %get-tuple-element.86), channel_id=1, source_target_pairs={{0,2},{2,0},{4,6},{6,4},{8,10},{10,8},{12,14},{14,12},{16,32},{18,... | collective-permute-start | bytes 319496 | tf_op jit(solution)/shard_map/ppermute | solution.py:665
  22.8 1.4 %shard_map.92 = (bf16[2,1280,128]{2,1,0:T(8,128)(2,1)S(1)}, bf16[2,46,32,128]{3,2,1,0:T(8,128)(2,1)S(1)}, f32[2,4,32,128]{3,2,1,0:T(8,128)S(1)}) custom-call(bf16[4,46,32,128]{3,2,1,0:T(8,128)(2,1)S(1)} %get-tuple-element.77.v_ref, bf16[36,32,128]{2,1,0:T(8,128)(2,1)S(1)} %collective-permute-done.3.xe_ref, ...), custom_call_target="tpu_custom_call" | custom-call | tf_op jit(solution)/shard_map/pallas_call | solution.py:587
  24.2 1.7 %shard_map.91 = (bf16[3,2,32,128]{3,2,1,0:T(8,128)(2,1)S(1)}, f32[4,4,40,128]{3,2,1,0:T(8,128)S(1)}, f32[4,4,40,128]{3,2,1,0:T(8,128)S(1)}, bf16[2,3,40,128]{3,2...) custom-call(bf16[4,46,32,128]{3,2,1,0:T(8,128)(2,1)S(1)} %get-tuple-element.77.v_ref, ...), custom_call_target="tpu_custom_call" | custom-call | tf_op jit(solution)/shard_map/pallas_call | solution.py:587
  25.9 0.3 collective-permute-done.6.xo_ref
  26.2 1.7 %shard_map.93 = (bf16[3,2,32,128]{3,2,1,0:T(8,128)(2,1)S(1)}, f32[2,3,40,128]{3,2,1,0:T(8,128)S(1)}, f32[2,3,40,128]{3,2,1,0:T(8,128)S(1)}, bf16[12,40,128]{2,1,0:T(8,128)(2,1)S(1)}, bf16[12,40,128]{2,1,0:T(8,128)(2,1)S(1)}) custom-call(bf16[4,46,32,128]{3,2,1,0:T(8,128)(2,1)S(1)} %get-tuple-element.77.v_ref, ...), custom_call_target="tpu_custom_call" | custom-call | tf_op jit(solution)/shard_map/pallas_call | solution.py:587
  27.9 0.1 collective-permute-start.7
  28.0 3.9 %collective-permute-start.8 = (bf16[12,40,128]{2,1,0:T(8,128)(2,1)S(1)}, bf16[12,40,128]{2,1,0:T(8,128)(2,1)S(1)}, u32[]{:S(2)}, u32[]{:S(2)}) collective-permute-start(bf16[12,40,128]{2,1,0:T(8,128)(2,1)S(1)} %get-tuple-element.107), channel_id=1, source_target_pairs={{0,2},{2,0},{4,6},{6,4},{8,10},{10,8},{12,14},{14,12},{16,32},{18,... | collective-permute-start | bytes 368648 | tf_op jit(solution)/shard_map/ppermute | solution.py:700
  31.9 1.0 %collective-permute-done.7.re_ref = bf16[12,40,128]{2,1,0:T(8,128)(2,1)S(1)} collective-permute-done((bf16[12,40,128]{2,1,0:T(8,128)(2,1)S(1)}, bf16[12,40,128]{2,1,0:T(8,128)(2,1)S(1)}, u32[]{:S(2)}, u32[]{:S(2)}) %collective-permute-start.7) | collective-permute-done | bytes 122912 | tf_op jit(solution)/shard_map/ppermute | solution.py:701
  32.9 2.2 %collective-permute-done.8.ro_ref = bf16[12,40,128]{2,1,0:T(8,128)(2,1)S(1)} collective-permute-done((bf16[12,40,128]{2,1,0:T(8,128)(2,1)S(1)}, bf16[12,40,128]{2,1,0:T(8,128)(2,1)S(1)}, u32[]{:S(2)}, u32[]{:S(2)}) %collective-permute-start.8) | collective-permute-done | bytes 122912 | tf_op jit(solution)/shard_map/ppermute | solution.py:700
  35.1 1.7 %shard_map.94 = (bf16[3,4,32,128]{3,2,1,0:T(8,128)(2,1)}, f32[4,32,128]{2,1,0:T(8,128)}) custom-call(bf16[3,2,32,128]{3,2,1,0:T(8,128)(2,1)S(1)} %get-tuple-element.84.ai_ref, bf16[3,2,32,128]{3,2,1,0:T(8,128)(2,1)S(1)} %get-tuple-element.101.ab_ref, f32[4,4,40,128]{3,2,1,0:T(8,128)S(1)} %get-tuple-element.97.e_in.ei_ref, ...), custom_call_target="tpu_custom_call" | custom-call | tf_op jit(solution)/shard_map/pallas_call | solution.py:587
  (3 shorter events, 0.0 us)
Async XLA Ops:
  2.4 10.0 %collective-permute-start = (bf16[320,128]{1,0:T(8,128)(2,1)S(1)}, bf16[320,128]{1,0:T(8,128)(2,1)S(1)}, u32[]{:S(2)}, u32[]{:S(2)}) collective-permute-start(bf16[320,128]{1,0:T(8,128)(2,1)S(1)} %get-tuple-element.56.zs_ref), channel_id=1, source_target_pairs={{0,1},{1,0},{2,3},{3,2},{4,5},{5,4},{6,7},{7,6},{8,9},{9,8},{10,11... | collective-permute-start | bytes 245768 | tf_op jit(solution)/shard_map/ppermute | solution.py:616
  4.8 13.4 %collective-permute-start.3 = (bf16[36,32,128]{2,1,0:T(8,128)(2,1)S(1)}, bf16[36,32,128]{2,1,0:T(8,128)(2,1)S(1)}, u32[]{:S(2)}, u32[]{:S(2)}) collective-permute-start(bf16[36,32,128]{2,1,0:T(8,128)(2,1)S(1)} %get-tuple-element.75), channel_id=1, source_target_pairs={{0,16},{2,18},{4,20},{6,22},{8,24},{10,26},{12,28},{14,30},{16,0},... | collective-permute-start | bytes 884744 | tf_op jit(solution)/shard_map/ppermute | solution.py:620
  6.7 12.2 %collective-permute-start.4 = (bf16[36,32,128]{2,1,0:T(8,128)(2,1)S(1)}, bf16[36,32,128]{2,1,0:T(8,128)(2,1)S(1)}, u32[]{:S(2)}, u32[]{:S(2)}) collective-permute-start(bf16[36,32,128]{2,1,0:T(8,128)(2,1)S(1)} %get-tuple-element.76), channel_id=1, source_target_pairs={{0,2},{2,0},{4,6},{6,4},{8,10},{10,8},{12,14},{14,12},{16,32},{18,... | collective-permute-start | bytes 884744 | tf_op jit(solution)/shard_map/ppermute | solution.py:619
  12.6 3.5 %collective-permute-start.1 = (bf16[4,208,128]{2,1,0:T(8,128)(2,1)S(1)}, bf16[4,208,128]{2,1,0:T(8,128)(2,1)S(1)}, u32[]{:S(2)}, u32[]{:S(2)}) collective-permute-start(bf16[4,208,128]{2,1,0:T(8,128)(2,1)S(1)} %get-tuple-element.61), channel_id=1, source_target_pairs={{0,2},{2,0},{4,6},{6,4},{8,10},{10,8},{12,14},{14,12},{16,18},{18,... | collective-permute-start | bytes 638984 | tf_op jit(solution)/shard_map/ppermute | solution.py:657
  12.7 5.4 %collective-permute-start.2 = (bf16[4,208,128]{2,1,0:T(8,128)(2,1)S(1)}, bf16[4,208,128]{2,1,0:T(8,128)(2,1)S(1)}, u32[]{:S(2)}, u32[]{:S(2)}) collective-permute-start(bf16[4,208,128]{2,1,0:T(8,128)(2,1)S(1)} %get-tuple-element.62), channel_id=1, source_target_pairs={{0,16},{2,4},{4,2},{6,8},{8,6},{10,12},{12,10},{14,30},{16,0},{18,... | collective-permute-start | bytes 638984 | tf_op jit(solution)/shard_map/ppermute | solution.py:656
  18.9 7.0 %collective-permute-start.5 = (bf16[13,32,128]{2,1,0:T(8,128)(2,1)S(1)}, bf16[13,32,128]{2,1,0:T(8,128)(2,1)S(1)}, u32[]{:S(2)}, u32[]{:S(2)}) collective-permute-start(bf16[13,32,128]{2,1,0:T(8,128)(2,1)S(1)} %get-tuple-element.85), channel_id=1, source_target_pairs={{0,16},{2,18},{4,20},{6,22},{8,24},{10,26},{12,28},{14,30},{16,0},... | collective-permute-start | bytes 319496 | tf_op jit(solution)/shard_map/ppermute | solution.py:666
  18.9 7.2 %collective-permute-start.6 = (bf16[13,32,128]{2,1,0:T(8,128)(2,1)S(1)}, bf16[13,32,128]{2,1,0:T(8,128)(2,1)S(1)}, u32[]{:S(2)}, u32[]{:S(2)}) collective-permute-start(bf16[13,32,128]{2,1,0:T(8,128)(2,1)S(1)} %get-tuple-element.86), channel_id=1, source_target_pairs={{0,2},{2,0},{4,6},{6,4},{8,10},{10,8},{12,14},{14,12},{16,32},{18,... | collective-permute-start | bytes 319496 | tf_op jit(solution)/shard_map/ppermute | solution.py:665
  27.9 5.0 %collective-permute-start.7 = (bf16[12,40,128]{2,1,0:T(8,128)(2,1)S(1)}, bf16[12,40,128]{2,1,0:T(8,128)(2,1)S(1)}, u32[]{:S(2)}, u32[]{:S(2)}) collective-permute-start(bf16[12,40,128]{2,1,0:T(8,128)(2,1)S(1)} %get-tuple-element.106), channel_id=1, source_target_pairs={{0,16},{2,18},{4,20},{6,22},{8,24},{10,26},{12,28},{14,30},{16,0},... | collective-permute-start | bytes 368648 | tf_op jit(solution)/shard_map/ppermute | solution.py:701
  28.0 7.2 %collective-permute-start.8 = (bf16[12,40,128]{2,1,0:T(8,128)(2,1)S(1)}, bf16[12,40,128]{2,1,0:T(8,128)(2,1)S(1)}, u32[]{:S(2)}, u32[]{:S(2)}) collective-permute-start(bf16[12,40,128]{2,1,0:T(8,128)(2,1)S(1)} %get-tuple-element.107), channel_id=1, source_target_pairs={{0,2},{2,0},{4,6},{6,4},{8,10},{10,8},{12,14},{14,12},{16,32},{18,... | collective-permute-start | bytes 368648 | tf_op jit(solution)/shard_map/ppermute | solution.py:700

commit v7 on v6

--- a/solution.py
+++ b/solution.py
@@ -46,13 +46,15 @@
         pltpu.make_async_copy(m_hbm, m_ref, sems.at[4]),
         pltpu.make_async_copy(s_hbm, s_ref, sems.at[5]),
     ]
-    for copy in small + copies:
+    for copy in copies[:1] + small + copies[1:]:
         copy.start()
     lane = iota((128, 128), 1)
     row = iota((128, 128), 0)
     base = jnp.where(gz == 0, 120, 0)
     hit = row == base + lane % 8
     sels = [jnp.where(hit & (lane // 8 == y), 1.0, 0.0).astype(BF16) for y in range(16)]
+    copies[0].wait()
+    v_ref[0, 5:37] = jnp.swapaxes(x_ref[0], 0, 1)
     for copy in small:
         copy.wait()
     lane = iota((32, 128), 1)
@@ -69,7 +71,7 @@
             value = jnp.where(edge, value, 0.0)
             packed = packed + (pltpu.roll(value, 8 * slot, 1) if slot else value)
     zs_ref[256:288] = packed.astype(BF16)
-    for x in range(4):
+    for x in range(1, 4):
         copies[x].wait()
         v_ref[x, 5:37] = jnp.swapaxes(x_ref[x], 0, 1)
     lhs = jnp.concatenate(

time: 37.4 us -> 37.4 us (level)
  no operation moved by 1% of the time
where the time goes in v7:
time: 37.4 us; the launch traced here: 36.9 us
  starting transfers between devices  18.9 us (51%)
  Pallas kernels  11.1 us (30%)
  waiting for transfers between devices  6.12 us (16%)
  between operations  0.73 us (2%)
    pallas_call x9, Pallas kernels, call(): pl.pallas_call(kernel, out_shape=[jax.ShapeDtypeStruct(s, d) for s, d in...  11.1 us
    ppermute x1, starting transfers between devices, body(): fo = lax.ppermute(fo, axes, odd_x)  5.73 us
    ppermute x1, starting transfers between devices, body(): so = lax.ppermute(so, axes, odd_x)  3.93 us
    ppermute x1, starting transfers between devices, body(): xo = lax.ppermute(xo, axes, odd_x)  3.85 us
    ppermute x1, starting transfers between devices, body(): zr = lax.ppermute(zs, 'gz', [(0, 1), (1, 0)])  2.38 us
    ppermute x1, waiting for transfers between devices, body(): so = lax.ppermute(so, axes, odd_x)  2.21 us
    ppermute x1, waiting for transfers between devices, body(): yo = lax.ppermute(yo, axes, odd)  1.93 us
    ppermute x1, starting transfers between devices, body(): fe = lax.ppermute(fe, axes, even_x)  1.91 us
  transfers between devices with their start and end apart: 9, of which 5 were waited for; matrix products, arithmetic and copies ran while one was open for 0% of the time, Pallas kernels for 16%

profile of v7, /device:TPU:14, one launch (start us, length us, event | category | flops | bytes accessed | tf_op | source)
XLA Modules:
  0.0 36.9 jit_solution(8825007410721687066)
XLA Ops:
  0.6 1.8 %shard_map.86 = (bf16[4,46,32,128]{3,2,1,0:T(8,128)(2,1)S(1)}, bf16[320,128]{1,0:T(8,128)(2,1)S(1)}, f32[2,4,32,128]{3,2,1,0:T(8,128)S(1)}, bf16[36,32,128]{2,1,0:T(8,128)(2,1)S(1)}, bf16[36,32,128]{2,1,0:T(8,128)(2,1)S(1)}) custom-call(bf16[32,4,32,128]{3,2,1,0:T(8,128)(2,1)} %x_hbm.1, s32[4,32,128]{2,1,0:T(8,128)} %m_hbm.1, s32[4,32,128]{2,1,0:T(8,128)} %s_hbm.1), custom_call_target="tpu_custom_call" | custom-call | tf_op jit(solution)/shard_map/pallas_call | solution.py:589
  2.5 2.4 %collective-permute-start = (bf16[320,128]{1,0:T(8,128)(2,1)S(1)}, bf16[320,128]{1,0:T(8,128)(2,1)S(1)}, u32[]{:S(2)}, u32[]{:S(2)}) collective-permute-start(bf16[320,128]{1,0:T(8,128)(2,1)S(1)} %get-tuple-element.56.zs_ref), channel_id=1, source_target_pairs={{0,1},{1,0},{2,3},{3,2},{4,5},{5,4},{6,7},{7,6},{8,9},{9,8},{10,11... | collective-permute-start | bytes 245768 | tf_op jit(solution)/shard_map/ppermute | solution.py:618
  4.9 1.9 %collective-permute-start.3 = (bf16[36,32,128]{2,1,0:T(8,128)(2,1)S(1)}, bf16[36,32,128]{2,1,0:T(8,128)(2,1)S(1)}, u32[]{:S(2)}, u32[]{:S(2)}) collective-permute-start(bf16[36,32,128]{2,1,0:T(8,128)(2,1)S(1)} %get-tuple-element.75), channel_id=1, source_target_pairs={{0,16},{2,18},{4,20},{6,22},{8,24},{10,26},{12,28},{14,30},{16,0},... | collective-permute-start | bytes 884744 | tf_op jit(solution)/shard_map/ppermute | solution.py:622
  6.8 5.7 %collective-permute-start.4 = (bf16[36,32,128]{2,1,0:T(8,128)(2,1)S(1)}, bf16[36,32,128]{2,1,0:T(8,128)(2,1)S(1)}, u32[]{:S(2)}, u32[]{:S(2)}) collective-permute-start(bf16[36,32,128]{2,1,0:T(8,128)(2,1)S(1)} %get-tuple-element.76), channel_id=1, source_target_pairs={{0,2},{2,0},{4,6},{6,4},{8,10},{10,8},{12,14},{14,12},{16,32},{18,... | collective-permute-start | bytes 884744 | tf_op jit(solution)/shard_map/ppermute | solution.py:621
  12.5 0.0 collective-permute-done.zr_ref
  12.5 0.1 shard_map.87
  12.7 0.1 collective-permute-start.1
  12.8 0.9 %collective-permute-start.2 = (bf16[4,208,128]{2,1,0:T(8,128)(2,1)S(1)}, bf16[4,208,128]{2,1,0:T(8,128)(2,1)S(1)}, u32[]{:S(2)}, u32[]{:S(2)}) collective-permute-start(bf16[4,208,128]{2,1,0:T(8,128)(2,1)S(1)} %get-tuple-element.62), channel_id=1, source_target_pairs={{0,16},{2,4},{4,2},{6,8},{8,6},{10,12},{12,10},{14,30},{16,0},{18,... | collective-permute-start | bytes 638984 | tf_op jit(solution)/shard_map/ppermute | solution.py:658
  13.7 1.2 %shard_map.88 = (bf16[96,288]{1,0:T(8,128)(2,1)S(1)}, bf16[288,96]{1,0:T(8,128)(2,1)S(1)}, f32[32,128]{1,0:T(8,128)S(1)}, f32[24,256]{1,0:T(8,128)S(1)}, f32[24,...) custom-call(bf16[27,32,32]{2,1,0:T(8,128)(2,1)} %bitcast.4, f32[1,32]{1,0:T(1,128)} %bitcast.5, ...), custom_call_target="tpu_custom_call" | custom-call | tf_op jit(solution)/shard_map/pallas_call | solution.py:589
  14.9 1.3 %shard_map.89.rows_ref = bf16[2,1280,128]{2,1,0:T(8,128)(2,1)S(1)} custom-call(bf16[4,46,32,128]{3,2,1,0:T(8,128)(2,1)S(1)} %get-tuple-element.63.v_ref.v_in_ref, bf16[96,288]{1,0:T(8,128)(2,1)S(1)} %get-tuple-element.68.w_ref, f32[32,128]{1,0:T(8,128)S(1)} %get-tuple-element.69.b_ref), custom_call_target="tpu_custom_call" | custom-call | tf_op jit(solution)/shard_map/pallas_call | solution.py:589
  16.2 0.0 collective-permute-done.1.ye_ref
  16.2 1.9 %collective-permute-done.2.yo_ref = bf16[4,208,128]{2,1,0:T(8,128)(2,1)S(1)} collective-permute-done((bf16[4,208,128]{2,1,0:T(8,128)(2,1)S(1)}, bf16[4,208,128]{2,1,0:T(8,128)(2,1)S(1)}, u32[]{:S(2)}, u32[]{:S(2)}) %collective-permute-start.2) | collective-permute-done | bytes 213024 | tf_op jit(solution)/shard_map/ppermute | solution.py:658
  18.1 0.1 shard_map.90
  18.3 0.7 %collective-permute-done.4.xo_ref = bf16[36,32,128]{2,1,0:T(8,128)(2,1)S(1)} collective-permute-done((bf16[36,32,128]{2,1,0:T(8,128)(2,1)S(1)}, bf16[36,32,128]{2,1,0:T(8,128)(2,1)S(1)}, u32[]{:S(2)}, u32[]{:S(2)}) %collective-permute-start.4) | collective-permute-done | bytes 294944 | tf_op jit(solution)/shard_map/ppermute | solution.py:621
  19.0 3.9 %collective-permute-start.6 = (bf16[13,32,128]{2,1,0:T(8,128)(2,1)S(1)}, bf16[13,32,128]{2,1,0:T(8,128)(2,1)S(1)}, u32[]{:S(2)}, u32[]{:S(2)}) collective-permute-start(bf16[13,32,128]{2,1,0:T(8,128)(2,1)S(1)} %get-tuple-element.86), channel_id=1, source_target_pairs={{0,2},{2,0},{4,6},{6,4},{8,10},{10,8},{12,14},{14,12},{16,32},{18,... | collective-permute-start | bytes 319496 | tf_op jit(solution)/shard_map/ppermute | solution.py:667
  22.8 1.4 %shard_map.92 = (bf16[2,1280,128]{2,1,0:T(8,128)(2,1)S(1)}, bf16[2,46,32,128]{3,2,1,0:T(8,128)(2,1)S(1)}, f32[2,4,32,128]{3,2,1,0:T(8,128)S(1)}) custom-call(bf16[4,46,32,128]{3,2,1,0:T(8,128)(2,1)S(1)} %get-tuple-element.77.v_ref, bf16[36,32,128]{2,1,0:T(8,128)(2,1)S(1)} %collective-permute-done.3.xe_ref, ...), custom_call_target="tpu_custom_call" | custom-call | tf_op jit(solution)/shard_map/pallas_call | solution.py:589
  24.2 1.7 %shard_map.91 = (bf16[3,2,32,128]{3,2,1,0:T(8,128)(2,1)S(1)}, f32[4,4,40,128]{3,2,1,0:T(8,128)S(1)}, f32[4,4,40,128]{3,2,1,0:T(8,128)S(1)}, bf16[2,3,40,128]{3,2...) custom-call(bf16[4,46,32,128]{3,2,1,0:T(8,128)(2,1)S(1)} %get-tuple-element.77.v_ref, ...), custom_call_target="tpu_custom_call" | custom-call | tf_op jit(solution)/shard_map/pallas_call | solution.py:589
  25.9 0.3 collective-permute-done.6.xo_ref
  26.2 1.7 %shard_map.93 = (bf16[3,2,32,128]{3,2,1,0:T(8,128)(2,1)S(1)}, f32[2,3,40,128]{3,2,1,0:T(8,128)S(1)}, f32[2,3,40,128]{3,2,1,0:T(8,128)S(1)}, bf16[12,40,128]{2,1,0:T(8,128)(2,1)S(1)}, bf16[12,40,128]{2,1,0:T(8,128)(2,1)S(1)}) custom-call(bf16[4,46,32,128]{3,2,1,0:T(8,128)(2,1)S(1)} %get-tuple-element.77.v_ref, ...), custom_call_target="tpu_custom_call" | custom-call | tf_op jit(solution)/shard_map/pallas_call | solution.py:589
  27.9 0.1 collective-permute-start.7
  28.0 3.9 %collective-permute-start.8 = (bf16[12,40,128]{2,1,0:T(8,128)(2,1)S(1)}, bf16[12,40,128]{2,1,0:T(8,128)(2,1)S(1)}, u32[]{:S(2)}, u32[]{:S(2)}) collective-permute-start(bf16[12,40,128]{2,1,0:T(8,128)(2,1)S(1)} %get-tuple-element.107), channel_id=1, source_target_pairs={{0,2},{2,0},{4,6},{6,4},{8,10},{10,8},{12,14},{14,12},{16,32},{18,... | collective-permute-start | bytes 368648 | tf_op jit(solution)/shard_map/ppermute | solution.py:702
  31.9 1.0 %collective-permute-done.7.re_ref = bf16[12,40,128]{2,1,0:T(8,128)(2,1)S(1)} collective-permute-done((bf16[12,40,128]{2,1,0:T(8,128)(2,1)S(1)}, bf16[12,40,128]{2,1,0:T(8,128)(2,1)S(1)}, u32[]{:S(2)}, u32[]{:S(2)}) %collective-permute-start.7) | collective-permute-done | bytes 122912 | tf_op jit(solution)/shard_map/ppermute | solution.py:703
  33.0 2.2 %collective-permute-done.8.ro_ref = bf16[12,40,128]{2,1,0:T(8,128)(2,1)S(1)} collective-permute-done((bf16[12,40,128]{2,1,0:T(8,128)(2,1)S(1)}, bf16[12,40,128]{2,1,0:T(8,128)(2,1)S(1)}, u32[]{:S(2)}, u32[]{:S(2)}) %collective-permute-start.8) | collective-permute-done | bytes 122912 | tf_op jit(solution)/shard_map/ppermute | solution.py:702
  35.2 1.7 %shard_map.94 = (bf16[3,4,32,128]{3,2,1,0:T(8,128)(2,1)}, f32[4,32,128]{2,1,0:T(8,128)}) custom-call(bf16[3,2,32,128]{3,2,1,0:T(8,128)(2,1)S(1)} %get-tuple-element.84.ai_ref, bf16[3,2,32,128]{3,2,1,0:T(8,128)(2,1)S(1)} %get-tuple-element.101.ab_ref, f32[4,4,40,128]{3,2,1,0:T(8,128)S(1)} %get-tuple-element.97.e_in.ei_ref, ...), custom_call_target="tpu_custom_call" | custom-call | tf_op jit(solution)/shard_map/pallas_call | solution.py:589
  (3 shorter events, 0.0 us)
Async XLA Ops:
  2.5 10.0 %collective-permute-start = (bf16[320,128]{1,0:T(8,128)(2,1)S(1)}, bf16[320,128]{1,0:T(8,128)(2,1)S(1)}, u32[]{:S(2)}, u32[]{:S(2)}) collective-permute-start(bf16[320,128]{1,0:T(8,128)(2,1)S(1)} %get-tuple-element.56.zs_ref), channel_id=1, source_target_pairs={{0,1},{1,0},{2,3},{3,2},{4,5},{5,4},{6,7},{7,6},{8,9},{9,8},{10,11... | collective-permute-start | bytes 245768 | tf_op jit(solution)/shard_map/ppermute | solution.py:618
  4.9 13.4 %collective-permute-start.3 = (bf16[36,32,128]{2,1,0:T(8,128)(2,1)S(1)}, bf16[36,32,128]{2,1,0:T(8,128)(2,1)S(1)}, u32[]{:S(2)}, u32[]{:S(2)}) collective-permute-start(bf16[36,32,128]{2,1,0:T(8,128)(2,1)S(1)} %get-tuple-element.75), channel_id=1, source_target_pairs={{0,16},{2,18},{4,20},{6,22},{8,24},{10,26},{12,28},{14,30},{16,0},... | collective-permute-start | bytes 884744 | tf_op jit(solution)/shard_map/ppermute | solution.py:622
  6.8 12.2 %collective-permute-start.4 = (bf16[36,32,128]{2,1,0:T(8,128)(2,1)S(1)}, bf16[36,32,128]{2,1,0:T(8,128)(2,1)S(1)}, u32[]{:S(2)}, u32[]{:S(2)}) collective-permute-start(bf16[36,32,128]{2,1,0:T(8,128)(2,1)S(1)} %get-tuple-element.76), channel_id=1, source_target_pairs={{0,2},{2,0},{4,6},{6,4},{8,10},{10,8},{12,14},{14,12},{16,32},{18,... | collective-permute-start | bytes 884744 | tf_op jit(solution)/shard_map/ppermute | solution.py:621
  12.7 3.5 %collective-permute-start.1 = (bf16[4,208,128]{2,1,0:T(8,128)(2,1)S(1)}, bf16[4,208,128]{2,1,0:T(8,128)(2,1)S(1)}, u32[]{:S(2)}, u32[]{:S(2)}) collective-permute-start(bf16[4,208,128]{2,1,0:T(8,128)(2,1)S(1)} %get-tuple-element.61), channel_id=1, source_target_pairs={{0,2},{2,0},{4,6},{6,4},{8,10},{10,8},{12,14},{14,12},{16,18},{18,... | collective-permute-start | bytes 638984 | tf_op jit(solution)/shard_map/ppermute | solution.py:659
  12.8 5.4 %collective-permute-start.2 = (bf16[4,208,128]{2,1,0:T(8,128)(2,1)S(1)}, bf16[4,208,128]{2,1,0:T(8,128)(2,1)S(1)}, u32[]{:S(2)}, u32[]{:S(2)}) collective-permute-start(bf16[4,208,128]{2,1,0:T(8,128)(2,1)S(1)} %get-tuple-element.62), channel_id=1, source_target_pairs={{0,16},{2,4},{4,2},{6,8},{8,6},{10,12},{12,10},{14,30},{16,0},{18,... | collective-permute-start | bytes 638984 | tf_op jit(solution)/shard_map/ppermute | solution.py:658
  19.0 7.0 %collective-permute-start.5 = (bf16[13,32,128]{2,1,0:T(8,128)(2,1)S(1)}, bf16[13,32,128]{2,1,0:T(8,128)(2,1)S(1)}, u32[]{:S(2)}, u32[]{:S(2)}) collective-permute-start(bf16[13,32,128]{2,1,0:T(8,128)(2,1)S(1)} %get-tuple-element.85), channel_id=1, source_target_pairs={{0,16},{2,18},{4,20},{6,22},{8,24},{10,26},{12,28},{14,30},{16,0},... | collective-permute-start | bytes 319496 | tf_op jit(solution)/shard_map/ppermute | solution.py:668
  19.0 7.2 %collective-permute-start.6 = (bf16[13,32,128]{2,1,0:T(8,128)(2,1)S(1)}, bf16[13,32,128]{2,1,0:T(8,128)(2,1)S(1)}, u32[]{:S(2)}, u32[]{:S(2)}) collective-permute-start(bf16[13,32,128]{2,1,0:T(8,128)(2,1)S(1)} %get-tuple-element.86), channel_id=1, source_target_pairs={{0,2},{2,0},{4,6},{6,4},{8,10},{10,8},{12,14},{14,12},{16,32},{18,... | collective-permute-start | bytes 319496 | tf_op jit(solution)/shard_map/ppermute | solution.py:667
  27.9 5.1 %collective-permute-start.7 = (bf16[12,40,128]{2,1,0:T(8,128)(2,1)S(1)}, bf16[12,40,128]{2,1,0:T(8,128)(2,1)S(1)}, u32[]{:S(2)}, u32[]{:S(2)}) collective-permute-start(bf16[12,40,128]{2,1,0:T(8,128)(2,1)S(1)} %get-tuple-element.106), channel_id=1, source_target_pairs={{0,16},{2,18},{4,20},{6,22},{8,24},{10,26},{12,28},{14,30},{16,0},... | collective-permute-start | bytes 368648 | tf_op jit(solution)/shard_map/ppermute | solution.py:703
  28.0 7.2 %collective-permute-start.8 = (bf16[12,40,128]{2,1,0:T(8,128)(2,1)S(1)}, bf16[12,40,128]{2,1,0:T(8,128)(2,1)S(1)}, u32[]{:S(2)}, u32[]{:S(2)}) collective-permute-start(bf16[12,40,128]{2,1,0:T(8,128)(2,1)S(1)} %get-tuple-element.107), channel_id=1, source_target_pairs={{0,2},{2,0},{4,6},{6,4},{8,10},{10,8},{12,14},{14,12},{16,32},{18,... | collective-permute-start | bytes 368648 | tf_op jit(solution)/shard_map/ppermute | solution.py:702
